TPU v7x, 32 devices: a whole 2x2x4 slice. The times are simulated.
32 devices in a mesh: ifg: 8 (over z, core), strip: 4 (over y, x).
Axes of the slice: x: 2, y: 2, z: 4, core: 2. Of those that a mesh axis runs over, the one named last changes fastest.
Arguments:
- grad_x: float32 [64, 256, 1024], P('ifg', 'strip'), may hold values from -3 to 3
- grad_y: float32 [64, 256, 1024], P('ifg', 'strip'), may hold values from -3 to 3
- coherence: float32 [64, 256, 1024], P('ifg', 'strip'), may hold values from 0 to 1, as said below
- pairs: int32 [64, 2], replicated, may hold values from 0 to 31, as said below
Outputs:
- unwrapped: float32 [64, 256, 1024], P('ifg', 'strip')
- series: float32 [32, 256, 1024], P('ifg', 'strip')
Inputs may be any that keep to these rules, and one draw needn't show every extreme that they name: Every row names an earlier date first and a later date second; the pairs connect all 32 dates. `coherence`: positive weights.
All inputs are finite; a program needn't handle non-finite values.
Results may differ from a plain program's by a relative error of at most 0.0003.
Values sent between devices are 32-bit elements; how exact they have to be, the bound alone decides.
No kernel may reach another device: no remote copies, remote signals or barrier semaphores. Data moves between devices by JAX's collectives and lax.ppermute only.
A program may use at most 64 MiB of HBM per device.

v0:
```python
import jax
import jax.numpy as jnp
from jax import lax
from jax.experimental import pallas as pl
from jax.experimental.pallas import tpu as pltpu
from jax.sharding import PartitionSpec as P

DATES = 32
SLICES = (1, 2, 2, 2, 1)
CHUNKS = len(SLICES)
PAD = 8
damping = 0.1
TINY = 1e-6
F32 = jnp.float32
ANY = pl.BlockSpec(memory_space=pl.ANY)
SMEM = pl.BlockSpec(memory_space=pltpu.SMEM)
VMEM = pl.BlockSpec(memory_space=pltpu.VMEM)


def room(mib):
    return pltpu.CompilerParams(vmem_limit_bytes=mib * 2**20)


def near(x):
    return pltpu.with_memory_space_constraint(x, pltpu.VMEM)


def far_off(x):
    return pltpu.with_memory_space_constraint(x, pltpu.HBM)


def half_and_member(groups):
    index = lax.axis_index("ifg").astype(jnp.int32)
    return (index // groups, index % groups)


def in_vmem(*shape):
    return pltpu.VMEM(shape, F32)


def turned_cols(x, by, at):
    lane = lax.broadcasted_iota(jnp.int32, (x.shape[0], 128), 1)
    turned = [pltpu.roll(x[:, i : i + 128], by % 128, axis=1) for i in range(0, x.shape[1], 128)]
    moved = turned[-by:] + turned[:-by]
    return jnp.concatenate([jnp.where(lane == at, m, t) for m, t in zip(moved, turned)], axis=1)


def next_col(x):
    return turned_cols(x, -1, 127)


def prev_col(x):
    return turned_cols(x, 1, 0)


def col_weights(c):
    lane = lax.broadcasted_iota(jnp.int32, c.shape, 1)
    return jnp.where(lane < c.shape[1] - 1, c * next_col(c), 0.0)


def col_part(w, f):
    fx = w * (f - next_col(f))
    return fx - prev_col(fx)


def folded(x):
    parts = [x[:, i : i + 128] for i in range(0, x.shape[1], 128)]
    while len(parts) > 1:
        parts = [sum(parts[i : i + 2][1:], parts[i]) for i in range(0, len(parts), 2)]
    return parts[0]


def inverse_map(pairs, groups):
    number = pairs.shape[0]
    inner = number // 2
    wide = -(-(DATES + number) // 128) * 128
    share = DATES // (2 * groups)
    count = number // (2 * groups)

    def body(pair, out, work):
        h, me = half_and_member(groups)

        def twin(i, each):
            return jnp.bitwise_xor(i // each, me) * each + i % each

        d = lax.broadcasted_iota(jnp.int32, (DATES, number), 0)
        half = DATES // 2
        slots = jnp.where(d < half, (1 - h) * half + d, h * half + twin(d % half, share))
        k = lax.broadcasted_iota(jnp.int32, (number, number), 1)
        source = jnp.where(k < inner, h * inner + twin(k % inner, count), (1 - h) * inner + k % inner)
        turn = (source == lax.broadcasted_iota(jnp.int32, (number, number), 0)).astype(F32)
        p = jnp.dot(
            pair[...].astype(F32), turn, precision=lax.Precision.HIGHEST, preferred_element_type=F32
        )
        slots = slots.astype(F32)
        back = (p[1:2] == slots).astype(F32) - (p[0:1] == slots).astype(F32)
        normal = 1.0 + lax.dot_general(
            back, back, (((1,), (1,)), ((), ())), precision=lax.Precision.HIGHEST, preferred_element_type=F32
        )
        work[...] = jnp.zeros_like(work)
        work[:, :DATES] = normal
        work[:, DATES : DATES + number] = back
        w = work[...]
        row = lax.broadcasted_iota(jnp.int32, (DATES, wide), 0)
        for j in range(DATES):
            pivot = w[j : j + 1] / w[j : j + 1, j : j + 1]
            w = jnp.where(row == j, pivot, w - w[:, j : j + 1] * pivot)
        work[...] = w
        out[...] = work[:, DATES : DATES + inner]

    return pl.pallas_call(
        body,
        in_specs=[VMEM],
        out_specs=VMEM,
        out_shape=jax.ShapeDtypeStruct((DATES, inner), F32),
        scratch_shapes=[pltpu.VMEM((DATES, wide), F32)],
        name="inverse_map",
        compiler_params=room(2),
    )(pairs.T)


def edges(coh, gx, gy):
    count, rows, cols = coh.shape
    last_tile = rows // 8 - 1

    def body(ct, xt, yt, cb, xb, yb, down, up):
        row = lax.broadcasted_iota(jnp.int32, (8, cols), 0)

        def partial_rhs(c, x, y):
            fx = col_weights(c) * x
            fy = jnp.where(row < 7, c * pltpu.roll(c, 7, axis=0) * y, 0.0)
            return -(fx - prev_col(fx) + fy - pltpu.roll(fy, 1, axis=0))

        for k in range(count):
            c, y = (cb[k], yb[k])
            r = partial_rhs(c, xb[k], y)
            down[0, k : k + 1, :] = r[6:7]
            down[1, k : k + 1, :] = r[7:8]
            down[2, k : k + 1, :] = y[7:8]
            down[3, k : k + 1, :] = c[6:7]
            down[4, k : k + 1, :] = c[7:8]
            c = ct[k]
            r = partial_rhs(c, xt[k], yt[k])
            for i in range(3):
                up[i, k : k + 1, :] = r[i : i + 1]
                up[3 + i, k : k + 1, :] = c[i : i + 1]

    top = pl.BlockSpec((count, 8, cols), lambda i: (0, 0, 0))
    bottom = pl.BlockSpec((count, 8, cols), lambda i: (0, last_tile, 0))
    return pl.pallas_call(
        body,
        grid=(1,),
        in_specs=[top, top, top, bottom, bottom, bottom],
        out_specs=[
            pl.BlockSpec((5, count, cols), lambda i: (0, 0, 0)),
            pl.BlockSpec((6, count, cols), lambda i: (0, 0, 0)),
        ],
        out_shape=[
            jax.ShapeDtypeStruct((5, count, cols), F32),
            jax.ShapeDtypeStruct((6, count, cols), F32),
        ],
        name="edges",
        compiler_params=room(8),
    )(*(far_off(x) for x in (coh, gx, gy, coh, gx, gy)))


def interior(coh, gx, gy):
    count, rows, cols = coh.shape
    tiles, blocks = (rows // 8, cols // 128)

    def body(c_hbm, x_hbm, y_hbm, r, v, u, wx, wy, extra, mom, cs, xs, ys, sems):
        half = rows // 2

        def copies(s):
            return [
                pltpu.make_async_copy(
                    src.at[:, pl.ds(s * half, half), pl.ds(128 * b, 128)],
                    dst.at[b, :, pl.ds(s * half, half), :],
                    sems.at[s, n, b],
                )
                for n, (src, dst) in enumerate(((c_hbm, cs), (x_hbm, xs), (y_hbm, ys)))
                for b in range(blocks)
            ]

        for s in range(2):
            for copy in copies(s):
                copy.start()

        def row_of(ref, i):
            return jnp.concatenate(
                [
                    ref.at[b].reshape(count * (rows + PAD), 128)[pl.ds(i, count, stride=rows + PAD), :]
                    for b in range(blocks)
                ],
                axis=1,
            )

        fy = jnp.zeros((count, cols), F32)
        for copy in copies(0):
            copy.wait()
        c = row_of(cs, 0)
        extra[0] = c
        for at in range(rows):
            if at == half - 1:
                for copy in copies(1):
                    copy.wait()
            w = col_weights(c)
            fx = w * row_of(xs, at)
            rhs = prev_col(fx) - fx + fy
            wx[at] = w
            if at < rows - 1:
                later = row_of(cs, at + 1)
                h = c * later
                wy[at] = h
                fy = h * row_of(ys, at)
                rhs = rhs - fy
                c = later
            else:
                wy[at] = jnp.zeros((count, cols), F32)
                extra[1] = c
                extra[2] = row_of(ys, at)
            r[at] = rhs

        def apply_to(src, dst, first, bound, near_bound):
            def tile(t, carry, low, high):
                fy, a, b = carry
                for i in range(8):
                    at = 8 * t + i
                    f = src[at]
                    after = src[jnp.minimum(at + 1, rows - 1)] if i == 7 else src[at + 1]
                    now = wy[at] * (f - after)
                    g = col_part(wx[at], f) + now - fy
                    fy = now
                    dst[at] = g
                    if low is None or low + i >= bound and high - i >= bound:
                        a = a + folded(f * f)
                    if low is None or low + i >= near_bound and high - i >= near_bound:
                        b = b + folded(f * g)
                return fy, a, b

            none = jnp.zeros((count, 128), F32)
            carry = (jnp.zeros((count, cols), F32), none, none)
            carry = tile(0, carry, 0, rows - 1)
            carry = lax.fori_loop(1, tiles - 1, lambda t, c: tile(t, c, None, None), carry)
            _, a, b = tile(tiles - 1, carry, rows - 8, 7)
            mom[first] = a
            mom[first + 1] = b

        apply_to(r, v, 0, 1, 2)
        apply_to(v, u, 2, 2, 3)

        def energy(t, carry, low, high):
            a, b = carry
            for i in range(8):
                if low is not None and (low + i < 3 or high - i < 3):
                    continue
                at = 8 * t + i
                f = u[at]
                d = f - next_col(f)
                e = wx[at] * d * d
                if low is None or high - i >= 4:
                    d = f - u[at + 1]
                    e = e + wy[at] * d * d
                a = a + folded(f * f)
                b = b + folded(e)
            return a, b

        none = jnp.zeros((count, 128), F32)
        carry = energy(0, (none, none), 0, rows - 1)
        carry = lax.fori_loop(1, tiles - 1, lambda t, c: energy(t, c, None, None), carry)
        mom[4], mom[5] = energy(tiles - 1, carry, rows - 8, 7)

    field = in_vmem(rows, count, cols)
    staged = pltpu.VMEM((blocks, count, rows + PAD, 128), F32)
    return pl.pallas_call(
        body,
        in_specs=[ANY] * 3,
        out_specs=[VMEM] * 7,
        out_shape=[field] * 5 + [in_vmem(3, count, cols), in_vmem(6, count, 128)],
        scratch_shapes=[staged] * 3 + [pltpu.SemaphoreType.DMA((2, 3, blocks))],
        name="interior",
        compiler_params=room(12),
    )(*(far_off(x) for x in (coh, gx, gy)))


def join(above, below, r, v, u, wx, wy, extra, mom):
    rows, count, cols = r.shape

    def body(ab, be, r_in, v_in, u_in, wx_ref, wy_ref, ex, m_in, r_out, v_out, u_out, out):
        end = rows - 1
        rr, vv, uu = ({}, {}, {})
        gx_w, gy_w = ({}, {})
        for i in (0, 1, 2, 3, end - 3, end - 2, end - 1, end):
            gx_w[i] = wx_ref[i]
            if i != end:
                gy_w[i] = wy_ref[i]
        gx_w[-1] = col_weights(ab[4])
        gy_w[-1] = ab[4] * ex[0]
        gy_w[-2] = ab[3] * ab[4]
        gy_w[end] = ex[1] * be[3]
        gy_w[end + 1] = be[3] * be[4]
        gy_w[end + 2] = be[4] * be[5]
        gx_w[end + 1] = col_weights(be[3])
        gx_w[end + 2] = col_weights(be[4])
        top = gy_w[-1] * ab[2]
        low = gy_w[end] * ex[2]
        rr[-2] = ab[0]
        rr[-1] = ab[1] - top
        rr[0] = r_in[0] + top
        rr[1], rr[2] = (r_in[1], r_in[2])
        rr[end - 2], rr[end - 1] = (r_in[end - 2], r_in[end - 1])
        rr[end] = r_in[end] - low
        rr[end + 1] = be[0] + low
        rr[end + 2] = be[1]
        rr[end + 3] = be[2]
        r_out[0] = rr[0]
        r_out[end] = rr[end]

        def applied(f, i):
            return (
                col_part(gx_w[i], f[i]) + gy_w[i] * (f[i] - f[i + 1]) - gy_w[i - 1] * (f[i - 1] - f[i])
            )

        sums = [m_in[j] for j in range(6)]

        def add(j, x):
            sums[j] = sums[j] + folded(x)

        for i in (-1, 0, 1, end - 1, end, end + 1, end + 2):
            vv[i] = applied(rr, i)
            if 0 <= i <= end:
                v_out[i] = vv[i]
        vv[2], vv[3] = (v_in[2], v_in[3])
        vv[end - 2], vv[end - 3] = (v_in[end - 2], v_in[end - 3])
        for i in (0, 1, 2, end - 2, end - 1, end, end + 1):
            uu[i] = applied(vv, i)
            if i <= end:
                u_out[i] = uu[i]
        uu[3], uu[end - 3] = (u_in[3], u_in[end - 3])
        for i in (0, end):
            add(0, rr[i] * rr[i])
        for i in (0, 1, end - 1, end):
            add(1, rr[i] * vv[i])
            add(2, vv[i] * vv[i])
        for i in (0, 1, 2, end - 2, end - 1, end):
            add(3, vv[i] * uu[i])
            add(4, uu[i] * uu[i])
            d = uu[i] - next_col(uu[i])
            h = uu[i] - uu[i + 1]
            add(5, gx_w[i] * d * d + gy_w[i] * h * h)
        h = uu[end - 3] - uu[end - 2]
        add(5, gy_w[end - 3] * h * h)
        lane = lax.broadcasted_iota(jnp.int32, (count, 128), 1)
        line = jnp.zeros((count, 128), F32)
        for j in range(6):
            line = jnp.where(lane == j, jnp.sum(sums[j], axis=1, keepdims=True), line)
        out[...] = line

    field = in_vmem(rows, count, cols)
    return pl.pallas_call(
        body,
        in_specs=[VMEM] * 9,
        out_specs=[VMEM] * 4,
        out_shape=[field] * 3 + [in_vmem(count, 128)],
        input_output_aliases={2: 0, 3: 1, 4: 2},
        name="join",
        compiler_params=room(4),
    )(near(above), near(below), r, v, u, wx, wy, extra, mom)


def iterate(r, v, u, shares, groups, widths):
    rows, count, cols = r.shape
    high = rows // groups
    number = len(shares)

    def body(*refs):
        r_ref, v_ref, u_ref = refs[:3]
        terms = [ref[...] for ref in refs[3 : 3 + number]]
        out, keep, beside, *far = refs[3 + number : -2]
        whole, sem = refs[-2:]
        while len(terms) > 1:
            terms = [sum(terms[i : i + 2][1:], terms[i]) for i in range(0, len(terms), 2)]
        m = terms[0]
        m0, m1, m2, m3, m4, m5 = (m[:, j : j + 1] for j in range(6))
        a00 = damping * m0 + m1
        a01 = damping * m1 + m2
        a02 = damping * m2 + m3
        a12 = damping * m3 + m4
        a22 = damping * m4 + m5

        def over(a, b, good):
            return jnp.where(good, a / jnp.where(good, b, 1.0), 0.0)

        ok0 = a00 > 0.0
        l10 = over(a01, a00, ok0)
        l20 = over(a02, a00, ok0)
        d1 = a02 - l10 * a01
        e12 = a12 - l10 * a02
        ok1 = d1 > TINY * a02
        l21 = over(e12, d1, ok1)
        d2 = a22 - l20 * a02 - l21 * e12
        ok2 = ok1 & (d2 > TINY * a22)
        y1 = m1 - l10 * m0
        y2 = m2 - l20 * m0 - l21 * y1
        c2 = over(y2, d2, ok2)
        c1 = over(y1, d1, ok1) - l21 * c2
        c0 = over(m0, a00, ok0) - l10 * c1 - l20 * c2
        c0, c1, c2 = (jnp.broadcast_to(c, (count, cols)) for c in (c0, c1, c2))
        _, me = half_and_member(groups)

        def put(ref, at, pitch, x):
            for b in range(ref.shape[0]):
                ref.at[b].reshape(count * pitch, 128)[pl.ds(at, count, stride=pitch), :] = x[
                    :, 128 * b : 128 * b + 128
                ]

        def rows_for(mask, pieces):
            first = jnp.bitwise_xor(me, mask) * high
            for a in range(high):
                at = first + a
                x = c0 * r_ref[at] + c1 * v_ref[at] + c2 * u_ref[at]
                put(whole, at, rows + PAD, x)
                left = 0
                for piece in pieces:
                    wide = 128 * piece.shape[0]
                    put(piece, a, high, x[:, left : left + wide])
                    left += wide

        rows_for(0, [keep])
        rows_for(1, [beside])
        for mask in range(2, groups):
            rows_for(mask, [far[(mask - 2) * len(widths) + i] for i in range(len(widths))])
        copies = [
            pltpu.make_async_copy(
                whole.at[b, :, pl.ds(0, rows), :], out.at[:, :, pl.ds(128 * b, 128)], sem.at[b]
            )
            for b in range(cols // 128)
        ]
        for copy in copies:
            copy.start()
        for copy in copies:
            copy.wait()

    return pl.pallas_call(
        body,
        in_specs=[VMEM] * (3 + number),
        out_specs=[ANY] + [VMEM] * (2 + (groups - 2) * len(widths)),
        out_shape=[jax.ShapeDtypeStruct((count, rows, cols), F32)]
        + [in_vmem(cols // 128, count, high, 128)] * 2
        + [in_vmem(wide // 128, count, high, 128) for _ in range(groups - 2) for wide in widths],
        scratch_shapes=[
            pltpu.VMEM((cols // 128, count, rows + PAD, 128), F32),
            pltpu.SemaphoreType.DMA((cols // 128,)),
        ],
        name="iterate",
        compiler_params=room(6),
    )(r, v, u, *(near(x) for x in shares))


def half_sums(mapping, left, fields, start=None):
    groups = len(fields)
    blocks, count, high, _ = fields[-1].shape
    dates = DATES // 2
    share = dates // groups
    spots = [(b, a) for b in range(blocks) for a in range(0, high, 8)]

    def body(map_ref, *refs):
        us = refs[:groups]

        def sums_of(ds, accs):
            for m in range(groups):
                base = 0 if us[m].shape[0] == blocks else left // 128
                for k in range(count):
                    column = m * count + k
                    ws = [map_ref[d, column] for d in ds]
                    for i, (b, a) in enumerate(spots):
                        u = us[m][base + b, k, a : a + 8, :]
                        for acc, w in zip(accs, ws):
                            acc[i] = acc[i] + w * u
            return accs

        def store(out, d, acc):
            for (b, a), x in zip(spots, acc):
                out[b, d, a : a + 8, :] = x

        def pair_of(first, out, begin):
            def step(i, _):
                at = [2 * i, 2 * i + 1]
                for d, acc in zip(at, sums_of([first + d for d in at], [begin(d) for d in at])):
                    store(out, d, acc)
                return 0

            return step

        if start is None:
            none = lambda d: [jnp.zeros((8, 128), F32) for _ in spots]
            lax.fori_loop(0, dates // 2, pair_of(0, refs[groups], none), 0)
        else:
            me = half_and_member(groups)[1]
            begun = refs[groups]
            for m, out in enumerate(refs[groups + 1 :]):
                first = jnp.bitwise_xor(me, m) * share
                begin = lambda d, first=first: [begun[b, first + d, a : a + 8, :] for b, a in spots]
                lax.fori_loop(0, share // 2, pair_of(dates + m * share, out, begin), 0)

    args = list(fields) + ([] if start is None else [start])
    out_shape = (
        [in_vmem(blocks, dates, high, 128)]
        if start is None
        else [in_vmem(blocks, share, high, 128)] * groups
    )
    return pl.pallas_call(
        body,
        in_specs=[SMEM] + [VMEM] * len(args),
        out_specs=[VMEM] * len(out_shape),
        out_shape=out_shape,
        name="cross_sums" if start is None else "own_sums",
        compiler_params=room(4),
    )(mapping, *(near(x) for x in args))


def assemble(parts, rows, cols):
    groups = len(parts[0])
    _, dates, high, _ = parts[0][0].shape
    flat = [x for chunk in parts for x in chunk]

    def body(*refs):
        _, me = half_and_member(groups)
        out = refs[-1]
        left = 0
        for i in range(len(parts)):
            blocks = parts[i][0].shape[0]
            for m in range(groups):
                first = pl.multiple_of(jnp.bitwise_xor(me, m) * high, 8)
                for b in range(blocks):
                    at = left + 128 * b
                    out[:, pl.ds(first, high), at : at + 128] = refs[i * groups + m][b]
            left += 128 * blocks

    return pl.pallas_call(
        body,
        in_specs=[VMEM] * len(flat),
        out_specs=VMEM,
        out_shape=jax.ShapeDtypeStruct((dates, rows, cols), F32),
        name="assemble",
        compiler_params=room(4),
    )(*(near(x) for x in flat))


def exchange(x, axis, mask):
    size = lax.axis_size(axis)
    return lax.ppermute(x, axis, [(i, i ^ mask) for i in range(size)])


def summands(x, axis):
    size, bit, terms = (lax.axis_size(axis), 1, [x])
    while bit < size:
        if len(terms) > 1:
            terms = [(terms[0] + terms[1]) + (terms[2] + terms[3])]
        masks = [bit, 2 * bit, 3 * bit] if 4 * bit <= size else [bit]
        terms = terms + [exchange(terms[0], axis, m) for m in masks]
        bit *= len(masks) + 1
    return terms


def on_device(grad_x, grad_y, coherence, pairs):
    strips, size = (lax.axis_size("strip"), lax.axis_size("ifg"))
    _, rows, cols = coherence.shape
    groups = size // 2
    widths = [cols * part // sum(SLICES) for part in SLICES]
    down, up = edges(coherence, grad_x, grad_y)
    forward = [(i, i + 1) for i in range(strips - 1)]
    above = lax.ppermute(down, "strip", forward)
    below = lax.ppermute(up, "strip", [(j, i) for i, j in forward])
    fields = interior(coherence, grad_x, grad_y)
    r, v, u, moments = join(above, below, *fields)
    shares = summands(moments, "strip")
    mapping = inverse_map(pairs, groups)
    phase, keep, beside, *far = iterate(r, v, u, shares, groups, widths)
    beside = exchange(beside, "ifg", 1)
    parts, left = ([], 0)
    for i, wide in enumerate(widths):
        mine = [keep, beside]
        for m in range(2, groups):
            mine.append(exchange(far[(m - 2) * CHUNKS + i], "ifg", m))
        (other,) = half_sums(mapping, left, mine)
        other = exchange(other, "ifg", groups)
        full = half_sums(mapping, left, mine, other)
        part = [full[0]]
        for m in range(1, groups):
            part.append(exchange(full[m], "ifg", m))
        parts.append(part)
        left += wide
    return (phase, assemble(parts, rows, cols))


def solution(mesh):
    in_specs = (P("ifg", "strip", None), P("ifg", "strip", None), P("ifg", "strip", None), P())
    out_specs = (P("ifg", "strip", None), P("ifg", "strip", None))

    return jax.shard_map(on_device, mesh=mesh, in_specs=in_specs, out_specs=out_specs, check_vma=False)
```

profile of v0, /device:TPU:0, one launch (start us, length us, event | category | flops | bytes accessed | tf_op | source)
XLA Modules:
  0.0 123.4 jit_solution(6174403678699650529)
XLA Ops:
  0.6 2.2 %edges.1 = (f32[5,8,1024]{2,1,0:T(8,128)S(1)}, f32[6,8,1024]{2,1,0:T(8,128)S(1)}) custom-call(f32[8,64,1024]{2,1,0:T(8,128)} %c_hbm.1, f32[8,64,1024]{2,1,0:T(8,128)} %x_hbm.1, f32[8,64,1024]{2,1,0:T(8,128)} %y_hbm.1, f32[8,64,1024]{2,1,0:T(8,128)} %c_hbm.1, f32[8,64,1024]{2,1,0:T(8,128)} %x_hbm.1, f32[8,64,1024]{2,1,0:T(8,128)} %y_hbm.1), custom_call_target="tpu_custom_call" | custom-call | tf_op jit(solution)/shard_map/edges/pallas_call | solution.py:150
  2.8 1.3 %collective-permute-start.1 = (f32[6,8,1024]{2,1,0:T(8,128)S(1)}, f32[6,8,1024]{2,1,0:T(8,128)S(1)}, u32[]{:S(2)}, u32[]{:S(2)}) collective-permute-start(f32[6,8,1024]{2,1,0:T(8,128)S(1)} %get-tuple-element.49), channel_id=1, source_target_pairs={{1,0},{2,1},{3,2},{5,4},{6,5},{7,6},{9,8},{10,9},{11,10},{13,12},{... | collective-permute-start | bytes 589832 | tf_op jit(solution)/shard_map/ppermute | solution.py:574
  4.1 5.5 %collective-permute-start = (f32[5,8,1024]{2,1,0:T(8,128)S(1)}, f32[5,8,1024]{2,1,0:T(8,128)S(1)}, u32[]{:S(2)}, u32[]{:S(2)}) collective-permute-start(f32[5,8,1024]{2,1,0:T(8,128)S(1)} %get-tuple-element.48), channel_id=1, source_target_pairs={{0,1},{1,2},{2,3},{4,5},{5,6},{6,7},{8,9},{9,10},{10,11},{12,13},{... | collective-permute-start | bytes 491528 | tf_op jit(solution)/shard_map/ppermute | solution.py:573
  9.6 13.0 %interior.1 = (f32[64,8,1024]{2,1,0:T(8,128)S(1)}, f32[64,8,1024]{2,1,0:T(8,128)S(1)}, f32[64,8,1024]{2,1,0:T(8,128)S(1)}, f32[64,8,1024]{2,1,0:T(8,128)S(1)}, f...) custom-call(f32[8,64,1024]{2,1,0:T(8,128)} %c_hbm.1, f32[8,64,1024]{2,1,0:T(8,128)} %x_hbm.1, ...), custom_call_target="tpu_custom_call" | custom-call | tf_op jit(solution)/shard_map/interior/pallas_call | solution.py:275
  22.6 0.0 collective-permute-done.ab
  22.6 0.9 join.1
  23.6 2.9 %collective-permute-start.2 = (f32[8,128]{1,0:T(8,128)S(1)}, f32[8,128]{1,0:T(8,128)S(1)}, u32[]{:S(2)}, u32[]{:S(2)}) collective-permute-start(f32[8,128]{1,0:T(8,128)S(1)} %get-tuple-element.60.refs_3_), channel_id=1, source_target_pairs={{0,1},{1,0},{2,3},{3,2},{4,5},{5,4},{6,7},{7,6},{8,9},{9,8},{10,11... | collective-permute-start | bytes 12296 | tf_op jit(solution)/shard_map/ppermute | solution.py:552
  26.5 0.0 collective-permute-start.3
  26.5 1.5 %collective-permute-start.4 = (f32[8,128]{1,0:T(8,128)S(1)}, f32[8,128]{1,0:T(8,128)S(1)}, u32[]{:S(2)}, u32[]{:S(2)}) collective-permute-start(f32[8,128]{1,0:T(8,128)S(1)} %get-tuple-element.60.refs_3_), channel_id=1, source_target_pairs={{0,3},{1,2},{2,1},{3,0},{4,7},{5,6},{6,5},{7,4},{8,11},{9,10},{10,... | collective-permute-start | bytes 12296 | tf_op jit(solution)/shard_map/ppermute | solution.py:552
  28.0 0.0 collective-permute-done.2.refs_4_
  28.1 2.0 %collective-permute-done.3.refs_5_ = f32[8,128]{1,0:T(8,128)S(1)} collective-permute-done((f32[8,128]{1,0:T(8,128)S(1)}, f32[8,128]{1,0:T(8,128)S(1)}, u32[]{:S(2)}, u32[]{:S(2)}) %collective-permute-start.3) | collective-permute-done | bytes 4128 | tf_op jit(solution)/shard_map/ppermute | solution.py:552
  30.1 0.9 collective-permute-done.4.refs_6_
  31.0 3.8 %iterate.1 = (f32[8,64,1024]{2,1,0:T(8,128)}, f32[8,8,16,128]{3,2,1,0:T(8,128)S(1)}, f32[8,8,16,128]{3,2,1,0:T(8,128)S(1)}, f32[1,8,16,128]{3,2,1,0:T(8,128)S(1)...) custom-call(f32[64,8,1024]{2,1,0:T(8,128)S(1)} %get-tuple-element.57, ...), custom_call_target="tpu_custom_call" | custom-call | tf_op jit(solution)/shard_map/iterate/pallas_call | solution.py:444
  34.8 0.1 collective-permute-start.5
  34.9 1.6 %collective-permute-start.24 = (f32[2,8,16,128]{3,2,1,0:T(8,128)S(1)}, f32[2,8,16,128]{3,2,1,0:T(8,128)S(1)}, u32[]{:S(2)}, u32[]{:S(2)}) collective-permute-start(f32[2,8,16,128]{3,2,1,0:T(8,128)S(1)} %get-tuple-element.82), channel_id=1, source_target_pairs={{0,8},{4,12},{8,0},{12,4},{16,24},{20,28},{24,16},{28,20},{1,9},{5... | collective-permute-start | bytes 393224 | tf_op jit(solution)/shard_map/ppermute | solution.py:552
  36.5 0.2 collective-permute-start.25
  36.7 1.6 %collective-permute-start.18 = (f32[2,8,16,128]{3,2,1,0:T(8,128)S(1)}, f32[2,8,16,128]{3,2,1,0:T(8,128)S(1)}, u32[]{:S(2)}, u32[]{:S(2)}) collective-permute-start(f32[2,8,16,128]{3,2,1,0:T(8,128)S(1)} %get-tuple-element.76), channel_id=1, source_target_pairs={{0,8},{4,12},{8,0},{12,4},{16,24},{20,28},{24,16},{28,20},{1,9},{5... | collective-permute-start | bytes 393224 | tf_op jit(solution)/shard_map/ppermute | solution.py:552
  38.3 0.1 collective-permute-start.19
  38.4 2.9 %collective-permute-done.24.refs_2_ = f32[2,8,16,128]{3,2,1,0:T(8,128)S(1)} collective-permute-done((f32[2,8,16,128]{3,2,1,0:T(8,128)S(1)}, f32[2,8,16,128]{3,2,1,0:T(8,128)S(1)}, u32[]{:S(2)}, u32[]{:S(2)}) %collective-permute-start.24) | collective-permute-done | bytes 131104 | tf_op jit(solution)/shard_map/ppermute | solution.py:552
  41.3 1.6 %collective-permute-start.12 = (f32[2,8,16,128]{3,2,1,0:T(8,128)S(1)}, f32[2,8,16,128]{3,2,1,0:T(8,128)S(1)}, u32[]{:S(2)}, u32[]{:S(2)}) collective-permute-start(f32[2,8,16,128]{3,2,1,0:T(8,128)S(1)} %get-tuple-element.70), channel_id=1, source_target_pairs={{0,8},{4,12},{8,0},{12,4},{16,24},{20,28},{24,16},{28,20},{1,9},{5... | collective-permute-start | bytes 393224 | tf_op jit(solution)/shard_map/ppermute | solution.py:552
  42.9 0.3 collective-permute-done.25.refs_3_
  43.2 1.9 %collective-permute-start.13 = (f32[2,8,16,128]{3,2,1,0:T(8,128)S(1)}, f32[2,8,16,128]{3,2,1,0:T(8,128)S(1)}, u32[]{:S(2)}, u32[]{:S(2)}) collective-permute-start(f32[2,8,16,128]{3,2,1,0:T(8,128)S(1)} %get-tuple-element.71), channel_id=1, source_target_pairs={{0,12},{4,8},{8,4},{12,0},{16,28},{20,24},{24,20},{28,16},{1,13},{... | collective-permute-start | bytes 393224 | tf_op jit(solution)/shard_map/ppermute | solution.py:552
  45.1 1.8 %collective-permute-done.18.refs_2_ = f32[2,8,16,128]{3,2,1,0:T(8,128)S(1)} collective-permute-done((f32[2,8,16,128]{3,2,1,0:T(8,128)S(1)}, f32[2,8,16,128]{3,2,1,0:T(8,128)S(1)}, u32[]{:S(2)}, u32[]{:S(2)}) %collective-permute-start.18) | collective-permute-done | bytes 131104 | tf_op jit(solution)/shard_map/ppermute | solution.py:552
  46.9 1.6 %collective-permute-start.30 = (f32[1,8,16,128]{3,2,1,0:T(8,128)S(1)}, f32[1,8,16,128]{3,2,1,0:T(8,128)S(1)}, u32[]{:S(2)}, u32[]{:S(2)}) collective-permute-start(f32[1,8,16,128]{3,2,1,0:T(8,128)S(1)} %get-tuple-element.88), channel_id=1, source_target_pairs={{0,8},{4,12},{8,0},{12,4},{16,24},{20,28},{24,16},{28,20},{1,9},{5... | collective-permute-start | bytes 196616 | tf_op jit(solution)/shard_map/ppermute | solution.py:552
  48.5 3.0 %inverse_map.1.map_ref = f32[32,32]{1,0:T(8,128)S(1)} custom-call(s32[2,64]{1,0:T(2,128)S(1)} %bitcast.1), custom_call_target="tpu_custom_call" | custom-call | tf_op jit(solution)/shard_map/inverse_map/pallas_call | solution.py:111
  51.5 1.6 %cross_sums.8 = f32[2,16,16,128]{3,2,1,0:T(8,128)S(1)} custom-call(f32[32,32]{1,0:T(8,128)S(1)} %inverse_map.1.map_ref, f32[8,8,16,128]{3,2,1,0:T(8,128)S(1)} %get-tuple-element.62.refs_0_, f32[8,8,16,128]{3,2,1,0:T(8,128)S(1)} %collective-permute-done.5.refs_1_, f32[2,8,16,128]{3,2,1,0:T(8,128)S(1)} %collective-permute-done.24.refs_2_, ...), custom_call_target="tpu_custom_call" | custom-call | tf_op jit(solution)/shard_map/cross_sums/pallas_call | solution.py:512
  53.2 2.7 %collective-permute-start.26 = (f32[2,16,16,128]{3,2,1,0:T(8,128)S(1)}, f32[2,16,16,128]{3,2,1,0:T(8,128)S(1)}, u32[]{:S(2)}, u32[]{:S(2)}) collective-permute-start(f32[2,16,16,128]{3,2,1,0:T(8,128)S(1)} %cross_sums.8), channel_id=1, source_target_pairs={{0,16},{4,20},{8,24},{12,28},{16,0},{20,4},{24,8},{28,12},{1,17},{... | collective-permute-start | bytes 786440 | tf_op jit(solution)/shard_map/ppermute | solution.py:552
  55.8 1.6 %cross_sums.7 = f32[2,16,16,128]{3,2,1,0:T(8,128)S(1)} custom-call(f32[32,32]{1,0:T(8,128)S(1)} %inverse_map.1.map_ref, f32[8,8,16,128]{3,2,1,0:T(8,128)S(1)} %get-tuple-element.62.refs_0_, f32[8,8,16,128]{3,2,1,0:T(8,128)S(1)} %collective-permute-done.5.refs_1_, f32[2,8,16,128]{3,2,1,0:T(8,128)S(1)} %collective-permute-done.18.refs_2_, ...), custom_call_target="tpu_custom_call" | custom-call | tf_op jit(solution)/shard_map/cross_sums/pallas_call | solution.py:512
  57.4 0.4 collective-permute-start.20
  57.8 0.5 collective-permute-start.6
  58.3 1.6 %cross_sums.6 = f32[2,16,16,128]{3,2,1,0:T(8,128)S(1)} custom-call(f32[32,32]{1,0:T(8,128)S(1)} %inverse_map.1.map_ref, f32[8,8,16,128]{3,2,1,0:T(8,128)S(1)} %get-tuple-element.62.refs_0_, f32[8,8,16,128]{3,2,1,0:T(8,128)S(1)} %collective-permute-done.5.refs_1_, f32[2,8,16,128]{3,2,1,0:T(8,128)S(1)} %collective-permute-done.12.refs_2_, ...), custom_call_target="tpu_custom_call" | custom-call | tf_op jit(solution)/shard_map/cross_sums/pallas_call | solution.py:512
  59.9 1.0 collective-permute-start.7
  60.9 2.6 %collective-permute-start.14 = (f32[2,16,16,128]{3,2,1,0:T(8,128)S(1)}, f32[2,16,16,128]{3,2,1,0:T(8,128)S(1)}, u32[]{:S(2)}, u32[]{:S(2)}) collective-permute-start(f32[2,16,16,128]{3,2,1,0:T(8,128)S(1)} %cross_sums.6), channel_id=1, source_target_pairs={{0,16},{4,20},{8,24},{12,28},{16,0},{20,4},{24,8},{28,12},{1,17},{... | collective-permute-start | bytes 786440 | tf_op jit(solution)/shard_map/ppermute | solution.py:552
  63.4 1.3 %cross_sums.9 = f32[1,16,16,128]{3,2,1,0:T(8,128)S(1)} custom-call(f32[32,32]{1,0:T(8,128)S(1)} %inverse_map.1.map_ref, f32[8,8,16,128]{3,2,1,0:T(8,128)S(1)} %get-tuple-element.62.refs_0_, f32[8,8,16,128]{3,2,1,0:T(8,128)S(1)} %collective-permute-done.5.refs_1_, f32[1,8,16,128]{3,2,1,0:T(8,128)S(1)} %collective-permute-done.30.refs_2_, ...), custom_call_target="tpu_custom_call" | custom-call | tf_op jit(solution)/shard_map/cross_sums/pallas_call | solution.py:512
  64.8 4.9 %collective-permute-done.6.refs_2_ = f32[1,8,16,128]{3,2,1,0:T(8,128)S(1)} collective-permute-done((f32[1,8,16,128]{3,2,1,0:T(8,128)S(1)}, f32[1,8,16,128]{3,2,1,0:T(8,128)S(1)}, u32[]{:S(2)}, u32[]{:S(2)}) %collective-permute-start.6) | collective-permute-done | bytes 65568 | tf_op jit(solution)/shard_map/ppermute | solution.py:552
  69.6 3.8 %collective-permute-start.32 = (f32[1,16,16,128]{3,2,1,0:T(8,128)S(1)}, f32[1,16,16,128]{3,2,1,0:T(8,128)S(1)}, u32[]{:S(2)}, u32[]{:S(2)}) collective-permute-start(f32[1,16,16,128]{3,2,1,0:T(8,128)S(1)} %cross_sums.9), channel_id=1, source_target_pairs={{0,16},{4,20},{8,24},{12,28},{16,0},{20,4},{24,8},{28,12},{1,17},{... | collective-permute-start | bytes 393224 | tf_op jit(solution)/shard_map/ppermute | solution.py:552
  73.4 1.3 %cross_sums.5 = f32[1,16,16,128]{3,2,1,0:T(8,128)S(1)} custom-call(f32[32,32]{1,0:T(8,128)S(1)} %inverse_map.1.map_ref, f32[8,8,16,128]{3,2,1,0:T(8,128)S(1)} %get-tuple-element.62.refs_0_, f32[8,8,16,128]{3,2,1,0:T(8,128)S(1)} %collective-permute-done.5.refs_1_, f32[1,8,16,128]{3,2,1,0:T(8,128)S(1)} %collective-permute-done.6.refs_2_, ...), custom_call_target="tpu_custom_call" | custom-call | tf_op jit(solution)/shard_map/cross_sums/pallas_call | solution.py:512
  74.7 0.4 collective-permute-start.8
  75.1 24.8 %collective-permute-done.32.refs_4_ = f32[1,16,16,128]{3,2,1,0:T(8,128)S(1)} collective-permute-done((f32[1,16,16,128]{3,2,1,0:T(8,128)S(1)}, f32[1,16,16,128]{3,2,1,0:T(8,128)S(1)}, u32[]{:S(2)}, u32[]{:S(2)}) %collective-permute-start.32) | collective-permute-done | bytes 131104 | tf_op jit(solution)/shard_map/ppermute | solution.py:552
  99.9 1.3 %own_sums.9 = (f32[1,4,16,128]{3,2,1,0:T(8,128)S(1)}, f32[1,4,16,128]{3,2,1,0:T(8,128)S(1)}, f32[1,4,16,128]{3,2,1,0:T(8,128)S(1)}, f32[1,4,16,128]{3,2,1,0:T(8,128)S(1)}) custom-call(f32[32,32]{1,0:T(8,128)S(1)} %inverse_map.1.map_ref, f32[8,8,16,128]{3,2,1,0:T(8,128)S(1)} %get-tuple-element.62.refs_0_, ...), custom_call_target="tpu_custom_call" | custom-call | tf_op jit(solution)/shard_map/own_sums/pallas_call | solution.py:512
  101.1 0.1 collective-permute-start.33
  101.2 1.1 collective-permute-done.8.refs_4_
  102.3 1.3 %own_sums.5 = (f32[1,4,16,128]{3,2,1,0:T(8,128)S(1)}, f32[1,4,16,128]{3,2,1,0:T(8,128)S(1)}, f32[1,4,16,128]{3,2,1,0:T(8,128)S(1)}, f32[1,4,16,128]{3,2,1,0:T(8,128)S(1)}) custom-call(f32[32,32]{1,0:T(8,128)S(1)} %inverse_map.1.map_ref, f32[8,8,16,128]{3,2,1,0:T(8,128)S(1)} %get-tuple-element.62.refs_0_, ...), custom_call_target="tpu_custom_call" | custom-call | tf_op jit(solution)/shard_map/own_sums/pallas_call | solution.py:512
  103.6 1.1 collective-permute-start.35
  104.7 1.1 collective-permute-start.10
  105.7 1.4 %collective-permute-start.11 = (f32[1,4,16,128]{3,2,1,0:T(8,128)S(1)}, f32[1,4,16,128]{3,2,1,0:T(8,128)S(1)}, u32[]{:S(2)}, u32[]{:S(2)}) collective-permute-start(f32[1,4,16,128]{3,2,1,0:T(8,128)S(1)} %get-tuple-element.69), channel_id=1, source_target_pairs={{0,12},{4,8},{8,4},{12,0},{16,28},{20,24},{24,20},{28,16},{1,13},{... | collective-permute-start | bytes 98312 | tf_op jit(solution)/shard_map/ppermute | solution.py:552
  107.1 1.6 %own_sums.8 = (f32[2,4,16,128]{3,2,1,0:T(8,128)S(1)}, f32[2,4,16,128]{3,2,1,0:T(8,128)S(1)}, f32[2,4,16,128]{3,2,1,0:T(8,128)S(1)}, f32[2,4,16,128]{3,2,1,0:T(8,128)S(1)}) custom-call(f32[32,32]{1,0:T(8,128)S(1)} %inverse_map.1.map_ref, f32[8,8,16,128]{3,2,1,0:T(8,128)S(1)} %get-tuple-element.62.refs_0_, ...), custom_call_target="tpu_custom_call" | custom-call | tf_op jit(solution)/shard_map/own_sums/pallas_call | solution.py:512
  108.7 1.6 %own_sums.7 = (f32[2,4,16,128]{3,2,1,0:T(8,128)S(1)}, f32[2,4,16,128]{3,2,1,0:T(8,128)S(1)}, f32[2,4,16,128]{3,2,1,0:T(8,128)S(1)}, f32[2,4,16,128]{3,2,1,0:T(8,128)S(1)}) custom-call(f32[32,32]{1,0:T(8,128)S(1)} %inverse_map.1.map_ref, f32[8,8,16,128]{3,2,1,0:T(8,128)S(1)} %get-tuple-element.62.refs_0_, ...), custom_call_target="tpu_custom_call" | custom-call | tf_op jit(solution)/shard_map/own_sums/pallas_call | solution.py:512
  110.3 0.1 collective-permute-start.27
  110.3 0.7 collective-permute-start.28
  111.1 1.1 collective-permute-start.29
  112.2 0.4 collective-permute-start.21
  112.6 0.1 collective-permute-start.9
  112.7 1.6 %own_sums.6 = (f32[2,4,16,128]{3,2,1,0:T(8,128)S(1)}, f32[2,4,16,128]{3,2,1,0:T(8,128)S(1)}, f32[2,4,16,128]{3,2,1,0:T(8,128)S(1)}, f32[2,4,16,128]{3,2,1,0:T(8,128)S(1)}) custom-call(f32[32,32]{1,0:T(8,128)S(1)} %inverse_map.1.map_ref, f32[8,8,16,128]{3,2,1,0:T(8,128)S(1)} %get-tuple-element.62.refs_0_, ...), custom_call_target="tpu_custom_call" | custom-call | tf_op jit(solution)/shard_map/own_sums/pallas_call | solution.py:512
  114.3 0.7 collective-permute-start.22
  114.9 1.1 collective-permute-start.23
  116.1 0.4 collective-permute-start.15
  116.5 0.6 collective-permute-start.16
  117.1 0.8 collective-permute-start.17
  117.9 1.4 %collective-permute-done.22.refs_10_ = f32[2,4,16,128]{3,2,1,0:T(8,128)S(1)} collective-permute-done((f32[2,4,16,128]{3,2,1,0:T(8,128)S(1)}, f32[2,4,16,128]{3,2,1,0:T(8,128)S(1)}, u32[]{:S(2)}, u32[]{:S(2)}) %collective-permute-start.22) | collective-permute-done | bytes 65568 | tf_op jit(solution)/shard_map/ppermute | solution.py:552
  119.3 0.2 collective-permute-done.23.refs_11_
  119.5 2.6 %collective-permute-done.16.refs_6_ = f32[2,4,16,128]{3,2,1,0:T(8,128)S(1)} collective-permute-done((f32[2,4,16,128]{3,2,1,0:T(8,128)S(1)}, f32[2,4,16,128]{3,2,1,0:T(8,128)S(1)}, u32[]{:S(2)}, u32[]{:S(2)}) %collective-permute-start.16) | collective-permute-done | bytes 65568 | tf_op jit(solution)/shard_map/ppermute | solution.py:552
  122.1 0.2 collective-permute-done.17.refs_7_
  122.3 1.1 assemble.1
  (26 shorter events, 0.1 us)
Async XLA Ops:
  2.8 19.8 %collective-permute-start.1 = (f32[6,8,1024]{2,1,0:T(8,128)S(1)}, f32[6,8,1024]{2,1,0:T(8,128)S(1)}, u32[]{:S(2)}, u32[]{:S(2)}) collective-permute-start(f32[6,8,1024]{2,1,0:T(8,128)S(1)} %get-tuple-element.49), channel_id=1, source_target_pairs={{1,0},{2,1},{3,2},{5,4},{6,5},{7,6},{9,8},{10,9},{11,10},{13,12},{... | collective-permute-start | bytes 589832 | tf_op jit(solution)/shard_map/ppermute | solution.py:574
  4.1 18.5 %collective-permute-start = (f32[5,8,1024]{2,1,0:T(8,128)S(1)}, f32[5,8,1024]{2,1,0:T(8,128)S(1)}, u32[]{:S(2)}, u32[]{:S(2)}) collective-permute-start(f32[5,8,1024]{2,1,0:T(8,128)S(1)} %get-tuple-element.48), channel_id=1, source_target_pairs={{0,1},{1,2},{2,3},{4,5},{5,6},{6,7},{8,9},{9,10},{10,11},{12,13},{... | collective-permute-start | bytes 491528 | tf_op jit(solution)/shard_map/ppermute | solution.py:573
  23.6 4.5 %collective-permute-start.2 = (f32[8,128]{1,0:T(8,128)S(1)}, f32[8,128]{1,0:T(8,128)S(1)}, u32[]{:S(2)}, u32[]{:S(2)}) collective-permute-start(f32[8,128]{1,0:T(8,128)S(1)} %get-tuple-element.60.refs_3_), channel_id=1, source_target_pairs={{0,1},{1,0},{2,3},{3,2},{4,5},{5,4},{6,7},{7,6},{8,9},{9,8},{10,11... | collective-permute-start | bytes 12296 | tf_op jit(solution)/shard_map/ppermute | solution.py:552
  26.5 3.6 %collective-permute-start.3 = (f32[8,128]{1,0:T(8,128)S(1)}, f32[8,128]{1,0:T(8,128)S(1)}, u32[]{:S(2)}, u32[]{:S(2)}) collective-permute-start(f32[8,128]{1,0:T(8,128)S(1)} %get-tuple-element.60.refs_3_), channel_id=1, source_target_pairs={{0,2},{1,3},{2,0},{3,1},{4,6},{5,7},{6,4},{7,5},{8,10},{9,11},{10,... | collective-permute-start | bytes 12296 | tf_op jit(solution)/shard_map/ppermute | solution.py:552
  26.5 4.5 %collective-permute-start.4 = (f32[8,128]{1,0:T(8,128)S(1)}, f32[8,128]{1,0:T(8,128)S(1)}, u32[]{:S(2)}, u32[]{:S(2)}) collective-permute-start(f32[8,128]{1,0:T(8,128)S(1)} %get-tuple-element.60.refs_3_), channel_id=1, source_target_pairs={{0,3},{1,2},{2,1},{3,0},{4,7},{5,6},{6,5},{7,4},{8,11},{9,10},{10,... | collective-permute-start | bytes 12296 | tf_op jit(solution)/shard_map/ppermute | solution.py:552
  31.0 17.5 %copy-start = (s32[64,2]{0,1:T(2,128)S(1)}, s32[64,2]{0,1:T(2,128)}, u32[]{:S(2)}) copy-start(s32[64,2]{0,1:T(2,128)} %param.7) | copy-start | bytes 1540
  34.8 13.7 %collective-permute-start.5 = (f32[8,8,16,128]{3,2,1,0:T(8,128)S(1)}, f32[8,8,16,128]{3,2,1,0:T(8,128)S(1)}, u32[]{:S(2)}, u32[]{:S(2)}) collective-permute-start(f32[8,8,16,128]{3,2,1,0:T(8,128)S(1)} %get-tuple-element.63), channel_id=1, source_target_pairs={{0,4},{4,0},{8,12},{12,8},{16,20},{20,16},{24,28},{28,24},{1,5},{5... | collective-permute-start | bytes 1572872 | tf_op jit(solution)/shard_map/ppermute | solution.py:552
  34.9 6.4 %collective-permute-start.24 = (f32[2,8,16,128]{3,2,1,0:T(8,128)S(1)}, f32[2,8,16,128]{3,2,1,0:T(8,128)S(1)}, u32[]{:S(2)}, u32[]{:S(2)}) collective-permute-start(f32[2,8,16,128]{3,2,1,0:T(8,128)S(1)} %get-tuple-element.82), channel_id=1, source_target_pairs={{0,8},{4,12},{8,0},{12,4},{16,24},{20,28},{24,16},{28,20},{1,9},{5... | collective-permute-start | bytes 393224 | tf_op jit(solution)/shard_map/ppermute | solution.py:552
  36.5 6.7 %collective-permute-start.25 = (f32[2,8,16,128]{3,2,1,0:T(8,128)S(1)}, f32[2,8,16,128]{3,2,1,0:T(8,128)S(1)}, u32[]{:S(2)}, u32[]{:S(2)}) collective-permute-start(f32[2,8,16,128]{3,2,1,0:T(8,128)S(1)} %get-tuple-element.83), channel_id=1, source_target_pairs={{0,12},{4,8},{8,4},{12,0},{16,28},{20,24},{24,20},{28,16},{1,13},{... | collective-permute-start | bytes 393224 | tf_op jit(solution)/shard_map/ppermute | solution.py:552
  36.7 10.2 %collective-permute-start.18 = (f32[2,8,16,128]{3,2,1,0:T(8,128)S(1)}, f32[2,8,16,128]{3,2,1,0:T(8,128)S(1)}, u32[]{:S(2)}, u32[]{:S(2)}) collective-permute-start(f32[2,8,16,128]{3,2,1,0:T(8,128)S(1)} %get-tuple-element.76), channel_id=1, source_target_pairs={{0,8},{4,12},{8,0},{12,4},{16,24},{20,28},{24,16},{28,20},{1,9},{5... | collective-permute-start | bytes 393224 | tf_op jit(solution)/shard_map/ppermute | solution.py:552
  38.3 14.9 %collective-permute-start.19 = (f32[2,8,16,128]{3,2,1,0:T(8,128)S(1)}, f32[2,8,16,128]{3,2,1,0:T(8,128)S(1)}, u32[]{:S(2)}, u32[]{:S(2)}) collective-permute-start(f32[2,8,16,128]{3,2,1,0:T(8,128)S(1)} %get-tuple-element.77), channel_id=1, source_target_pairs={{0,12},{4,8},{8,4},{12,0},{16,28},{20,24},{24,20},{28,16},{1,13},{... | collective-permute-start | bytes 393224 | tf_op jit(solution)/shard_map/ppermute | solution.py:552
  41.3 16.1 %collective-permute-start.12 = (f32[2,8,16,128]{3,2,1,0:T(8,128)S(1)}, f32[2,8,16,128]{3,2,1,0:T(8,128)S(1)}, u32[]{:S(2)}, u32[]{:S(2)}) collective-permute-start(f32[2,8,16,128]{3,2,1,0:T(8,128)S(1)} %get-tuple-element.70), channel_id=1, source_target_pairs={{0,8},{4,12},{8,0},{12,4},{16,24},{20,28},{24,16},{28,20},{1,9},{5... | collective-permute-start | bytes 393224 | tf_op jit(solution)/shard_map/ppermute | solution.py:552
  43.2 14.6 %collective-permute-start.13 = (f32[2,8,16,128]{3,2,1,0:T(8,128)S(1)}, f32[2,8,16,128]{3,2,1,0:T(8,128)S(1)}, u32[]{:S(2)}, u32[]{:S(2)}) collective-permute-start(f32[2,8,16,128]{3,2,1,0:T(8,128)S(1)} %get-tuple-element.71), channel_id=1, source_target_pairs={{0,12},{4,8},{8,4},{12,0},{16,28},{20,24},{24,20},{28,16},{1,13},{... | collective-permute-start | bytes 393224 | tf_op jit(solution)/shard_map/ppermute | solution.py:552
  46.9 13.0 %collective-permute-start.30 = (f32[1,8,16,128]{3,2,1,0:T(8,128)S(1)}, f32[1,8,16,128]{3,2,1,0:T(8,128)S(1)}, u32[]{:S(2)}, u32[]{:S(2)}) collective-permute-start(f32[1,8,16,128]{3,2,1,0:T(8,128)S(1)} %get-tuple-element.88), channel_id=1, source_target_pairs={{0,8},{4,12},{8,0},{12,4},{16,24},{20,28},{24,16},{28,20},{1,9},{5... | collective-permute-start | bytes 196616 | tf_op jit(solution)/shard_map/ppermute | solution.py:552
  48.5 12.4 %collective-permute-start.31 = (f32[1,8,16,128]{3,2,1,0:T(8,128)S(1)}, f32[1,8,16,128]{3,2,1,0:T(8,128)S(1)}, u32[]{:S(2)}, u32[]{:S(2)}) collective-permute-start(f32[1,8,16,128]{3,2,1,0:T(8,128)S(1)} %get-tuple-element.89), channel_id=1, source_target_pairs={{0,12},{4,8},{8,4},{12,0},{16,28},{20,24},{24,20},{28,16},{1,13},{... | collective-permute-start | bytes 196616 | tf_op jit(solution)/shard_map/ppermute | solution.py:552
  53.2 51.5 %collective-permute-start.26 = (f32[2,16,16,128]{3,2,1,0:T(8,128)S(1)}, f32[2,16,16,128]{3,2,1,0:T(8,128)S(1)}, u32[]{:S(2)}, u32[]{:S(2)}) collective-permute-start(f32[2,16,16,128]{3,2,1,0:T(8,128)S(1)} %cross_sums.8), channel_id=1, source_target_pairs={{0,16},{4,20},{8,24},{12,28},{16,0},{20,4},{24,8},{28,12},{1,17},{... | collective-permute-start | bytes 786440 | tf_op jit(solution)/shard_map/ppermute | solution.py:552
  57.4 48.3 %collective-permute-start.20 = (f32[2,16,16,128]{3,2,1,0:T(8,128)S(1)}, f32[2,16,16,128]{3,2,1,0:T(8,128)S(1)}, u32[]{:S(2)}, u32[]{:S(2)}) collective-permute-start(f32[2,16,16,128]{3,2,1,0:T(8,128)S(1)} %cross_sums.7), channel_id=1, source_target_pairs={{0,16},{4,20},{8,24},{12,28},{16,0},{20,4},{24,8},{28,12},{1,17},{... | collective-permute-start | bytes 786440 | tf_op jit(solution)/shard_map/ppermute | solution.py:552
  57.8 11.8 %collective-permute-start.6 = (f32[1,8,16,128]{3,2,1,0:T(8,128)S(1)}, f32[1,8,16,128]{3,2,1,0:T(8,128)S(1)}, u32[]{:S(2)}, u32[]{:S(2)}) collective-permute-start(f32[1,8,16,128]{3,2,1,0:T(8,128)S(1)} %get-tuple-element.64), channel_id=1, source_target_pairs={{0,8},{4,12},{8,0},{12,4},{16,24},{20,28},{24,16},{28,20},{1,9},{5... | collective-permute-start | bytes 196616 | tf_op jit(solution)/shard_map/ppermute | solution.py:552
  59.9 13.5 %collective-permute-start.7 = (f32[1,8,16,128]{3,2,1,0:T(8,128)S(1)}, f32[1,8,16,128]{3,2,1,0:T(8,128)S(1)}, u32[]{:S(2)}, u32[]{:S(2)}) collective-permute-start(f32[1,8,16,128]{3,2,1,0:T(8,128)S(1)} %get-tuple-element.65), channel_id=1, source_target_pairs={{0,12},{4,8},{8,4},{12,0},{16,28},{20,24},{24,20},{28,16},{1,13},{... | collective-permute-start | bytes 196616 | tf_op jit(solution)/shard_map/ppermute | solution.py:552
  60.9 51.7 %collective-permute-start.14 = (f32[2,16,16,128]{3,2,1,0:T(8,128)S(1)}, f32[2,16,16,128]{3,2,1,0:T(8,128)S(1)}, u32[]{:S(2)}, u32[]{:S(2)}) collective-permute-start(f32[2,16,16,128]{3,2,1,0:T(8,128)S(1)} %cross_sums.6), channel_id=1, source_target_pairs={{0,16},{4,20},{8,24},{12,28},{16,0},{20,4},{24,8},{28,12},{1,17},{... | collective-permute-start | bytes 786440 | tf_op jit(solution)/shard_map/ppermute | solution.py:552
  69.6 30.3 %collective-permute-start.32 = (f32[1,16,16,128]{3,2,1,0:T(8,128)S(1)}, f32[1,16,16,128]{3,2,1,0:T(8,128)S(1)}, u32[]{:S(2)}, u32[]{:S(2)}) collective-permute-start(f32[1,16,16,128]{3,2,1,0:T(8,128)S(1)} %cross_sums.9), channel_id=1, source_target_pairs={{0,16},{4,20},{8,24},{12,28},{16,0},{20,4},{24,8},{28,12},{1,17},{... | collective-permute-start | bytes 393224 | tf_op jit(solution)/shard_map/ppermute | solution.py:552
  74.7 27.5 %collective-permute-start.8 = (f32[1,16,16,128]{3,2,1,0:T(8,128)S(1)}, f32[1,16,16,128]{3,2,1,0:T(8,128)S(1)}, u32[]{:S(2)}, u32[]{:S(2)}) collective-permute-start(f32[1,16,16,128]{3,2,1,0:T(8,128)S(1)} %cross_sums.5), channel_id=1, source_target_pairs={{0,16},{4,20},{8,24},{12,28},{16,0},{20,4},{24,8},{28,12},{1,17},{... | collective-permute-start | bytes 393224 | tf_op jit(solution)/shard_map/ppermute | solution.py:552
  101.1 2.4 %collective-permute-start.33 = (f32[1,4,16,128]{3,2,1,0:T(8,128)S(1)}, f32[1,4,16,128]{3,2,1,0:T(8,128)S(1)}, u32[]{:S(2)}, u32[]{:S(2)}) collective-permute-start(f32[1,4,16,128]{3,2,1,0:T(8,128)S(1)} %get-tuple-element.91), channel_id=1, source_target_pairs={{0,4},{4,0},{8,12},{12,8},{16,20},{20,16},{24,28},{28,24},{1,5},{5... | collective-permute-start | bytes 98312 | tf_op jit(solution)/shard_map/ppermute | solution.py:552
  102.3 8.0 %collective-permute-start.34 = (f32[1,4,16,128]{3,2,1,0:T(8,128)S(1)}, f32[1,4,16,128]{3,2,1,0:T(8,128)S(1)}, u32[]{:S(2)}, u32[]{:S(2)}) collective-permute-start(f32[1,4,16,128]{3,2,1,0:T(8,128)S(1)} %get-tuple-element.92), channel_id=1, source_target_pairs={{0,8},{4,12},{8,0},{12,4},{16,24},{20,28},{24,16},{28,20},{1,9},{5... | collective-permute-start | bytes 98312 | tf_op jit(solution)/shard_map/ppermute | solution.py:552
  103.6 6.8 %collective-permute-start.35 = (f32[1,4,16,128]{3,2,1,0:T(8,128)S(1)}, f32[1,4,16,128]{3,2,1,0:T(8,128)S(1)}, u32[]{:S(2)}, u32[]{:S(2)}) collective-permute-start(f32[1,4,16,128]{3,2,1,0:T(8,128)S(1)} %get-tuple-element.93), channel_id=1, source_target_pairs={{0,12},{4,8},{8,4},{12,0},{16,28},{20,24},{24,20},{28,16},{1,13},{... | collective-permute-start | bytes 98312 | tf_op jit(solution)/shard_map/ppermute | solution.py:552
  104.7 6.4 %collective-permute-start.10 = (f32[1,4,16,128]{3,2,1,0:T(8,128)S(1)}, f32[1,4,16,128]{3,2,1,0:T(8,128)S(1)}, u32[]{:S(2)}, u32[]{:S(2)}) collective-permute-start(f32[1,4,16,128]{3,2,1,0:T(8,128)S(1)} %get-tuple-element.68), channel_id=1, source_target_pairs={{0,8},{4,12},{8,0},{12,4},{16,24},{20,28},{24,16},{28,20},{1,9},{5... | collective-permute-start | bytes 98312 | tf_op jit(solution)/shard_map/ppermute | solution.py:552
  105.7 6.5 %collective-permute-start.11 = (f32[1,4,16,128]{3,2,1,0:T(8,128)S(1)}, f32[1,4,16,128]{3,2,1,0:T(8,128)S(1)}, u32[]{:S(2)}, u32[]{:S(2)}) collective-permute-start(f32[1,4,16,128]{3,2,1,0:T(8,128)S(1)} %get-tuple-element.69), channel_id=1, source_target_pairs={{0,12},{4,8},{8,4},{12,0},{16,28},{20,24},{24,20},{28,16},{1,13},{... | collective-permute-start | bytes 98312 | tf_op jit(solution)/shard_map/ppermute | solution.py:552
  110.3 4.7 %collective-permute-start.27 = (f32[2,4,16,128]{3,2,1,0:T(8,128)S(1)}, f32[2,4,16,128]{3,2,1,0:T(8,128)S(1)}, u32[]{:S(2)}, u32[]{:S(2)}) collective-permute-start(f32[2,4,16,128]{3,2,1,0:T(8,128)S(1)} %get-tuple-element.85), channel_id=1, source_target_pairs={{0,4},{4,0},{8,12},{12,8},{16,20},{20,16},{24,28},{28,24},{1,5},{5... | collective-permute-start | bytes 196616 | tf_op jit(solution)/shard_map/ppermute | solution.py:552
  110.3 5.7 %collective-permute-start.28 = (f32[2,4,16,128]{3,2,1,0:T(8,128)S(1)}, f32[2,4,16,128]{3,2,1,0:T(8,128)S(1)}, u32[]{:S(2)}, u32[]{:S(2)}) collective-permute-start(f32[2,4,16,128]{3,2,1,0:T(8,128)S(1)} %get-tuple-element.86), channel_id=1, source_target_pairs={{0,8},{4,12},{8,0},{12,4},{16,24},{20,28},{24,16},{28,20},{1,9},{5... | collective-permute-start | bytes 196616 | tf_op jit(solution)/shard_map/ppermute | solution.py:552
  111.1 5.4 %collective-permute-start.29 = (f32[2,4,16,128]{3,2,1,0:T(8,128)S(1)}, f32[2,4,16,128]{3,2,1,0:T(8,128)S(1)}, u32[]{:S(2)}, u32[]{:S(2)}) collective-permute-start(f32[2,4,16,128]{3,2,1,0:T(8,128)S(1)} %get-tuple-element.87), channel_id=1, source_target_pairs={{0,12},{4,8},{8,4},{12,0},{16,28},{20,24},{24,20},{28,16},{1,13},{... | collective-permute-start | bytes 196616 | tf_op jit(solution)/shard_map/ppermute | solution.py:552
  112.2 4.9 %collective-permute-start.21 = (f32[2,4,16,128]{3,2,1,0:T(8,128)S(1)}, f32[2,4,16,128]{3,2,1,0:T(8,128)S(1)}, u32[]{:S(2)}, u32[]{:S(2)}) collective-permute-start(f32[2,4,16,128]{3,2,1,0:T(8,128)S(1)} %get-tuple-element.79), channel_id=1, source_target_pairs={{0,4},{4,0},{8,12},{12,8},{16,20},{20,16},{24,28},{28,24},{1,5},{5... | collective-permute-start | bytes 196616 | tf_op jit(solution)/shard_map/ppermute | solution.py:552
  112.6 1.7 %collective-permute-start.9 = (f32[1,4,16,128]{3,2,1,0:T(8,128)S(1)}, f32[1,4,16,128]{3,2,1,0:T(8,128)S(1)}, u32[]{:S(2)}, u32[]{:S(2)}) collective-permute-start(f32[1,4,16,128]{3,2,1,0:T(8,128)S(1)} %get-tuple-element.67), channel_id=1, source_target_pairs={{0,4},{4,0},{8,12},{12,8},{16,20},{20,16},{24,28},{28,24},{1,5},{5... | collective-permute-start | bytes 98312 | tf_op jit(solution)/shard_map/ppermute | solution.py:552
  114.3 5.0 %collective-permute-start.22 = (f32[2,4,16,128]{3,2,1,0:T(8,128)S(1)}, f32[2,4,16,128]{3,2,1,0:T(8,128)S(1)}, u32[]{:S(2)}, u32[]{:S(2)}) collective-permute-start(f32[2,4,16,128]{3,2,1,0:T(8,128)S(1)} %get-tuple-element.80), channel_id=1, source_target_pairs={{0,8},{4,12},{8,0},{12,4},{16,24},{20,28},{24,16},{28,20},{1,9},{5... | collective-permute-start | bytes 196616 | tf_op jit(solution)/shard_map/ppermute | solution.py:552
  114.9 4.6 %collective-permute-start.23 = (f32[2,4,16,128]{3,2,1,0:T(8,128)S(1)}, f32[2,4,16,128]{3,2,1,0:T(8,128)S(1)}, u32[]{:S(2)}, u32[]{:S(2)}) collective-permute-start(f32[2,4,16,128]{3,2,1,0:T(8,128)S(1)} %get-tuple-element.81), channel_id=1, source_target_pairs={{0,12},{4,8},{8,4},{12,0},{16,28},{20,24},{24,20},{28,16},{1,13},{... | collective-permute-start | bytes 196616 | tf_op jit(solution)/shard_map/ppermute | solution.py:552
  116.1 3.4 %collective-permute-start.15 = (f32[2,4,16,128]{3,2,1,0:T(8,128)S(1)}, f32[2,4,16,128]{3,2,1,0:T(8,128)S(1)}, u32[]{:S(2)}, u32[]{:S(2)}) collective-permute-start(f32[2,4,16,128]{3,2,1,0:T(8,128)S(1)} %get-tuple-element.73), channel_id=1, source_target_pairs={{0,4},{4,0},{8,12},{12,8},{16,20},{20,16},{24,28},{28,24},{1,5},{5... | collective-permute-start | bytes 196616 | tf_op jit(solution)/shard_map/ppermute | solution.py:552
  116.5 5.6 %collective-permute-start.16 = (f32[2,4,16,128]{3,2,1,0:T(8,128)S(1)}, f32[2,4,16,128]{3,2,1,0:T(8,128)S(1)}, u32[]{:S(2)}, u32[]{:S(2)}) collective-permute-start(f32[2,4,16,128]{3,2,1,0:T(8,128)S(1)} %get-tuple-element.74), channel_id=1, source_target_pairs={{0,8},{4,12},{8,0},{12,4},{16,24},{20,28},{24,16},{28,20},{1,9},{5... | collective-permute-start | bytes 196616 | tf_op jit(solution)/shard_map/ppermute | solution.py:552
  117.1 5.2 %collective-permute-start.17 = (f32[2,4,16,128]{3,2,1,0:T(8,128)S(1)}, f32[2,4,16,128]{3,2,1,0:T(8,128)S(1)}, u32[]{:S(2)}, u32[]{:S(2)}) collective-permute-start(f32[2,4,16,128]{3,2,1,0:T(8,128)S(1)} %get-tuple-element.75), channel_id=1, source_target_pairs={{0,12},{4,8},{8,4},{12,0},{16,28},{20,24},{24,20},{28,16},{1,13},{... | collective-permute-start | bytes 196616 | tf_op jit(solution)/shard_map/ppermute | solution.py:552
where the time goes:
time: 124 us; the launch traced here: 123 us
  waiting for transfers between devices  43.1 us (35%)
  starting transfers between devices  40.9 us (33%)
  Pallas kernels  38.6 us (31%)
    ppermute x34, waiting for transfers between devices, exchange(): return lax.ppermute(x, axis, [(i, i ^ mask) for i in range(size)])  43.1 us
    ppermute x34, starting transfers between devices, exchange(): return lax.ppermute(x, axis, [(i, i ^ mask) for i in range(size)])  34.1 us
    pallas_call x10, Pallas kernels, half_sums(): pl.pallas_call(body, in_specs=[SMEM] + [VMEM] * len(args), out_specs=[VME...  14.6 us
    pallas_call x1, Pallas kernels, interior(): pl.pallas_call(body, in_specs=[ANY] * 3, out_specs=[VMEM] * 7, out_shape=...  13 us
    ppermute x1, starting transfers between devices, on_device(): above = lax.ppermute(down, 'strip', forward)  5.51 us
    pallas_call x1, Pallas kernels, iterate(): pl.pallas_call(body, in_specs=[VMEM] * (3 + number), out_specs=[ANY] + [V...  3.8 us
    pallas_call x1, Pallas kernels, inverse_map(): pl.pallas_call(body, in_specs=[VMEM], out_specs=VMEM, out_shape=jax.Shape...  3.04 us
  transfers between devices with their start and end apart: 36, of which 12 were waited for; matrix products, arithmetic and copies ran while one was open for 0% of the time, Pallas kernels for 25%

commit v1 on v0

--- a/solution.py
+++ b/solution.py
@@ -123,7 +123,7 @@
     count, rows, cols = coh.shape
     last_tile = rows // 8 - 1
 
-    def body(ct, xt, yt, cb, xb, yb, down, up):
+    def body(ct, xt, yt, cb, xb, yb, first, second):
         row = lax.broadcasted_iota(jnp.int32, (8, cols), 0)
 
         def partial_rhs(c, x, y):
@@ -131,19 +131,28 @@
             fy = jnp.where(row < 7, c * pltpu.roll(c, 7, axis=0) * y, 0.0)
             return -(fx - prev_col(fx) + fy - pltpu.roll(fy, 1, axis=0))
 
-        for k in range(count):
-            c, y = (cb[k], yb[k])
-            r = partial_rhs(c, xb[k], y)
-            down[0, k : k + 1, :] = r[6:7]
-            down[1, k : k + 1, :] = r[7:8]
-            down[2, k : k + 1, :] = y[7:8]
-            down[3, k : k + 1, :] = c[6:7]
-            down[4, k : k + 1, :] = c[7:8]
-            c = ct[k]
-            r = partial_rhs(c, xt[k], yt[k])
-            for i in range(3):
-                up[i, k : k + 1, :] = r[i : i + 1]
-                up[3 + i, k : k + 1, :] = c[i : i + 1]
+        def send(down, up):
+            for k in range(count):
+                c, y = (cb[k], yb[k])
+                r = partial_rhs(c, xb[k], y)
+                for i, x in enumerate((r[6:7], r[7:8], y[7:8], c[6:7], c[7:8])):
+                    down[i, k : k + 1, :] = x
+                c = ct[k]
+                r = partial_rhs(c, xt[k], yt[k])
+                for i in range(3):
+                    up[i, k : k + 1, :] = r[i : i + 1]
+                    up[3 + i, k : k + 1, :] = c[i : i + 1]
+            down[5] = jnp.zeros((count, cols), F32)
+
+        even = lax.axis_index("strip") % 2 == 0
+
+        @pl.when(even)
+        def _():
+            send(first, second)
+
+        @pl.when(jnp.logical_not(even))
+        def _():
+            send(second, first)
 
     top = pl.BlockSpec((count, 8, cols), lambda i: (0, 0, 0))
     bottom = pl.BlockSpec((count, 8, cols), lambda i: (0, last_tile, 0))
@@ -152,11 +161,11 @@
         grid=(1,),
         in_specs=[top, top, top, bottom, bottom, bottom],
         out_specs=[
-            pl.BlockSpec((5, count, cols), lambda i: (0, 0, 0)),
+            pl.BlockSpec((6, count, cols), lambda i: (0, 0, 0)),
             pl.BlockSpec((6, count, cols), lambda i: (0, 0, 0)),
         ],
         out_shape=[
-            jax.ShapeDtypeStruct((5, count, cols), F32),
+            jax.ShapeDtypeStruct((6, count, cols), F32),
             jax.ShapeDtypeStruct((6, count, cols), F32),
         ],
         name="edges",
@@ -283,11 +292,14 @@
     )(*(far_off(x) for x in (coh, gx, gy)))
 
 
-def join(above, below, r, v, u, wx, wy, extra, mom):
+def join(first, second, r, v, u, wx, wy, extra, mom):
     rows, count, cols = r.shape
 
-    def body(ab, be, r_in, v_in, u_in, wx_ref, wy_ref, ex, m_in, r_out, v_out, u_out, out):
+    def body(got_first, got_second, r_in, v_in, u_in, wx_ref, wy_ref, ex, m_in, r_out, v_out, u_out, out):
         end = rows - 1
+        even = lax.axis_index("strip") % 2 == 0
+        ab = [jnp.where(even, got_second[i], got_first[i]) for i in range(5)]
+        be = [jnp.where(even, got_first[i], got_second[i]) for i in range(6)]
         rr, vv, uu = ({}, {}, {})
         gx_w, gy_w = ({}, {})
         for i in (0, 1, 2, 3, end - 3, end - 2, end - 1, end):
@@ -365,7 +377,7 @@
         input_output_aliases={2: 0, 3: 1, 4: 2},
         name="join",
         compiler_params=room(4),
-    )(near(above), near(below), r, v, u, wx, wy, extra, mom)
+    )(near(first), near(second), r, v, u, wx, wy, extra, mom)
 
 
 def iterate(r, v, u, shares, groups, widths):
@@ -568,12 +580,13 @@
     _, rows, cols = coherence.shape
     groups = size // 2
     widths = [cols * part // sum(SLICES) for part in SLICES]
-    down, up = edges(coherence, grad_x, grad_y)
-    forward = [(i, i + 1) for i in range(strips - 1)]
-    above = lax.ppermute(down, "strip", forward)
-    below = lax.ppermute(up, "strip", [(j, i) for i, j in forward])
+    first, second = edges(coherence, grad_x, grad_y)
+    first, second = (
+        lax.ppermute(x, "strip", [p for i in range(at, strips - 1, 2) for p in ((i, i + 1), (i + 1, i))])
+        for at, x in enumerate((first, second))
+    )
     fields = interior(coherence, grad_x, grad_y)
-    r, v, u, moments = join(above, below, *fields)
+    r, v, u, moments = join(first, second, *fields)
     shares = summands(moments, "strip")
     mapping = inverse_map(pairs, groups)
     phase, keep, beside, *far = iterate(r, v, u, shares, groups, widths)

time: 124 us -> 122 us (0.984)
  starting transfers between devices: 40.9 us -> 39.1 us
    ppermute x2, starting transfers between devices: 6.8 us -> 3.69 us  [on_device(): lax.ppermute(x, 'strip', [p for i in range(at, strips - 1, 2) for p in ((...]
    ppermute x34, starting transfers between devices: 34.1 us -> 35.4 us  [exchange(): return lax.ppermute(x, axis, [(i, i ^ mask) for i in range(size)])]
where the time goes in v1:
time: 122 us
  waiting for transfers between devices  43.1 us (35%)
  starting transfers between devices  39.1 us (32%)
  Pallas kernels  38.6 us (32%)
    ppermute x34, waiting for transfers between devices, exchange(): return lax.ppermute(x, axis, [(i, i ^ mask) for i in range(size)])  43.1 us
    ppermute x34, starting transfers between devices, exchange(): return lax.ppermute(x, axis, [(i, i ^ mask) for i in range(size)])  35.4 us
    pallas_call x10, Pallas kernels, half_sums(): pl.pallas_call(body, in_specs=[SMEM] + [VMEM] * len(args), out_specs=[VME...  14.6 us
    pallas_call x1, Pallas kernels, interior(): pl.pallas_call(body, in_specs=[ANY] * 3, out_specs=[VMEM] * 7, out_shape=...  13 us
    pallas_call x1, Pallas kernels, iterate(): pl.pallas_call(body, in_specs=[VMEM] * (3 + number), out_specs=[ANY] + [V...  3.78 us
    ppermute x2, starting transfers between devices, on_device(): lax.ppermute(x, 'strip', [p for i in range(at, strips - 1, 2) for p in ((...  3.69 us
    pallas_call x1, Pallas kernels, inverse_map(): pl.pallas_call(body, in_specs=[VMEM], out_specs=VMEM, out_shape=jax.Shape...  3.04 us
  transfers between devices with their start and end apart: 36, of which 12 were waited for; matrix products, arithmetic and copies ran while one was open for 0% of the time, Pallas kernels for 25%

profile of v1, /device:TPU:0, one launch (start us, length us, event | category | flops | bytes accessed | tf_op | source)
XLA Modules:
  0.0 121.6 jit_solution(17772641583402370650)
XLA Ops:
  0.6 2.2 %edges.1 = (f32[6,8,1024]{2,1,0:T(8,128)S(1)}, f32[6,8,1024]{2,1,0:T(8,128)S(1)}) custom-call(f32[8,64,1024]{2,1,0:T(8,128)} %c_hbm.1, f32[8,64,1024]{2,1,0:T(8,128)} %x_hbm.1, f32[8,64,1024]{2,1,0:T(8,128)} %y_hbm.1, f32[8,64,1024]{2,1,0:T(8,128)} %c_hbm.1, f32[8,64,1024]{2,1,0:T(8,128)} %x_hbm.1, f32[8,64,1024]{2,1,0:T(8,128)} %y_hbm.1), custom_call_target="tpu_custom_call" | custom-call | tf_op jit(solution)/shard_map/edges/pallas_call | solution.py:159
  2.9 3.0 %collective-permute-start = (f32[6,8,1024]{2,1,0:T(8,128)S(1)}, f32[6,8,1024]{2,1,0:T(8,128)S(1)}, u32[]{:S(2)}, u32[]{:S(2)}) collective-permute-start(f32[6,8,1024]{2,1,0:T(8,128)S(1)} %get-tuple-element.48), channel_id=1, source_target_pairs={{0,1},{1,0},{2,3},{3,2},{4,5},{5,4},{6,7},{7,6},{8,9},{9,8},{10,11... | collective-permute-start | bytes 589832 | tf_op jit(solution)/shard_map/ppermute | solution.py:585
  5.9 0.7 collective-permute-start.1
  6.6 13.0 %interior.1 = (f32[64,8,1024]{2,1,0:T(8,128)S(1)}, f32[64,8,1024]{2,1,0:T(8,128)S(1)}, f32[64,8,1024]{2,1,0:T(8,128)S(1)}, f32[64,8,1024]{2,1,0:T(8,128)S(1)}, f...) custom-call(f32[8,64,1024]{2,1,0:T(8,128)} %c_hbm.1, f32[8,64,1024]{2,1,0:T(8,128)} %x_hbm.1, ...), custom_call_target="tpu_custom_call" | custom-call | tf_op jit(solution)/shard_map/interior/pallas_call | solution.py:284
  19.6 0.0 collective-permute-done.got_first
  19.6 0.9 join.1
  20.5 4.2 %collective-permute-start.2 = (f32[8,128]{1,0:T(8,128)S(1)}, f32[8,128]{1,0:T(8,128)S(1)}, u32[]{:S(2)}, u32[]{:S(2)}) collective-permute-start(f32[8,128]{1,0:T(8,128)S(1)} %get-tuple-element.60.refs_3_), channel_id=1, source_target_pairs={{0,1},{1,0},{2,3},{3,2},{4,5},{5,4},{6,7},{7,6},{8,9},{9,8},{10,11... | collective-permute-start | bytes 12296 | tf_op jit(solution)/shard_map/ppermute | solution.py:564
  24.7 0.0 collective-permute-start.3
  24.7 1.5 %collective-permute-start.4 = (f32[8,128]{1,0:T(8,128)S(1)}, f32[8,128]{1,0:T(8,128)S(1)}, u32[]{:S(2)}, u32[]{:S(2)}) collective-permute-start(f32[8,128]{1,0:T(8,128)S(1)} %get-tuple-element.60.refs_3_), channel_id=1, source_target_pairs={{0,3},{1,2},{2,1},{3,0},{4,7},{5,6},{6,5},{7,4},{8,11},{9,10},{10,... | collective-permute-start | bytes 12296 | tf_op jit(solution)/shard_map/ppermute | solution.py:564
  26.2 0.0 collective-permute-done.2.refs_4_
  26.3 2.0 %collective-permute-done.3.refs_5_ = f32[8,128]{1,0:T(8,128)S(1)} collective-permute-done((f32[8,128]{1,0:T(8,128)S(1)}, f32[8,128]{1,0:T(8,128)S(1)}, u32[]{:S(2)}, u32[]{:S(2)}) %collective-permute-start.3) | collective-permute-done | bytes 4128 | tf_op jit(solution)/shard_map/ppermute | solution.py:564
  28.3 0.9 collective-permute-done.4.refs_6_
  29.2 3.8 %iterate.1 = (f32[8,64,1024]{2,1,0:T(8,128)}, f32[8,8,16,128]{3,2,1,0:T(8,128)S(1)}, f32[8,8,16,128]{3,2,1,0:T(8,128)S(1)}, f32[1,8,16,128]{3,2,1,0:T(8,128)S(1)...) custom-call(f32[64,8,1024]{2,1,0:T(8,128)S(1)} %get-tuple-element.57, ...), custom_call_target="tpu_custom_call" | custom-call | tf_op jit(solution)/shard_map/iterate/pallas_call | solution.py:456
  33.0 0.1 collective-permute-start.5
  33.1 1.6 %collective-permute-start.24 = (f32[2,8,16,128]{3,2,1,0:T(8,128)S(1)}, f32[2,8,16,128]{3,2,1,0:T(8,128)S(1)}, u32[]{:S(2)}, u32[]{:S(2)}) collective-permute-start(f32[2,8,16,128]{3,2,1,0:T(8,128)S(1)} %get-tuple-element.82), channel_id=1, source_target_pairs={{0,8},{4,12},{8,0},{12,4},{16,24},{20,28},{24,16},{28,20},{1,9},{5... | collective-permute-start | bytes 393224 | tf_op jit(solution)/shard_map/ppermute | solution.py:564
  34.7 0.2 collective-permute-start.25
  34.9 1.6 %collective-permute-start.18 = (f32[2,8,16,128]{3,2,1,0:T(8,128)S(1)}, f32[2,8,16,128]{3,2,1,0:T(8,128)S(1)}, u32[]{:S(2)}, u32[]{:S(2)}) collective-permute-start(f32[2,8,16,128]{3,2,1,0:T(8,128)S(1)} %get-tuple-element.76), channel_id=1, source_target_pairs={{0,8},{4,12},{8,0},{12,4},{16,24},{20,28},{24,16},{28,20},{1,9},{5... | collective-permute-start | bytes 393224 | tf_op jit(solution)/shard_map/ppermute | solution.py:564
  36.5 0.1 collective-permute-start.19
  36.6 2.9 %collective-permute-done.24.refs_2_ = f32[2,8,16,128]{3,2,1,0:T(8,128)S(1)} collective-permute-done((f32[2,8,16,128]{3,2,1,0:T(8,128)S(1)}, f32[2,8,16,128]{3,2,1,0:T(8,128)S(1)}, u32[]{:S(2)}, u32[]{:S(2)}) %collective-permute-start.24) | collective-permute-done | bytes 131104 | tf_op jit(solution)/shard_map/ppermute | solution.py:564
  39.5 1.6 %collective-permute-start.12 = (f32[2,8,16,128]{3,2,1,0:T(8,128)S(1)}, f32[2,8,16,128]{3,2,1,0:T(8,128)S(1)}, u32[]{:S(2)}, u32[]{:S(2)}) collective-permute-start(f32[2,8,16,128]{3,2,1,0:T(8,128)S(1)} %get-tuple-element.70), channel_id=1, source_target_pairs={{0,8},{4,12},{8,0},{12,4},{16,24},{20,28},{24,16},{28,20},{1,9},{5... | collective-permute-start | bytes 393224 | tf_op jit(solution)/shard_map/ppermute | solution.py:564
  41.1 0.3 collective-permute-done.25.refs_3_
  41.4 1.9 %collective-permute-start.13 = (f32[2,8,16,128]{3,2,1,0:T(8,128)S(1)}, f32[2,8,16,128]{3,2,1,0:T(8,128)S(1)}, u32[]{:S(2)}, u32[]{:S(2)}) collective-permute-start(f32[2,8,16,128]{3,2,1,0:T(8,128)S(1)} %get-tuple-element.71), channel_id=1, source_target_pairs={{0,12},{4,8},{8,4},{12,0},{16,28},{20,24},{24,20},{28,16},{1,13},{... | collective-permute-start | bytes 393224 | tf_op jit(solution)/shard_map/ppermute | solution.py:564
  43.3 1.8 %collective-permute-done.18.refs_2_ = f32[2,8,16,128]{3,2,1,0:T(8,128)S(1)} collective-permute-done((f32[2,8,16,128]{3,2,1,0:T(8,128)S(1)}, f32[2,8,16,128]{3,2,1,0:T(8,128)S(1)}, u32[]{:S(2)}, u32[]{:S(2)}) %collective-permute-start.18) | collective-permute-done | bytes 131104 | tf_op jit(solution)/shard_map/ppermute | solution.py:564
  45.1 1.6 %collective-permute-start.30 = (f32[1,8,16,128]{3,2,1,0:T(8,128)S(1)}, f32[1,8,16,128]{3,2,1,0:T(8,128)S(1)}, u32[]{:S(2)}, u32[]{:S(2)}) collective-permute-start(f32[1,8,16,128]{3,2,1,0:T(8,128)S(1)} %get-tuple-element.88), channel_id=1, source_target_pairs={{0,8},{4,12},{8,0},{12,4},{16,24},{20,28},{24,16},{28,20},{1,9},{5... | collective-permute-start | bytes 196616 | tf_op jit(solution)/shard_map/ppermute | solution.py:564
  46.7 3.0 %inverse_map.1.map_ref = f32[32,32]{1,0:T(8,128)S(1)} custom-call(s32[2,64]{1,0:T(2,128)S(1)} %bitcast.1), custom_call_target="tpu_custom_call" | custom-call | tf_op jit(solution)/shard_map/inverse_map/pallas_call | solution.py:111
  49.7 1.6 %cross_sums.8 = f32[2,16,16,128]{3,2,1,0:T(8,128)S(1)} custom-call(f32[32,32]{1,0:T(8,128)S(1)} %inverse_map.1.map_ref, f32[8,8,16,128]{3,2,1,0:T(8,128)S(1)} %get-tuple-element.62.refs_0_, f32[8,8,16,128]{3,2,1,0:T(8,128)S(1)} %collective-permute-done.5.refs_1_, f32[2,8,16,128]{3,2,1,0:T(8,128)S(1)} %collective-permute-done.24.refs_2_, ...), custom_call_target="tpu_custom_call" | custom-call | tf_op jit(solution)/shard_map/cross_sums/pallas_call | solution.py:524
  51.4 2.7 %collective-permute-start.26 = (f32[2,16,16,128]{3,2,1,0:T(8,128)S(1)}, f32[2,16,16,128]{3,2,1,0:T(8,128)S(1)}, u32[]{:S(2)}, u32[]{:S(2)}) collective-permute-start(f32[2,16,16,128]{3,2,1,0:T(8,128)S(1)} %cross_sums.8), channel_id=1, source_target_pairs={{0,16},{4,20},{8,24},{12,28},{16,0},{20,4},{24,8},{28,12},{1,17},{... | collective-permute-start | bytes 786440 | tf_op jit(solution)/shard_map/ppermute | solution.py:564
  54.0 1.6 %cross_sums.7 = f32[2,16,16,128]{3,2,1,0:T(8,128)S(1)} custom-call(f32[32,32]{1,0:T(8,128)S(1)} %inverse_map.1.map_ref, f32[8,8,16,128]{3,2,1,0:T(8,128)S(1)} %get-tuple-element.62.refs_0_, f32[8,8,16,128]{3,2,1,0:T(8,128)S(1)} %collective-permute-done.5.refs_1_, f32[2,8,16,128]{3,2,1,0:T(8,128)S(1)} %collective-permute-done.18.refs_2_, ...), custom_call_target="tpu_custom_call" | custom-call | tf_op jit(solution)/shard_map/cross_sums/pallas_call | solution.py:524
  55.6 0.4 collective-permute-start.20
  56.0 0.5 collective-permute-start.6
  56.5 1.6 %cross_sums.6 = f32[2,16,16,128]{3,2,1,0:T(8,128)S(1)} custom-call(f32[32,32]{1,0:T(8,128)S(1)} %inverse_map.1.map_ref, f32[8,8,16,128]{3,2,1,0:T(8,128)S(1)} %get-tuple-element.62.refs_0_, f32[8,8,16,128]{3,2,1,0:T(8,128)S(1)} %collective-permute-done.5.refs_1_, f32[2,8,16,128]{3,2,1,0:T(8,128)S(1)} %collective-permute-done.12.refs_2_, ...), custom_call_target="tpu_custom_call" | custom-call | tf_op jit(solution)/shard_map/cross_sums/pallas_call | solution.py:524
  58.1 1.0 collective-permute-start.7
  59.1 2.6 %collective-permute-start.14 = (f32[2,16,16,128]{3,2,1,0:T(8,128)S(1)}, f32[2,16,16,128]{3,2,1,0:T(8,128)S(1)}, u32[]{:S(2)}, u32[]{:S(2)}) collective-permute-start(f32[2,16,16,128]{3,2,1,0:T(8,128)S(1)} %cross_sums.6), channel_id=1, source_target_pairs={{0,16},{4,20},{8,24},{12,28},{16,0},{20,4},{24,8},{28,12},{1,17},{... | collective-permute-start | bytes 786440 | tf_op jit(solution)/shard_map/ppermute | solution.py:564
  61.6 1.3 %cross_sums.9 = f32[1,16,16,128]{3,2,1,0:T(8,128)S(1)} custom-call(f32[32,32]{1,0:T(8,128)S(1)} %inverse_map.1.map_ref, f32[8,8,16,128]{3,2,1,0:T(8,128)S(1)} %get-tuple-element.62.refs_0_, f32[8,8,16,128]{3,2,1,0:T(8,128)S(1)} %collective-permute-done.5.refs_1_, f32[1,8,16,128]{3,2,1,0:T(8,128)S(1)} %collective-permute-done.30.refs_2_, ...), custom_call_target="tpu_custom_call" | custom-call | tf_op jit(solution)/shard_map/cross_sums/pallas_call | solution.py:524
  63.0 4.9 %collective-permute-done.6.refs_2_ = f32[1,8,16,128]{3,2,1,0:T(8,128)S(1)} collective-permute-done((f32[1,8,16,128]{3,2,1,0:T(8,128)S(1)}, f32[1,8,16,128]{3,2,1,0:T(8,128)S(1)}, u32[]{:S(2)}, u32[]{:S(2)}) %collective-permute-start.6) | collective-permute-done | bytes 65568 | tf_op jit(solution)/shard_map/ppermute | solution.py:564
  67.8 3.8 %collective-permute-start.32 = (f32[1,16,16,128]{3,2,1,0:T(8,128)S(1)}, f32[1,16,16,128]{3,2,1,0:T(8,128)S(1)}, u32[]{:S(2)}, u32[]{:S(2)}) collective-permute-start(f32[1,16,16,128]{3,2,1,0:T(8,128)S(1)} %cross_sums.9), channel_id=1, source_target_pairs={{0,16},{4,20},{8,24},{12,28},{16,0},{20,4},{24,8},{28,12},{1,17},{... | collective-permute-start | bytes 393224 | tf_op jit(solution)/shard_map/ppermute | solution.py:564
  71.6 1.3 %cross_sums.5 = f32[1,16,16,128]{3,2,1,0:T(8,128)S(1)} custom-call(f32[32,32]{1,0:T(8,128)S(1)} %inverse_map.1.map_ref, f32[8,8,16,128]{3,2,1,0:T(8,128)S(1)} %get-tuple-element.62.refs_0_, f32[8,8,16,128]{3,2,1,0:T(8,128)S(1)} %collective-permute-done.5.refs_1_, f32[1,8,16,128]{3,2,1,0:T(8,128)S(1)} %collective-permute-done.6.refs_2_, ...), custom_call_target="tpu_custom_call" | custom-call | tf_op jit(solution)/shard_map/cross_sums/pallas_call | solution.py:524
  72.9 0.4 collective-permute-start.8
  73.3 24.8 %collective-permute-done.32.refs_4_ = f32[1,16,16,128]{3,2,1,0:T(8,128)S(1)} collective-permute-done((f32[1,16,16,128]{3,2,1,0:T(8,128)S(1)}, f32[1,16,16,128]{3,2,1,0:T(8,128)S(1)}, u32[]{:S(2)}, u32[]{:S(2)}) %collective-permute-start.32) | collective-permute-done | bytes 131104 | tf_op jit(solution)/shard_map/ppermute | solution.py:564
  98.1 1.3 %own_sums.9 = (f32[1,4,16,128]{3,2,1,0:T(8,128)S(1)}, f32[1,4,16,128]{3,2,1,0:T(8,128)S(1)}, f32[1,4,16,128]{3,2,1,0:T(8,128)S(1)}, f32[1,4,16,128]{3,2,1,0:T(8,128)S(1)}) custom-call(f32[32,32]{1,0:T(8,128)S(1)} %inverse_map.1.map_ref, f32[8,8,16,128]{3,2,1,0:T(8,128)S(1)} %get-tuple-element.62.refs_0_, ...), custom_call_target="tpu_custom_call" | custom-call | tf_op jit(solution)/shard_map/own_sums/pallas_call | solution.py:524
  99.3 0.1 collective-permute-start.33
  99.4 1.1 collective-permute-done.8.refs_4_
  100.5 1.3 %own_sums.5 = (f32[1,4,16,128]{3,2,1,0:T(8,128)S(1)}, f32[1,4,16,128]{3,2,1,0:T(8,128)S(1)}, f32[1,4,16,128]{3,2,1,0:T(8,128)S(1)}, f32[1,4,16,128]{3,2,1,0:T(8,128)S(1)}) custom-call(f32[32,32]{1,0:T(8,128)S(1)} %inverse_map.1.map_ref, f32[8,8,16,128]{3,2,1,0:T(8,128)S(1)} %get-tuple-element.62.refs_0_, ...), custom_call_target="tpu_custom_call" | custom-call | tf_op jit(solution)/shard_map/own_sums/pallas_call | solution.py:524
  101.8 1.1 collective-permute-start.35
  102.9 1.1 collective-permute-start.10
  103.9 1.4 %collective-permute-start.11 = (f32[1,4,16,128]{3,2,1,0:T(8,128)S(1)}, f32[1,4,16,128]{3,2,1,0:T(8,128)S(1)}, u32[]{:S(2)}, u32[]{:S(2)}) collective-permute-start(f32[1,4,16,128]{3,2,1,0:T(8,128)S(1)} %get-tuple-element.69), channel_id=1, source_target_pairs={{0,12},{4,8},{8,4},{12,0},{16,28},{20,24},{24,20},{28,16},{1,13},{... | collective-permute-start | bytes 98312 | tf_op jit(solution)/shard_map/ppermute | solution.py:564
  105.3 1.6 %own_sums.8 = (f32[2,4,16,128]{3,2,1,0:T(8,128)S(1)}, f32[2,4,16,128]{3,2,1,0:T(8,128)S(1)}, f32[2,4,16,128]{3,2,1,0:T(8,128)S(1)}, f32[2,4,16,128]{3,2,1,0:T(8,128)S(1)}) custom-call(f32[32,32]{1,0:T(8,128)S(1)} %inverse_map.1.map_ref, f32[8,8,16,128]{3,2,1,0:T(8,128)S(1)} %get-tuple-element.62.refs_0_, ...), custom_call_target="tpu_custom_call" | custom-call | tf_op jit(solution)/shard_map/own_sums/pallas_call | solution.py:524
  106.9 1.6 %own_sums.7 = (f32[2,4,16,128]{3,2,1,0:T(8,128)S(1)}, f32[2,4,16,128]{3,2,1,0:T(8,128)S(1)}, f32[2,4,16,128]{3,2,1,0:T(8,128)S(1)}, f32[2,4,16,128]{3,2,1,0:T(8,128)S(1)}) custom-call(f32[32,32]{1,0:T(8,128)S(1)} %inverse_map.1.map_ref, f32[8,8,16,128]{3,2,1,0:T(8,128)S(1)} %get-tuple-element.62.refs_0_, ...), custom_call_target="tpu_custom_call" | custom-call | tf_op jit(solution)/shard_map/own_sums/pallas_call | solution.py:524
  108.5 0.1 collective-permute-start.27
  108.5 0.7 collective-permute-start.28
  109.3 1.1 collective-permute-start.29
  110.4 0.4 collective-permute-start.21
  110.8 0.1 collective-permute-start.9
  110.9 1.6 %own_sums.6 = (f32[2,4,16,128]{3,2,1,0:T(8,128)S(1)}, f32[2,4,16,128]{3,2,1,0:T(8,128)S(1)}, f32[2,4,16,128]{3,2,1,0:T(8,128)S(1)}, f32[2,4,16,128]{3,2,1,0:T(8,128)S(1)}) custom-call(f32[32,32]{1,0:T(8,128)S(1)} %inverse_map.1.map_ref, f32[8,8,16,128]{3,2,1,0:T(8,128)S(1)} %get-tuple-element.62.refs_0_, ...), custom_call_target="tpu_custom_call" | custom-call | tf_op jit(solution)/shard_map/own_sums/pallas_call | solution.py:524
  112.5 0.7 collective-permute-start.22
  113.1 1.1 collective-permute-start.23
  114.3 0.4 collective-permute-start.15
  114.7 0.6 collective-permute-start.16
  115.3 0.8 collective-permute-start.17
  116.1 1.4 %collective-permute-done.22.refs_10_ = f32[2,4,16,128]{3,2,1,0:T(8,128)S(1)} collective-permute-done((f32[2,4,16,128]{3,2,1,0:T(8,128)S(1)}, f32[2,4,16,128]{3,2,1,0:T(8,128)S(1)}, u32[]{:S(2)}, u32[]{:S(2)}) %collective-permute-start.22) | collective-permute-done | bytes 65568 | tf_op jit(solution)/shard_map/ppermute | solution.py:564
  117.5 0.2 collective-permute-done.23.refs_11_
  117.7 2.6 %collective-permute-done.16.refs_6_ = f32[2,4,16,128]{3,2,1,0:T(8,128)S(1)} collective-permute-done((f32[2,4,16,128]{3,2,1,0:T(8,128)S(1)}, f32[2,4,16,128]{3,2,1,0:T(8,128)S(1)}, u32[]{:S(2)}, u32[]{:S(2)}) %collective-permute-start.16) | collective-permute-done | bytes 65568 | tf_op jit(solution)/shard_map/ppermute | solution.py:564
  120.3 0.2 collective-permute-done.17.refs_7_
  120.5 1.1 assemble.1
  (26 shorter events, 0.1 us)
Async XLA Ops:
  2.9 16.7 %collective-permute-start = (f32[6,8,1024]{2,1,0:T(8,128)S(1)}, f32[6,8,1024]{2,1,0:T(8,128)S(1)}, u32[]{:S(2)}, u32[]{:S(2)}) collective-permute-start(f32[6,8,1024]{2,1,0:T(8,128)S(1)} %get-tuple-element.48), channel_id=1, source_target_pairs={{0,1},{1,0},{2,3},{3,2},{4,5},{5,4},{6,7},{7,6},{8,9},{9,8},{10,11... | collective-permute-start | bytes 589832 | tf_op jit(solution)/shard_map/ppermute | solution.py:585
  5.9 13.7 %collective-permute-start.1 = (f32[6,8,1024]{2,1,0:T(8,128)S(1)}, f32[6,8,1024]{2,1,0:T(8,128)S(1)}, u32[]{:S(2)}, u32[]{:S(2)}) collective-permute-start(f32[6,8,1024]{2,1,0:T(8,128)S(1)} %get-tuple-element.49), channel_id=1, source_target_pairs={{1,2},{2,1},{5,6},{6,5},{9,10},{10,9},{13,14},{14,13},{17,18},{18,... | collective-permute-start | bytes 589832 | tf_op jit(solution)/shard_map/ppermute | solution.py:585
  20.5 5.8 %collective-permute-start.2 = (f32[8,128]{1,0:T(8,128)S(1)}, f32[8,128]{1,0:T(8,128)S(1)}, u32[]{:S(2)}, u32[]{:S(2)}) collective-permute-start(f32[8,128]{1,0:T(8,128)S(1)} %get-tuple-element.60.refs_3_), channel_id=1, source_target_pairs={{0,1},{1,0},{2,3},{3,2},{4,5},{5,4},{6,7},{7,6},{8,9},{9,8},{10,11... | collective-permute-start | bytes 12296 | tf_op jit(solution)/shard_map/ppermute | solution.py:564
  24.7 3.6 %collective-permute-start.3 = (f32[8,128]{1,0:T(8,128)S(1)}, f32[8,128]{1,0:T(8,128)S(1)}, u32[]{:S(2)}, u32[]{:S(2)}) collective-permute-start(f32[8,128]{1,0:T(8,128)S(1)} %get-tuple-element.60.refs_3_), channel_id=1, source_target_pairs={{0,2},{1,3},{2,0},{3,1},{4,6},{5,7},{6,4},{7,5},{8,10},{9,11},{10,... | collective-permute-start | bytes 12296 | tf_op jit(solution)/shard_map/ppermute | solution.py:564
  24.7 4.5 %collective-permute-start.4 = (f32[8,128]{1,0:T(8,128)S(1)}, f32[8,128]{1,0:T(8,128)S(1)}, u32[]{:S(2)}, u32[]{:S(2)}) collective-permute-start(f32[8,128]{1,0:T(8,128)S(1)} %get-tuple-element.60.refs_3_), channel_id=1, source_target_pairs={{0,3},{1,2},{2,1},{3,0},{4,7},{5,6},{6,5},{7,4},{8,11},{9,10},{10,... | collective-permute-start | bytes 12296 | tf_op jit(solution)/shard_map/ppermute | solution.py:564
  29.2 17.5 %copy-start = (s32[64,2]{0,1:T(2,128)S(1)}, s32[64,2]{0,1:T(2,128)}, u32[]{:S(2)}) copy-start(s32[64,2]{0,1:T(2,128)} %param.7) | copy-start | bytes 1540
  33.0 13.7 %collective-permute-start.5 = (f32[8,8,16,128]{3,2,1,0:T(8,128)S(1)}, f32[8,8,16,128]{3,2,1,0:T(8,128)S(1)}, u32[]{:S(2)}, u32[]{:S(2)}) collective-permute-start(f32[8,8,16,128]{3,2,1,0:T(8,128)S(1)} %get-tuple-element.63), channel_id=1, source_target_pairs={{0,4},{4,0},{8,12},{12,8},{16,20},{20,16},{24,28},{28,24},{1,5},{5... | collective-permute-start | bytes 1572872 | tf_op jit(solution)/shard_map/ppermute | solution.py:564
  33.1 6.4 %collective-permute-start.24 = (f32[2,8,16,128]{3,2,1,0:T(8,128)S(1)}, f32[2,8,16,128]{3,2,1,0:T(8,128)S(1)}, u32[]{:S(2)}, u32[]{:S(2)}) collective-permute-start(f32[2,8,16,128]{3,2,1,0:T(8,128)S(1)} %get-tuple-element.82), channel_id=1, source_target_pairs={{0,8},{4,12},{8,0},{12,4},{16,24},{20,28},{24,16},{28,20},{1,9},{5... | collective-permute-start | bytes 393224 | tf_op jit(solution)/shard_map/ppermute | solution.py:564
  34.7 6.7 %collective-permute-start.25 = (f32[2,8,16,128]{3,2,1,0:T(8,128)S(1)}, f32[2,8,16,128]{3,2,1,0:T(8,128)S(1)}, u32[]{:S(2)}, u32[]{:S(2)}) collective-permute-start(f32[2,8,16,128]{3,2,1,0:T(8,128)S(1)} %get-tuple-element.83), channel_id=1, source_target_pairs={{0,12},{4,8},{8,4},{12,0},{16,28},{20,24},{24,20},{28,16},{1,13},{... | collective-permute-start | bytes 393224 | tf_op jit(solution)/shard_map/ppermute | solution.py:564
  34.9 10.2 %collective-permute-start.18 = (f32[2,8,16,128]{3,2,1,0:T(8,128)S(1)}, f32[2,8,16,128]{3,2,1,0:T(8,128)S(1)}, u32[]{:S(2)}, u32[]{:S(2)}) collective-permute-start(f32[2,8,16,128]{3,2,1,0:T(8,128)S(1)} %get-tuple-element.76), channel_id=1, source_target_pairs={{0,8},{4,12},{8,0},{12,4},{16,24},{20,28},{24,16},{28,20},{1,9},{5... | collective-permute-start | bytes 393224 | tf_op jit(solution)/shard_map/ppermute | solution.py:564
  36.5 14.9 %collective-permute-start.19 = (f32[2,8,16,128]{3,2,1,0:T(8,128)S(1)}, f32[2,8,16,128]{3,2,1,0:T(8,128)S(1)}, u32[]{:S(2)}, u32[]{:S(2)}) collective-permute-start(f32[2,8,16,128]{3,2,1,0:T(8,128)S(1)} %get-tuple-element.77), channel_id=1, source_target_pairs={{0,12},{4,8},{8,4},{12,0},{16,28},{20,24},{24,20},{28,16},{1,13},{... | collective-permute-start | bytes 393224 | tf_op jit(solution)/shard_map/ppermute | solution.py:564
  39.5 16.1 %collective-permute-start.12 = (f32[2,8,16,128]{3,2,1,0:T(8,128)S(1)}, f32[2,8,16,128]{3,2,1,0:T(8,128)S(1)}, u32[]{:S(2)}, u32[]{:S(2)}) collective-permute-start(f32[2,8,16,128]{3,2,1,0:T(8,128)S(1)} %get-tuple-element.70), channel_id=1, source_target_pairs={{0,8},{4,12},{8,0},{12,4},{16,24},{20,28},{24,16},{28,20},{1,9},{5... | collective-permute-start | bytes 393224 | tf_op jit(solution)/shard_map/ppermute | solution.py:564
  41.4 14.6 %collective-permute-start.13 = (f32[2,8,16,128]{3,2,1,0:T(8,128)S(1)}, f32[2,8,16,128]{3,2,1,0:T(8,128)S(1)}, u32[]{:S(2)}, u32[]{:S(2)}) collective-permute-start(f32[2,8,16,128]{3,2,1,0:T(8,128)S(1)} %get-tuple-element.71), channel_id=1, source_target_pairs={{0,12},{4,8},{8,4},{12,0},{16,28},{20,24},{24,20},{28,16},{1,13},{... | collective-permute-start | bytes 393224 | tf_op jit(solution)/shard_map/ppermute | solution.py:564
  45.1 13.0 %collective-permute-start.30 = (f32[1,8,16,128]{3,2,1,0:T(8,128)S(1)}, f32[1,8,16,128]{3,2,1,0:T(8,128)S(1)}, u32[]{:S(2)}, u32[]{:S(2)}) collective-permute-start(f32[1,8,16,128]{3,2,1,0:T(8,128)S(1)} %get-tuple-element.88), channel_id=1, source_target_pairs={{0,8},{4,12},{8,0},{12,4},{16,24},{20,28},{24,16},{28,20},{1,9},{5... | collective-permute-start | bytes 196616 | tf_op jit(solution)/shard_map/ppermute | solution.py:564
  46.7 12.4 %collective-permute-start.31 = (f32[1,8,16,128]{3,2,1,0:T(8,128)S(1)}, f32[1,8,16,128]{3,2,1,0:T(8,128)S(1)}, u32[]{:S(2)}, u32[]{:S(2)}) collective-permute-start(f32[1,8,16,128]{3,2,1,0:T(8,128)S(1)} %get-tuple-element.89), channel_id=1, source_target_pairs={{0,12},{4,8},{8,4},{12,0},{16,28},{20,24},{24,20},{28,16},{1,13},{... | collective-permute-start | bytes 196616 | tf_op jit(solution)/shard_map/ppermute | solution.py:564
  51.4 51.5 %collective-permute-start.26 = (f32[2,16,16,128]{3,2,1,0:T(8,128)S(1)}, f32[2,16,16,128]{3,2,1,0:T(8,128)S(1)}, u32[]{:S(2)}, u32[]{:S(2)}) collective-permute-start(f32[2,16,16,128]{3,2,1,0:T(8,128)S(1)} %cross_sums.8), channel_id=1, source_target_pairs={{0,16},{4,20},{8,24},{12,28},{16,0},{20,4},{24,8},{28,12},{1,17},{... | collective-permute-start | bytes 786440 | tf_op jit(solution)/shard_map/ppermute | solution.py:564
  55.6 48.3 %collective-permute-start.20 = (f32[2,16,16,128]{3,2,1,0:T(8,128)S(1)}, f32[2,16,16,128]{3,2,1,0:T(8,128)S(1)}, u32[]{:S(2)}, u32[]{:S(2)}) collective-permute-start(f32[2,16,16,128]{3,2,1,0:T(8,128)S(1)} %cross_sums.7), channel_id=1, source_target_pairs={{0,16},{4,20},{8,24},{12,28},{16,0},{20,4},{24,8},{28,12},{1,17},{... | collective-permute-start | bytes 786440 | tf_op jit(solution)/shard_map/ppermute | solution.py:564
  56.0 11.8 %collective-permute-start.6 = (f32[1,8,16,128]{3,2,1,0:T(8,128)S(1)}, f32[1,8,16,128]{3,2,1,0:T(8,128)S(1)}, u32[]{:S(2)}, u32[]{:S(2)}) collective-permute-start(f32[1,8,16,128]{3,2,1,0:T(8,128)S(1)} %get-tuple-element.64), channel_id=1, source_target_pairs={{0,8},{4,12},{8,0},{12,4},{16,24},{20,28},{24,16},{28,20},{1,9},{5... | collective-permute-start | bytes 196616 | tf_op jit(solution)/shard_map/ppermute | solution.py:564
  58.1 13.5 %collective-permute-start.7 = (f32[1,8,16,128]{3,2,1,0:T(8,128)S(1)}, f32[1,8,16,128]{3,2,1,0:T(8,128)S(1)}, u32[]{:S(2)}, u32[]{:S(2)}) collective-permute-start(f32[1,8,16,128]{3,2,1,0:T(8,128)S(1)} %get-tuple-element.65), channel_id=1, source_target_pairs={{0,12},{4,8},{8,4},{12,0},{16,28},{20,24},{24,20},{28,16},{1,13},{... | collective-permute-start | bytes 196616 | tf_op jit(solution)/shard_map/ppermute | solution.py:564
  59.1 51.7 %collective-permute-start.14 = (f32[2,16,16,128]{3,2,1,0:T(8,128)S(1)}, f32[2,16,16,128]{3,2,1,0:T(8,128)S(1)}, u32[]{:S(2)}, u32[]{:S(2)}) collective-permute-start(f32[2,16,16,128]{3,2,1,0:T(8,128)S(1)} %cross_sums.6), channel_id=1, source_target_pairs={{0,16},{4,20},{8,24},{12,28},{16,0},{20,4},{24,8},{28,12},{1,17},{... | collective-permute-start | bytes 786440 | tf_op jit(solution)/shard_map/ppermute | solution.py:564
  67.8 30.3 %collective-permute-start.32 = (f32[1,16,16,128]{3,2,1,0:T(8,128)S(1)}, f32[1,16,16,128]{3,2,1,0:T(8,128)S(1)}, u32[]{:S(2)}, u32[]{:S(2)}) collective-permute-start(f32[1,16,16,128]{3,2,1,0:T(8,128)S(1)} %cross_sums.9), channel_id=1, source_target_pairs={{0,16},{4,20},{8,24},{12,28},{16,0},{20,4},{24,8},{28,12},{1,17},{... | collective-permute-start | bytes 393224 | tf_op jit(solution)/shard_map/ppermute | solution.py:564
  72.9 27.5 %collective-permute-start.8 = (f32[1,16,16,128]{3,2,1,0:T(8,128)S(1)}, f32[1,16,16,128]{3,2,1,0:T(8,128)S(1)}, u32[]{:S(2)}, u32[]{:S(2)}) collective-permute-start(f32[1,16,16,128]{3,2,1,0:T(8,128)S(1)} %cross_sums.5), channel_id=1, source_target_pairs={{0,16},{4,20},{8,24},{12,28},{16,0},{20,4},{24,8},{28,12},{1,17},{... | collective-permute-start | bytes 393224 | tf_op jit(solution)/shard_map/ppermute | solution.py:564
  99.3 2.4 %collective-permute-start.33 = (f32[1,4,16,128]{3,2,1,0:T(8,128)S(1)}, f32[1,4,16,128]{3,2,1,0:T(8,128)S(1)}, u32[]{:S(2)}, u32[]{:S(2)}) collective-permute-start(f32[1,4,16,128]{3,2,1,0:T(8,128)S(1)} %get-tuple-element.91), channel_id=1, source_target_pairs={{0,4},{4,0},{8,12},{12,8},{16,20},{20,16},{24,28},{28,24},{1,5},{5... | collective-permute-start | bytes 98312 | tf_op jit(solution)/shard_map/ppermute | solution.py:564
  100.5 8.0 %collective-permute-start.34 = (f32[1,4,16,128]{3,2,1,0:T(8,128)S(1)}, f32[1,4,16,128]{3,2,1,0:T(8,128)S(1)}, u32[]{:S(2)}, u32[]{:S(2)}) collective-permute-start(f32[1,4,16,128]{3,2,1,0:T(8,128)S(1)} %get-tuple-element.92), channel_id=1, source_target_pairs={{0,8},{4,12},{8,0},{12,4},{16,24},{20,28},{24,16},{28,20},{1,9},{5... | collective-permute-start | bytes 98312 | tf_op jit(solution)/shard_map/ppermute | solution.py:564
  101.8 6.8 %collective-permute-start.35 = (f32[1,4,16,128]{3,2,1,0:T(8,128)S(1)}, f32[1,4,16,128]{3,2,1,0:T(8,128)S(1)}, u32[]{:S(2)}, u32[]{:S(2)}) collective-permute-start(f32[1,4,16,128]{3,2,1,0:T(8,128)S(1)} %get-tuple-element.93), channel_id=1, source_target_pairs={{0,12},{4,8},{8,4},{12,0},{16,28},{20,24},{24,20},{28,16},{1,13},{... | collective-permute-start | bytes 98312 | tf_op jit(solution)/shard_map/ppermute | solution.py:564
  102.9 6.4 %collective-permute-start.10 = (f32[1,4,16,128]{3,2,1,0:T(8,128)S(1)}, f32[1,4,16,128]{3,2,1,0:T(8,128)S(1)}, u32[]{:S(2)}, u32[]{:S(2)}) collective-permute-start(f32[1,4,16,128]{3,2,1,0:T(8,128)S(1)} %get-tuple-element.68), channel_id=1, source_target_pairs={{0,8},{4,12},{8,0},{12,4},{16,24},{20,28},{24,16},{28,20},{1,9},{5... | collective-permute-start | bytes 98312 | tf_op jit(solution)/shard_map/ppermute | solution.py:564
  103.9 6.5 %collective-permute-start.11 = (f32[1,4,16,128]{3,2,1,0:T(8,128)S(1)}, f32[1,4,16,128]{3,2,1,0:T(8,128)S(1)}, u32[]{:S(2)}, u32[]{:S(2)}) collective-permute-start(f32[1,4,16,128]{3,2,1,0:T(8,128)S(1)} %get-tuple-element.69), channel_id=1, source_target_pairs={{0,12},{4,8},{8,4},{12,0},{16,28},{20,24},{24,20},{28,16},{1,13},{... | collective-permute-start | bytes 98312 | tf_op jit(solution)/shard_map/ppermute | solution.py:564
  108.5 4.7 %collective-permute-start.27 = (f32[2,4,16,128]{3,2,1,0:T(8,128)S(1)}, f32[2,4,16,128]{3,2,1,0:T(8,128)S(1)}, u32[]{:S(2)}, u32[]{:S(2)}) collective-permute-start(f32[2,4,16,128]{3,2,1,0:T(8,128)S(1)} %get-tuple-element.85), channel_id=1, source_target_pairs={{0,4},{4,0},{8,12},{12,8},{16,20},{20,16},{24,28},{28,24},{1,5},{5... | collective-permute-start | bytes 196616 | tf_op jit(solution)/shard_map/ppermute | solution.py:564
  108.5 5.7 %collective-permute-start.28 = (f32[2,4,16,128]{3,2,1,0:T(8,128)S(1)}, f32[2,4,16,128]{3,2,1,0:T(8,128)S(1)}, u32[]{:S(2)}, u32[]{:S(2)}) collective-permute-start(f32[2,4,16,128]{3,2,1,0:T(8,128)S(1)} %get-tuple-element.86), channel_id=1, source_target_pairs={{0,8},{4,12},{8,0},{12,4},{16,24},{20,28},{24,16},{28,20},{1,9},{5... | collective-permute-start | bytes 196616 | tf_op jit(solution)/shard_map/ppermute | solution.py:564
  109.3 5.4 %collective-permute-start.29 = (f32[2,4,16,128]{3,2,1,0:T(8,128)S(1)}, f32[2,4,16,128]{3,2,1,0:T(8,128)S(1)}, u32[]{:S(2)}, u32[]{:S(2)}) collective-permute-start(f32[2,4,16,128]{3,2,1,0:T(8,128)S(1)} %get-tuple-element.87), channel_id=1, source_target_pairs={{0,12},{4,8},{8,4},{12,0},{16,28},{20,24},{24,20},{28,16},{1,13},{... | collective-permute-start | bytes 196616 | tf_op jit(solution)/shard_map/ppermute | solution.py:564
  110.4 4.9 %collective-permute-start.21 = (f32[2,4,16,128]{3,2,1,0:T(8,128)S(1)}, f32[2,4,16,128]{3,2,1,0:T(8,128)S(1)}, u32[]{:S(2)}, u32[]{:S(2)}) collective-permute-start(f32[2,4,16,128]{3,2,1,0:T(8,128)S(1)} %get-tuple-element.79), channel_id=1, source_target_pairs={{0,4},{4,0},{8,12},{12,8},{16,20},{20,16},{24,28},{28,24},{1,5},{5... | collective-permute-start | bytes 196616 | tf_op jit(solution)/shard_map/ppermute | solution.py:564
  110.8 1.7 %collective-permute-start.9 = (f32[1,4,16,128]{3,2,1,0:T(8,128)S(1)}, f32[1,4,16,128]{3,2,1,0:T(8,128)S(1)}, u32[]{:S(2)}, u32[]{:S(2)}) collective-permute-start(f32[1,4,16,128]{3,2,1,0:T(8,128)S(1)} %get-tuple-element.67), channel_id=1, source_target_pairs={{0,4},{4,0},{8,12},{12,8},{16,20},{20,16},{24,28},{28,24},{1,5},{5... | collective-permute-start | bytes 98312 | tf_op jit(solution)/shard_map/ppermute | solution.py:564
  112.5 5.0 %collective-permute-start.22 = (f32[2,4,16,128]{3,2,1,0:T(8,128)S(1)}, f32[2,4,16,128]{3,2,1,0:T(8,128)S(1)}, u32[]{:S(2)}, u32[]{:S(2)}) collective-permute-start(f32[2,4,16,128]{3,2,1,0:T(8,128)S(1)} %get-tuple-element.80), channel_id=1, source_target_pairs={{0,8},{4,12},{8,0},{12,4},{16,24},{20,28},{24,16},{28,20},{1,9},{5... | collective-permute-start | bytes 196616 | tf_op jit(solution)/shard_map/ppermute | solution.py:564
  113.1 4.6 %collective-permute-start.23 = (f32[2,4,16,128]{3,2,1,0:T(8,128)S(1)}, f32[2,4,16,128]{3,2,1,0:T(8,128)S(1)}, u32[]{:S(2)}, u32[]{:S(2)}) collective-permute-start(f32[2,4,16,128]{3,2,1,0:T(8,128)S(1)} %get-tuple-element.81), channel_id=1, source_target_pairs={{0,12},{4,8},{8,4},{12,0},{16,28},{20,24},{24,20},{28,16},{1,13},{... | collective-permute-start | bytes 196616 | tf_op jit(solution)/shard_map/ppermute | solution.py:564
  114.3 3.4 %collective-permute-start.15 = (f32[2,4,16,128]{3,2,1,0:T(8,128)S(1)}, f32[2,4,16,128]{3,2,1,0:T(8,128)S(1)}, u32[]{:S(2)}, u32[]{:S(2)}) collective-permute-start(f32[2,4,16,128]{3,2,1,0:T(8,128)S(1)} %get-tuple-element.73), channel_id=1, source_target_pairs={{0,4},{4,0},{8,12},{12,8},{16,20},{20,16},{24,28},{28,24},{1,5},{5... | collective-permute-start | bytes 196616 | tf_op jit(solution)/shard_map/ppermute | solution.py:564
  114.7 5.6 %collective-permute-start.16 = (f32[2,4,16,128]{3,2,1,0:T(8,128)S(1)}, f32[2,4,16,128]{3,2,1,0:T(8,128)S(1)}, u32[]{:S(2)}, u32[]{:S(2)}) collective-permute-start(f32[2,4,16,128]{3,2,1,0:T(8,128)S(1)} %get-tuple-element.74), channel_id=1, source_target_pairs={{0,8},{4,12},{8,0},{12,4},{16,24},{20,28},{24,16},{28,20},{1,9},{5... | collective-permute-start | bytes 196616 | tf_op jit(solution)/shard_map/ppermute | solution.py:564
  115.3 5.2 %collective-permute-start.17 = (f32[2,4,16,128]{3,2,1,0:T(8,128)S(1)}, f32[2,4,16,128]{3,2,1,0:T(8,128)S(1)}, u32[]{:S(2)}, u32[]{:S(2)}) collective-permute-start(f32[2,4,16,128]{3,2,1,0:T(8,128)S(1)} %get-tuple-element.75), channel_id=1, source_target_pairs={{0,12},{4,8},{8,4},{12,0},{16,28},{20,24},{24,20},{28,16},{1,13},{... | collective-permute-start | bytes 196616 | tf_op jit(solution)/shard_map/ppermute | solution.py:564

commit v2 on v1

--- a/solution.py
+++ b/solution.py
@@ -380,6 +380,13 @@
     )(near(first), near(second), r, v, u, wx, wy, extra, mom)
 
 
+def strided_rows(ref, at, pitch, x):
+    for b in range(ref.shape[0]):
+        ref.at[b].reshape(x.shape[0] * pitch, 128)[pl.ds(at, x.shape[0], stride=pitch), :] = x[
+            :, 128 * b : 128 * b + 128
+        ]
+
+
 def iterate(r, v, u, shares, groups, widths):
     rows, count, cols = r.shape
     high = rows // groups
@@ -388,8 +395,7 @@
     def body(*refs):
         r_ref, v_ref, u_ref = refs[:3]
         terms = [ref[...] for ref in refs[3 : 3 + number]]
-        out, keep, beside, *far = refs[3 + number : -2]
-        whole, sem = refs[-2:]
+        out, keep, beside, *far = refs[3 + number :]
         while len(terms) > 1:
             terms = [sum(terms[i : i + 2][1:], terms[i]) for i in range(0, len(terms), 2)]
         m = terms[0]
@@ -417,31 +423,53 @@
         c2 = over(y2, d2, ok2)
         c1 = over(y1, d1, ok1) - l21 * c2
         c0 = over(m0, a00, ok0) - l10 * c1 - l20 * c2
+        lane = lax.broadcasted_iota(jnp.int32, (count, 128), 1)
+        out[...] = jnp.where(lane == 0, c0, jnp.where(lane == 1, c1, c2))
         c0, c1, c2 = (jnp.broadcast_to(c, (count, cols)) for c in (c0, c1, c2))
         _, me = half_and_member(groups)
-
-        def put(ref, at, pitch, x):
-            for b in range(ref.shape[0]):
-                ref.at[b].reshape(count * pitch, 128)[pl.ds(at, count, stride=pitch), :] = x[
-                    :, 128 * b : 128 * b + 128
-                ]
 
         def rows_for(mask, pieces):
             first = jnp.bitwise_xor(me, mask) * high
             for a in range(high):
                 at = first + a
                 x = c0 * r_ref[at] + c1 * v_ref[at] + c2 * u_ref[at]
-                put(whole, at, rows + PAD, x)
                 left = 0
                 for piece in pieces:
                     wide = 128 * piece.shape[0]
-                    put(piece, a, high, x[:, left : left + wide])
+                    strided_rows(piece, a, high, x[:, left : left + wide])
                     left += wide
 
         rows_for(0, [keep])
         rows_for(1, [beside])
         for mask in range(2, groups):
             rows_for(mask, [far[(mask - 2) * len(widths) + i] for i in range(len(widths))])
+
+    return pl.pallas_call(
+        body,
+        in_specs=[VMEM] * (3 + number),
+        out_specs=[VMEM] * (3 + (groups - 2) * len(widths)),
+        out_shape=[in_vmem(count, 128)]
+        + [in_vmem(cols // 128, count, high, 128)] * 2
+        + [in_vmem(wide // 128, count, high, 128) for _ in range(groups - 2) for wide in widths],
+        name="iterate",
+        compiler_params=room(4),
+    )(r, v, u, *(near(x) for x in shares))
+
+
+def combine(r, v, u, weights):
+    rows, count, cols = r.shape
+
+    def body(r_ref, v_ref, u_ref, weights_ref, out, whole, sem):
+        w = weights_ref[...]
+        c0, c1, c2 = (jnp.broadcast_to(w[:, j : j + 1], (count, cols)) for j in range(3))
+
+        def tile(t, _):
+            for i in range(8):
+                at = 8 * t + i
+                strided_rows(whole, at, rows + PAD, c0 * r_ref[at] + c1 * v_ref[at] + c2 * u_ref[at])
+            return 0
+
+        lax.fori_loop(0, rows // 8, tile, 0)
         copies = [
             pltpu.make_async_copy(
                 whole.at[b, :, pl.ds(0, rows), :], out.at[:, :, pl.ds(128 * b, 128)], sem.at[b]
@@ -455,18 +483,16 @@
 
     return pl.pallas_call(
         body,
-        in_specs=[VMEM] * (3 + number),
-        out_specs=[ANY] + [VMEM] * (2 + (groups - 2) * len(widths)),
-        out_shape=[jax.ShapeDtypeStruct((count, rows, cols), F32)]
-        + [in_vmem(cols // 128, count, high, 128)] * 2
-        + [in_vmem(wide // 128, count, high, 128) for _ in range(groups - 2) for wide in widths],
+        in_specs=[VMEM] * 4,
+        out_specs=ANY,
+        out_shape=jax.ShapeDtypeStruct((count, rows, cols), F32),
         scratch_shapes=[
             pltpu.VMEM((cols // 128, count, rows + PAD, 128), F32),
             pltpu.SemaphoreType.DMA((cols // 128,)),
         ],
-        name="iterate",
+        name="combine",
         compiler_params=room(6),
-    )(r, v, u, *(near(x) for x in shares))
+    )(r, v, u, weights)
 
 
 def half_sums(mapping, left, fields, start=None):
@@ -495,9 +521,11 @@
             for (b, a), x in zip(spots, acc):
                 out[b, d, a : a + 8, :] = x
 
-        def pair_of(first, out, begin):
+        per = min(4 if len(spots) <= 2 else 2, share)
+
+        def step_of(first, out, begin):
             def step(i, _):
-                at = [2 * i, 2 * i + 1]
+                at = [per * i + j for j in range(per)]
                 for d, acc in zip(at, sums_of([first + d for d in at], [begin(d) for d in at])):
                     store(out, d, acc)
                 return 0
@@ -506,14 +534,14 @@
 
         if start is None:
             none = lambda d: [jnp.zeros((8, 128), F32) for _ in spots]
-            lax.fori_loop(0, dates // 2, pair_of(0, refs[groups], none), 0)
+            lax.fori_loop(0, dates // per, step_of(0, refs[groups], none), 0)
         else:
             me = half_and_member(groups)[1]
             begun = refs[groups]
             for m, out in enumerate(refs[groups + 1 :]):
                 first = jnp.bitwise_xor(me, m) * share
                 begin = lambda d, first=first: [begun[b, first + d, a : a + 8, :] for b, a in spots]
-                lax.fori_loop(0, share // 2, pair_of(dates + m * share, out, begin), 0)
+                lax.fori_loop(0, share // per, step_of(dates + m * share, out, begin), 0)
 
     args = list(fields) + ([] if start is None else [start])
     out_shape = (
@@ -589,7 +617,8 @@
     r, v, u, moments = join(first, second, *fields)
     shares = summands(moments, "strip")
     mapping = inverse_map(pairs, groups)
-    phase, keep, beside, *far = iterate(r, v, u, shares, groups, widths)
+    weights, keep, beside, *far = iterate(r, v, u, shares, groups, widths)
+    phase = combine(r, v, u, weights)
     beside = exchange(beside, "ifg", 1)
     parts, left = ([], 0)
     for i, wide in enumerate(widths):

time: 122 us -> 120 us (0.984)
  waiting for transfers between devices: 43.1 us -> 41.1 us
    ppermute x34, waiting for transfers between devices: 43.1 us -> 41.1 us  [exchange(): return lax.ppermute(x, axis, [(i, i ^ mask) for i in range(size)])]
    pallas_call x1 -> x2, Pallas kernels: 3.78 us -> 4.05 us  [the longest x1 2.1 us: combine(): pl.pallas_call(body, in_specs=[VMEM] * 4, out_specs=ANY, out_shape=jax.Sh...]
  transfers between devices with their start and end apart: 36 -> 36, of which waited for: 12 -> 10; matrix products, arithmetic and copies ran while one was open for 0% -> 0% of each run, Pallas kernels for 25% -> 27%
where the time goes in v2:
time: 120 us
  waiting for transfers between devices  41.1 us (34%)
  starting transfers between devices  39 us (32%)
  Pallas kernels  38.9 us (32%)
    ppermute x34, waiting for transfers between devices, exchange(): return lax.ppermute(x, axis, [(i, i ^ mask) for i in range(size)])  41.1 us
    ppermute x34, starting transfers between devices, exchange(): return lax.ppermute(x, axis, [(i, i ^ mask) for i in range(size)])  35.4 us
    pallas_call x10, Pallas kernels, half_sums(): pl.pallas_call(body, in_specs=[SMEM] + [VMEM] * len(args), out_specs=[VME...  14.6 us
    pallas_call x1, Pallas kernels, interior(): pl.pallas_call(body, in_specs=[ANY] * 3, out_specs=[VMEM] * 7, out_shape=...  13 us
    ppermute x2, starting transfers between devices, on_device(): lax.ppermute(x, 'strip', [p for i in range(at, strips - 1, 2) for p in ((...  3.69 us
    pallas_call x1, Pallas kernels, inverse_map(): pl.pallas_call(body, in_specs=[VMEM], out_specs=VMEM, out_shape=jax.Shape...  3.04 us
  transfers between devices with their start and end apart: 36, of which 10 were waited for; matrix products, arithmetic and copies ran while one was open for 0% of the time, Pallas kernels for 27%

profile of v2, /device:TPU:0, one launch (start us, length us, event | category | flops | bytes accessed | tf_op | source)
XLA Modules:
  0.0 119.8 jit_solution(10331947087731112271)
XLA Ops:
  0.6 2.2 %edges.1 = (f32[6,8,1024]{2,1,0:T(8,128)S(1)}, f32[6,8,1024]{2,1,0:T(8,128)S(1)}) custom-call(f32[8,64,1024]{2,1,0:T(8,128)} %c_hbm.1, f32[8,64,1024]{2,1,0:T(8,128)} %x_hbm.1, f32[8,64,1024]{2,1,0:T(8,128)} %y_hbm.1, f32[8,64,1024]{2,1,0:T(8,128)} %c_hbm.1, f32[8,64,1024]{2,1,0:T(8,128)} %x_hbm.1, f32[8,64,1024]{2,1,0:T(8,128)} %y_hbm.1), custom_call_target="tpu_custom_call" | custom-call | tf_op jit(solution)/shard_map/edges/pallas_call | solution.py:159
  2.9 3.0 %collective-permute-start = (f32[6,8,1024]{2,1,0:T(8,128)S(1)}, f32[6,8,1024]{2,1,0:T(8,128)S(1)}, u32[]{:S(2)}, u32[]{:S(2)}) collective-permute-start(f32[6,8,1024]{2,1,0:T(8,128)S(1)} %get-tuple-element.48), channel_id=1, source_target_pairs={{0,1},{1,0},{2,3},{3,2},{4,5},{5,4},{6,7},{7,6},{8,9},{9,8},{10,11... | collective-permute-start | bytes 589832 | tf_op jit(solution)/shard_map/ppermute | solution.py:613
  5.9 0.7 collective-permute-start.1
  6.6 13.0 %interior.1 = (f32[64,8,1024]{2,1,0:T(8,128)S(1)}, f32[64,8,1024]{2,1,0:T(8,128)S(1)}, f32[64,8,1024]{2,1,0:T(8,128)S(1)}, f32[64,8,1024]{2,1,0:T(8,128)S(1)}, f...) custom-call(f32[8,64,1024]{2,1,0:T(8,128)} %c_hbm.1, f32[8,64,1024]{2,1,0:T(8,128)} %x_hbm.1, ...), custom_call_target="tpu_custom_call" | custom-call | tf_op jit(solution)/shard_map/interior/pallas_call | solution.py:284
  19.6 0.0 collective-permute-done.got_first
  19.6 0.9 join.1
  20.5 4.2 %collective-permute-start.2 = (f32[8,128]{1,0:T(8,128)S(1)}, f32[8,128]{1,0:T(8,128)S(1)}, u32[]{:S(2)}, u32[]{:S(2)}) collective-permute-start(f32[8,128]{1,0:T(8,128)S(1)} %get-tuple-element.60.refs_3_), channel_id=1, source_target_pairs={{0,1},{1,0},{2,3},{3,2},{4,5},{5,4},{6,7},{7,6},{8,9},{9,8},{10,11... | collective-permute-start | bytes 12296 | tf_op jit(solution)/shard_map/ppermute | solution.py:592
  24.7 0.0 collective-permute-start.3
  24.7 1.5 %collective-permute-start.4 = (f32[8,128]{1,0:T(8,128)S(1)}, f32[8,128]{1,0:T(8,128)S(1)}, u32[]{:S(2)}, u32[]{:S(2)}) collective-permute-start(f32[8,128]{1,0:T(8,128)S(1)} %get-tuple-element.60.refs_3_), channel_id=1, source_target_pairs={{0,3},{1,2},{2,1},{3,0},{4,7},{5,6},{6,5},{7,4},{8,11},{9,10},{10,... | collective-permute-start | bytes 12296 | tf_op jit(solution)/shard_map/ppermute | solution.py:592
  26.2 0.0 collective-permute-done.2.refs_4_
  26.3 2.0 %collective-permute-done.3.refs_5_ = f32[8,128]{1,0:T(8,128)S(1)} collective-permute-done((f32[8,128]{1,0:T(8,128)S(1)}, f32[8,128]{1,0:T(8,128)S(1)}, u32[]{:S(2)}, u32[]{:S(2)}) %collective-permute-start.3) | collective-permute-done | bytes 4128 | tf_op jit(solution)/shard_map/ppermute | solution.py:592
  28.3 0.9 collective-permute-done.4.refs_6_
  29.2 1.9 %iterate.1 = (f32[8,128]{1,0:T(8,128)S(1)}, f32[8,8,16,128]{3,2,1,0:T(8,128)S(1)}, f32[8,8,16,128]{3,2,1,0:T(8,128)S(1)}, f32[1,8,16,128]{3,2,1,0:T(8,128)S(1)},...) custom-call(f32[64,8,1024]{2,1,0:T(8,128)S(1)} %get-tuple-element.57, ...), custom_call_target="tpu_custom_call" | custom-call | tf_op jit(solution)/shard_map/iterate/pallas_call | solution.py:447
  31.1 0.1 collective-permute-start.5
  31.2 1.6 %collective-permute-start.24 = (f32[2,8,16,128]{3,2,1,0:T(8,128)S(1)}, f32[2,8,16,128]{3,2,1,0:T(8,128)S(1)}, u32[]{:S(2)}, u32[]{:S(2)}) collective-permute-start(f32[2,8,16,128]{3,2,1,0:T(8,128)S(1)} %get-tuple-element.82), channel_id=1, source_target_pairs={{0,8},{4,12},{8,0},{12,4},{16,24},{20,28},{24,16},{28,20},{1,9},{5... | collective-permute-start | bytes 393224 | tf_op jit(solution)/shard_map/ppermute | solution.py:592
  32.9 0.2 collective-permute-start.25
  33.1 1.6 %collective-permute-start.18 = (f32[2,8,16,128]{3,2,1,0:T(8,128)S(1)}, f32[2,8,16,128]{3,2,1,0:T(8,128)S(1)}, u32[]{:S(2)}, u32[]{:S(2)}) collective-permute-start(f32[2,8,16,128]{3,2,1,0:T(8,128)S(1)} %get-tuple-element.76), channel_id=1, source_target_pairs={{0,8},{4,12},{8,0},{12,4},{16,24},{20,28},{24,16},{28,20},{1,9},{5... | collective-permute-start | bytes 393224 | tf_op jit(solution)/shard_map/ppermute | solution.py:592
  34.7 0.1 collective-permute-start.19
  34.8 2.9 %collective-permute-done.24.refs_2_ = f32[2,8,16,128]{3,2,1,0:T(8,128)S(1)} collective-permute-done((f32[2,8,16,128]{3,2,1,0:T(8,128)S(1)}, f32[2,8,16,128]{3,2,1,0:T(8,128)S(1)}, u32[]{:S(2)}, u32[]{:S(2)}) %collective-permute-start.24) | collective-permute-done | bytes 131104 | tf_op jit(solution)/shard_map/ppermute | solution.py:592
  37.7 1.6 %collective-permute-start.12 = (f32[2,8,16,128]{3,2,1,0:T(8,128)S(1)}, f32[2,8,16,128]{3,2,1,0:T(8,128)S(1)}, u32[]{:S(2)}, u32[]{:S(2)}) collective-permute-start(f32[2,8,16,128]{3,2,1,0:T(8,128)S(1)} %get-tuple-element.70), channel_id=1, source_target_pairs={{0,8},{4,12},{8,0},{12,4},{16,24},{20,28},{24,16},{28,20},{1,9},{5... | collective-permute-start | bytes 393224 | tf_op jit(solution)/shard_map/ppermute | solution.py:592
  39.2 0.3 collective-permute-done.25.refs_3_
  39.6 1.9 %collective-permute-start.13 = (f32[2,8,16,128]{3,2,1,0:T(8,128)S(1)}, f32[2,8,16,128]{3,2,1,0:T(8,128)S(1)}, u32[]{:S(2)}, u32[]{:S(2)}) collective-permute-start(f32[2,8,16,128]{3,2,1,0:T(8,128)S(1)} %get-tuple-element.71), channel_id=1, source_target_pairs={{0,12},{4,8},{8,4},{12,0},{16,28},{20,24},{24,20},{28,16},{1,13},{... | collective-permute-start | bytes 393224 | tf_op jit(solution)/shard_map/ppermute | solution.py:592
  41.5 1.8 %collective-permute-done.18.refs_2_ = f32[2,8,16,128]{3,2,1,0:T(8,128)S(1)} collective-permute-done((f32[2,8,16,128]{3,2,1,0:T(8,128)S(1)}, f32[2,8,16,128]{3,2,1,0:T(8,128)S(1)}, u32[]{:S(2)}, u32[]{:S(2)}) %collective-permute-start.18) | collective-permute-done | bytes 131104 | tf_op jit(solution)/shard_map/ppermute | solution.py:592
  43.3 1.6 %collective-permute-start.30 = (f32[1,8,16,128]{3,2,1,0:T(8,128)S(1)}, f32[1,8,16,128]{3,2,1,0:T(8,128)S(1)}, u32[]{:S(2)}, u32[]{:S(2)}) collective-permute-start(f32[1,8,16,128]{3,2,1,0:T(8,128)S(1)} %get-tuple-element.88), channel_id=1, source_target_pairs={{0,8},{4,12},{8,0},{12,4},{16,24},{20,28},{24,16},{28,20},{1,9},{5... | collective-permute-start | bytes 196616 | tf_op jit(solution)/shard_map/ppermute | solution.py:592
  44.9 0.0 collective-permute-start.31
  44.9 3.0 %inverse_map.1.map_ref = f32[32,32]{1,0:T(8,128)S(1)} custom-call(s32[2,64]{1,0:T(2,128)S(1)} %bitcast.1), custom_call_target="tpu_custom_call" | custom-call | tf_op jit(solution)/shard_map/inverse_map/pallas_call | solution.py:111
  47.9 1.7 %cross_sums.8 = f32[2,16,16,128]{3,2,1,0:T(8,128)S(1)} custom-call(f32[32,32]{1,0:T(8,128)S(1)} %inverse_map.1.map_ref, f32[8,8,16,128]{3,2,1,0:T(8,128)S(1)} %get-tuple-element.62.refs_0_, f32[8,8,16,128]{3,2,1,0:T(8,128)S(1)} %collective-permute-done.5.refs_1_, f32[2,8,16,128]{3,2,1,0:T(8,128)S(1)} %collective-permute-done.24.refs_2_, ...), custom_call_target="tpu_custom_call" | custom-call | tf_op jit(solution)/shard_map/cross_sums/pallas_call | solution.py:552
  49.6 2.7 %collective-permute-start.26 = (f32[2,16,16,128]{3,2,1,0:T(8,128)S(1)}, f32[2,16,16,128]{3,2,1,0:T(8,128)S(1)}, u32[]{:S(2)}, u32[]{:S(2)}) collective-permute-start(f32[2,16,16,128]{3,2,1,0:T(8,128)S(1)} %cross_sums.8), channel_id=1, source_target_pairs={{0,16},{4,20},{8,24},{12,28},{16,0},{20,4},{24,8},{28,12},{1,17},{... | collective-permute-start | bytes 786440 | tf_op jit(solution)/shard_map/ppermute | solution.py:592
  52.2 1.6 %cross_sums.7 = f32[2,16,16,128]{3,2,1,0:T(8,128)S(1)} custom-call(f32[32,32]{1,0:T(8,128)S(1)} %inverse_map.1.map_ref, f32[8,8,16,128]{3,2,1,0:T(8,128)S(1)} %get-tuple-element.62.refs_0_, f32[8,8,16,128]{3,2,1,0:T(8,128)S(1)} %collective-permute-done.5.refs_1_, f32[2,8,16,128]{3,2,1,0:T(8,128)S(1)} %collective-permute-done.18.refs_2_, ...), custom_call_target="tpu_custom_call" | custom-call | tf_op jit(solution)/shard_map/cross_sums/pallas_call | solution.py:552
  53.9 0.4 collective-permute-start.20
  54.3 0.5 collective-permute-start.6
  54.8 1.6 %cross_sums.6 = f32[2,16,16,128]{3,2,1,0:T(8,128)S(1)} custom-call(f32[32,32]{1,0:T(8,128)S(1)} %inverse_map.1.map_ref, f32[8,8,16,128]{3,2,1,0:T(8,128)S(1)} %get-tuple-element.62.refs_0_, f32[8,8,16,128]{3,2,1,0:T(8,128)S(1)} %collective-permute-done.5.refs_1_, f32[2,8,16,128]{3,2,1,0:T(8,128)S(1)} %collective-permute-done.12.refs_2_, ...), custom_call_target="tpu_custom_call" | custom-call | tf_op jit(solution)/shard_map/cross_sums/pallas_call | solution.py:552
  56.4 1.0 collective-permute-start.7
  57.4 2.6 %collective-permute-start.14 = (f32[2,16,16,128]{3,2,1,0:T(8,128)S(1)}, f32[2,16,16,128]{3,2,1,0:T(8,128)S(1)}, u32[]{:S(2)}, u32[]{:S(2)}) collective-permute-start(f32[2,16,16,128]{3,2,1,0:T(8,128)S(1)} %cross_sums.6), channel_id=1, source_target_pairs={{0,16},{4,20},{8,24},{12,28},{16,0},{20,4},{24,8},{28,12},{1,17},{... | collective-permute-start | bytes 786440 | tf_op jit(solution)/shard_map/ppermute | solution.py:592
  59.9 1.2 %cross_sums.9 = f32[1,16,16,128]{3,2,1,0:T(8,128)S(1)} custom-call(f32[32,32]{1,0:T(8,128)S(1)} %inverse_map.1.map_ref, f32[8,8,16,128]{3,2,1,0:T(8,128)S(1)} %get-tuple-element.62.refs_0_, f32[8,8,16,128]{3,2,1,0:T(8,128)S(1)} %collective-permute-done.5.refs_1_, f32[1,8,16,128]{3,2,1,0:T(8,128)S(1)} %collective-permute-done.30.refs_2_, ...), custom_call_target="tpu_custom_call" | custom-call | tf_op jit(solution)/shard_map/cross_sums/pallas_call | solution.py:552
  61.2 4.8 %collective-permute-done.6.refs_2_ = f32[1,8,16,128]{3,2,1,0:T(8,128)S(1)} collective-permute-done((f32[1,8,16,128]{3,2,1,0:T(8,128)S(1)}, f32[1,8,16,128]{3,2,1,0:T(8,128)S(1)}, u32[]{:S(2)}, u32[]{:S(2)}) %collective-permute-start.6) | collective-permute-done | bytes 65568 | tf_op jit(solution)/shard_map/ppermute | solution.py:592
  66.0 3.8 %collective-permute-start.32 = (f32[1,16,16,128]{3,2,1,0:T(8,128)S(1)}, f32[1,16,16,128]{3,2,1,0:T(8,128)S(1)}, u32[]{:S(2)}, u32[]{:S(2)}) collective-permute-start(f32[1,16,16,128]{3,2,1,0:T(8,128)S(1)} %cross_sums.9), channel_id=1, source_target_pairs={{0,16},{4,20},{8,24},{12,28},{16,0},{20,4},{24,8},{28,12},{1,17},{... | collective-permute-start | bytes 393224 | tf_op jit(solution)/shard_map/ppermute | solution.py:592
  69.8 1.2 %cross_sums.5 = f32[1,16,16,128]{3,2,1,0:T(8,128)S(1)} custom-call(f32[32,32]{1,0:T(8,128)S(1)} %inverse_map.1.map_ref, f32[8,8,16,128]{3,2,1,0:T(8,128)S(1)} %get-tuple-element.62.refs_0_, f32[8,8,16,128]{3,2,1,0:T(8,128)S(1)} %collective-permute-done.5.refs_1_, f32[1,8,16,128]{3,2,1,0:T(8,128)S(1)} %collective-permute-done.6.refs_2_, ...), custom_call_target="tpu_custom_call" | custom-call | tf_op jit(solution)/shard_map/cross_sums/pallas_call | solution.py:552
  71.0 0.4 collective-permute-start.8
  71.4 24.9 %collective-permute-done.32.refs_4_ = f32[1,16,16,128]{3,2,1,0:T(8,128)S(1)} collective-permute-done((f32[1,16,16,128]{3,2,1,0:T(8,128)S(1)}, f32[1,16,16,128]{3,2,1,0:T(8,128)S(1)}, u32[]{:S(2)}, u32[]{:S(2)}) %collective-permute-start.32) | collective-permute-done | bytes 131104 | tf_op jit(solution)/shard_map/ppermute | solution.py:592
  96.3 1.2 %own_sums.9 = (f32[1,4,16,128]{3,2,1,0:T(8,128)S(1)}, f32[1,4,16,128]{3,2,1,0:T(8,128)S(1)}, f32[1,4,16,128]{3,2,1,0:T(8,128)S(1)}, f32[1,4,16,128]{3,2,1,0:T(8,128)S(1)}) custom-call(f32[32,32]{1,0:T(8,128)S(1)} %inverse_map.1.map_ref, f32[8,8,16,128]{3,2,1,0:T(8,128)S(1)} %get-tuple-element.62.refs_0_, ...), custom_call_target="tpu_custom_call" | custom-call | tf_op jit(solution)/shard_map/own_sums/pallas_call | solution.py:552
  97.5 0.1 collective-permute-start.33
  97.6 1.1 collective-permute-done.8.refs_4_
  98.7 1.2 %own_sums.5 = (f32[1,4,16,128]{3,2,1,0:T(8,128)S(1)}, f32[1,4,16,128]{3,2,1,0:T(8,128)S(1)}, f32[1,4,16,128]{3,2,1,0:T(8,128)S(1)}, f32[1,4,16,128]{3,2,1,0:T(8,128)S(1)}) custom-call(f32[32,32]{1,0:T(8,128)S(1)} %inverse_map.1.map_ref, f32[8,8,16,128]{3,2,1,0:T(8,128)S(1)} %get-tuple-element.62.refs_0_, ...), custom_call_target="tpu_custom_call" | custom-call | tf_op jit(solution)/shard_map/own_sums/pallas_call | solution.py:552
  99.9 1.1 collective-permute-start.35
  101.0 1.1 collective-permute-start.10
  102.1 1.4 %collective-permute-start.11 = (f32[1,4,16,128]{3,2,1,0:T(8,128)S(1)}, f32[1,4,16,128]{3,2,1,0:T(8,128)S(1)}, u32[]{:S(2)}, u32[]{:S(2)}) collective-permute-start(f32[1,4,16,128]{3,2,1,0:T(8,128)S(1)} %get-tuple-element.69), channel_id=1, source_target_pairs={{0,12},{4,8},{8,4},{12,0},{16,28},{20,24},{24,20},{28,16},{1,13},{... | collective-permute-start | bytes 98312 | tf_op jit(solution)/shard_map/ppermute | solution.py:592
  103.5 1.6 %own_sums.8 = (f32[2,4,16,128]{3,2,1,0:T(8,128)S(1)}, f32[2,4,16,128]{3,2,1,0:T(8,128)S(1)}, f32[2,4,16,128]{3,2,1,0:T(8,128)S(1)}, f32[2,4,16,128]{3,2,1,0:T(8,128)S(1)}) custom-call(f32[32,32]{1,0:T(8,128)S(1)} %inverse_map.1.map_ref, f32[8,8,16,128]{3,2,1,0:T(8,128)S(1)} %get-tuple-element.62.refs_0_, ...), custom_call_target="tpu_custom_call" | custom-call | tf_op jit(solution)/shard_map/own_sums/pallas_call | solution.py:552
  105.1 1.6 %own_sums.7 = (f32[2,4,16,128]{3,2,1,0:T(8,128)S(1)}, f32[2,4,16,128]{3,2,1,0:T(8,128)S(1)}, f32[2,4,16,128]{3,2,1,0:T(8,128)S(1)}, f32[2,4,16,128]{3,2,1,0:T(8,128)S(1)}) custom-call(f32[32,32]{1,0:T(8,128)S(1)} %inverse_map.1.map_ref, f32[8,8,16,128]{3,2,1,0:T(8,128)S(1)} %get-tuple-element.62.refs_0_, ...), custom_call_target="tpu_custom_call" | custom-call | tf_op jit(solution)/shard_map/own_sums/pallas_call | solution.py:552
  106.7 0.1 collective-permute-start.27
  106.8 0.7 collective-permute-start.28
  107.5 1.1 collective-permute-start.29
  108.6 0.4 collective-permute-start.21
  109.0 0.1 collective-permute-start.9
  109.1 1.6 %own_sums.6 = (f32[2,4,16,128]{3,2,1,0:T(8,128)S(1)}, f32[2,4,16,128]{3,2,1,0:T(8,128)S(1)}, f32[2,4,16,128]{3,2,1,0:T(8,128)S(1)}, f32[2,4,16,128]{3,2,1,0:T(8,128)S(1)}) custom-call(f32[32,32]{1,0:T(8,128)S(1)} %inverse_map.1.map_ref, f32[8,8,16,128]{3,2,1,0:T(8,128)S(1)} %get-tuple-element.62.refs_0_, ...), custom_call_target="tpu_custom_call" | custom-call | tf_op jit(solution)/shard_map/own_sums/pallas_call | solution.py:552
  110.7 0.7 collective-permute-start.22
  111.4 1.1 collective-permute-start.23
  112.5 0.4 collective-permute-start.15
  112.9 0.6 collective-permute-start.16
  113.5 0.8 collective-permute-start.17
  114.4 2.1 %combine.1 = f32[8,64,1024]{2,1,0:T(8,128)} custom-call(f32[64,8,1024]{2,1,0:T(8,128)S(1)} %get-tuple-element.57.refs_0_.r_ref, f32[64,8,1024]{2,1,0:T(8,128)S(1)} %get-tuple-element.58.refs_1_.v_ref, f32[64,8,1024]{2,1,0:T(8,128)S(1)} %get-tuple-element.59.refs_2_.u_ref, f32[8,128]{1,0:T(8,128)S(1)} %get-tuple-element.61.weights_ref), custom_call_target="tpu_custom_call" | custom-call | tf_op jit(solution)/shard_map/combine/pallas_call | solution.py:484
  116.5 2.0 %collective-permute-done.16.refs_6_ = f32[2,4,16,128]{3,2,1,0:T(8,128)S(1)} collective-permute-done((f32[2,4,16,128]{3,2,1,0:T(8,128)S(1)}, f32[2,4,16,128]{3,2,1,0:T(8,128)S(1)}, u32[]{:S(2)}, u32[]{:S(2)}) %collective-permute-start.16) | collective-permute-done | bytes 65568 | tf_op jit(solution)/shard_map/ppermute | solution.py:592
  118.6 0.2 collective-permute-done.17.refs_7_
  118.8 1.1 assemble.1
  (27 shorter events, 0.1 us)
Async XLA Ops:
  2.9 16.7 %collective-permute-start = (f32[6,8,1024]{2,1,0:T(8,128)S(1)}, f32[6,8,1024]{2,1,0:T(8,128)S(1)}, u32[]{:S(2)}, u32[]{:S(2)}) collective-permute-start(f32[6,8,1024]{2,1,0:T(8,128)S(1)} %get-tuple-element.48), channel_id=1, source_target_pairs={{0,1},{1,0},{2,3},{3,2},{4,5},{5,4},{6,7},{7,6},{8,9},{9,8},{10,11... | collective-permute-start | bytes 589832 | tf_op jit(solution)/shard_map/ppermute | solution.py:613
  5.9 13.7 %collective-permute-start.1 = (f32[6,8,1024]{2,1,0:T(8,128)S(1)}, f32[6,8,1024]{2,1,0:T(8,128)S(1)}, u32[]{:S(2)}, u32[]{:S(2)}) collective-permute-start(f32[6,8,1024]{2,1,0:T(8,128)S(1)} %get-tuple-element.49), channel_id=1, source_target_pairs={{1,2},{2,1},{5,6},{6,5},{9,10},{10,9},{13,14},{14,13},{17,18},{18,... | collective-permute-start | bytes 589832 | tf_op jit(solution)/shard_map/ppermute | solution.py:613
  20.5 5.8 %collective-permute-start.2 = (f32[8,128]{1,0:T(8,128)S(1)}, f32[8,128]{1,0:T(8,128)S(1)}, u32[]{:S(2)}, u32[]{:S(2)}) collective-permute-start(f32[8,128]{1,0:T(8,128)S(1)} %get-tuple-element.60.refs_3_), channel_id=1, source_target_pairs={{0,1},{1,0},{2,3},{3,2},{4,5},{5,4},{6,7},{7,6},{8,9},{9,8},{10,11... | collective-permute-start | bytes 12296 | tf_op jit(solution)/shard_map/ppermute | solution.py:592
  24.7 3.6 %collective-permute-start.3 = (f32[8,128]{1,0:T(8,128)S(1)}, f32[8,128]{1,0:T(8,128)S(1)}, u32[]{:S(2)}, u32[]{:S(2)}) collective-permute-start(f32[8,128]{1,0:T(8,128)S(1)} %get-tuple-element.60.refs_3_), channel_id=1, source_target_pairs={{0,2},{1,3},{2,0},{3,1},{4,6},{5,7},{6,4},{7,5},{8,10},{9,11},{10,... | collective-permute-start | bytes 12296 | tf_op jit(solution)/shard_map/ppermute | solution.py:592
  24.7 4.5 %collective-permute-start.4 = (f32[8,128]{1,0:T(8,128)S(1)}, f32[8,128]{1,0:T(8,128)S(1)}, u32[]{:S(2)}, u32[]{:S(2)}) collective-permute-start(f32[8,128]{1,0:T(8,128)S(1)} %get-tuple-element.60.refs_3_), channel_id=1, source_target_pairs={{0,3},{1,2},{2,1},{3,0},{4,7},{5,6},{6,5},{7,4},{8,11},{9,10},{10,... | collective-permute-start | bytes 12296 | tf_op jit(solution)/shard_map/ppermute | solution.py:592
  29.2 15.7 %copy-start = (s32[64,2]{0,1:T(2,128)S(1)}, s32[64,2]{0,1:T(2,128)}, u32[]{:S(2)}) copy-start(s32[64,2]{0,1:T(2,128)} %param.7) | copy-start | bytes 1540
  31.1 13.7 %collective-permute-start.5 = (f32[8,8,16,128]{3,2,1,0:T(8,128)S(1)}, f32[8,8,16,128]{3,2,1,0:T(8,128)S(1)}, u32[]{:S(2)}, u32[]{:S(2)}) collective-permute-start(f32[8,8,16,128]{3,2,1,0:T(8,128)S(1)} %get-tuple-element.63), channel_id=1, source_target_pairs={{0,4},{4,0},{8,12},{12,8},{16,20},{20,16},{24,28},{28,24},{1,5},{5... | collective-permute-start | bytes 1572872 | tf_op jit(solution)/shard_map/ppermute | solution.py:592
  31.2 6.4 %collective-permute-start.24 = (f32[2,8,16,128]{3,2,1,0:T(8,128)S(1)}, f32[2,8,16,128]{3,2,1,0:T(8,128)S(1)}, u32[]{:S(2)}, u32[]{:S(2)}) collective-permute-start(f32[2,8,16,128]{3,2,1,0:T(8,128)S(1)} %get-tuple-element.82), channel_id=1, source_target_pairs={{0,8},{4,12},{8,0},{12,4},{16,24},{20,28},{24,16},{28,20},{1,9},{5... | collective-permute-start | bytes 393224 | tf_op jit(solution)/shard_map/ppermute | solution.py:592
  32.9 6.7 %collective-permute-start.25 = (f32[2,8,16,128]{3,2,1,0:T(8,128)S(1)}, f32[2,8,16,128]{3,2,1,0:T(8,128)S(1)}, u32[]{:S(2)}, u32[]{:S(2)}) collective-permute-start(f32[2,8,16,128]{3,2,1,0:T(8,128)S(1)} %get-tuple-element.83), channel_id=1, source_target_pairs={{0,12},{4,8},{8,4},{12,0},{16,28},{20,24},{24,20},{28,16},{1,13},{... | collective-permute-start | bytes 393224 | tf_op jit(solution)/shard_map/ppermute | solution.py:592
  33.1 10.2 %collective-permute-start.18 = (f32[2,8,16,128]{3,2,1,0:T(8,128)S(1)}, f32[2,8,16,128]{3,2,1,0:T(8,128)S(1)}, u32[]{:S(2)}, u32[]{:S(2)}) collective-permute-start(f32[2,8,16,128]{3,2,1,0:T(8,128)S(1)} %get-tuple-element.76), channel_id=1, source_target_pairs={{0,8},{4,12},{8,0},{12,4},{16,24},{20,28},{24,16},{28,20},{1,9},{5... | collective-permute-start | bytes 393224 | tf_op jit(solution)/shard_map/ppermute | solution.py:592
  34.7 14.9 %collective-permute-start.19 = (f32[2,8,16,128]{3,2,1,0:T(8,128)S(1)}, f32[2,8,16,128]{3,2,1,0:T(8,128)S(1)}, u32[]{:S(2)}, u32[]{:S(2)}) collective-permute-start(f32[2,8,16,128]{3,2,1,0:T(8,128)S(1)} %get-tuple-element.77), channel_id=1, source_target_pairs={{0,12},{4,8},{8,4},{12,0},{16,28},{20,24},{24,20},{28,16},{1,13},{... | collective-permute-start | bytes 393224 | tf_op jit(solution)/shard_map/ppermute | solution.py:592
  37.7 16.2 %collective-permute-start.12 = (f32[2,8,16,128]{3,2,1,0:T(8,128)S(1)}, f32[2,8,16,128]{3,2,1,0:T(8,128)S(1)}, u32[]{:S(2)}, u32[]{:S(2)}) collective-permute-start(f32[2,8,16,128]{3,2,1,0:T(8,128)S(1)} %get-tuple-element.70), channel_id=1, source_target_pairs={{0,8},{4,12},{8,0},{12,4},{16,24},{20,28},{24,16},{28,20},{1,9},{5... | collective-permute-start | bytes 393224 | tf_op jit(solution)/shard_map/ppermute | solution.py:592
  39.6 14.7 %collective-permute-start.13 = (f32[2,8,16,128]{3,2,1,0:T(8,128)S(1)}, f32[2,8,16,128]{3,2,1,0:T(8,128)S(1)}, u32[]{:S(2)}, u32[]{:S(2)}) collective-permute-start(f32[2,8,16,128]{3,2,1,0:T(8,128)S(1)} %get-tuple-element.71), channel_id=1, source_target_pairs={{0,12},{4,8},{8,4},{12,0},{16,28},{20,24},{24,20},{28,16},{1,13},{... | collective-permute-start | bytes 393224 | tf_op jit(solution)/shard_map/ppermute | solution.py:592
  43.3 13.1 %collective-permute-start.30 = (f32[1,8,16,128]{3,2,1,0:T(8,128)S(1)}, f32[1,8,16,128]{3,2,1,0:T(8,128)S(1)}, u32[]{:S(2)}, u32[]{:S(2)}) collective-permute-start(f32[1,8,16,128]{3,2,1,0:T(8,128)S(1)} %get-tuple-element.88), channel_id=1, source_target_pairs={{0,8},{4,12},{8,0},{12,4},{16,24},{20,28},{24,16},{28,20},{1,9},{5... | collective-permute-start | bytes 196616 | tf_op jit(solution)/shard_map/ppermute | solution.py:592
  44.9 12.5 %collective-permute-start.31 = (f32[1,8,16,128]{3,2,1,0:T(8,128)S(1)}, f32[1,8,16,128]{3,2,1,0:T(8,128)S(1)}, u32[]{:S(2)}, u32[]{:S(2)}) collective-permute-start(f32[1,8,16,128]{3,2,1,0:T(8,128)S(1)} %get-tuple-element.89), channel_id=1, source_target_pairs={{0,12},{4,8},{8,4},{12,0},{16,28},{20,24},{24,20},{28,16},{1,13},{... | collective-permute-start | bytes 196616 | tf_op jit(solution)/shard_map/ppermute | solution.py:592
  49.6 51.4 %collective-permute-start.26 = (f32[2,16,16,128]{3,2,1,0:T(8,128)S(1)}, f32[2,16,16,128]{3,2,1,0:T(8,128)S(1)}, u32[]{:S(2)}, u32[]{:S(2)}) collective-permute-start(f32[2,16,16,128]{3,2,1,0:T(8,128)S(1)} %cross_sums.8), channel_id=1, source_target_pairs={{0,16},{4,20},{8,24},{12,28},{16,0},{20,4},{24,8},{28,12},{1,17},{... | collective-permute-start | bytes 786440 | tf_op jit(solution)/shard_map/ppermute | solution.py:592
  53.9 48.2 %collective-permute-start.20 = (f32[2,16,16,128]{3,2,1,0:T(8,128)S(1)}, f32[2,16,16,128]{3,2,1,0:T(8,128)S(1)}, u32[]{:S(2)}, u32[]{:S(2)}) collective-permute-start(f32[2,16,16,128]{3,2,1,0:T(8,128)S(1)} %cross_sums.7), channel_id=1, source_target_pairs={{0,16},{4,20},{8,24},{12,28},{16,0},{20,4},{24,8},{28,12},{1,17},{... | collective-permute-start | bytes 786440 | tf_op jit(solution)/shard_map/ppermute | solution.py:592
  54.3 11.7 %collective-permute-start.6 = (f32[1,8,16,128]{3,2,1,0:T(8,128)S(1)}, f32[1,8,16,128]{3,2,1,0:T(8,128)S(1)}, u32[]{:S(2)}, u32[]{:S(2)}) collective-permute-start(f32[1,8,16,128]{3,2,1,0:T(8,128)S(1)} %get-tuple-element.64), channel_id=1, source_target_pairs={{0,8},{4,12},{8,0},{12,4},{16,24},{20,28},{24,16},{28,20},{1,9},{5... | collective-permute-start | bytes 196616 | tf_op jit(solution)/shard_map/ppermute | solution.py:592
  56.4 13.4 %collective-permute-start.7 = (f32[1,8,16,128]{3,2,1,0:T(8,128)S(1)}, f32[1,8,16,128]{3,2,1,0:T(8,128)S(1)}, u32[]{:S(2)}, u32[]{:S(2)}) collective-permute-start(f32[1,8,16,128]{3,2,1,0:T(8,128)S(1)} %get-tuple-element.65), channel_id=1, source_target_pairs={{0,12},{4,8},{8,4},{12,0},{16,28},{20,24},{24,20},{28,16},{1,13},{... | collective-permute-start | bytes 196616 | tf_op jit(solution)/shard_map/ppermute | solution.py:592
  57.4 51.6 %collective-permute-start.14 = (f32[2,16,16,128]{3,2,1,0:T(8,128)S(1)}, f32[2,16,16,128]{3,2,1,0:T(8,128)S(1)}, u32[]{:S(2)}, u32[]{:S(2)}) collective-permute-start(f32[2,16,16,128]{3,2,1,0:T(8,128)S(1)} %cross_sums.6), channel_id=1, source_target_pairs={{0,16},{4,20},{8,24},{12,28},{16,0},{20,4},{24,8},{28,12},{1,17},{... | collective-permute-start | bytes 786440 | tf_op jit(solution)/shard_map/ppermute | solution.py:592
  66.0 30.3 %collective-permute-start.32 = (f32[1,16,16,128]{3,2,1,0:T(8,128)S(1)}, f32[1,16,16,128]{3,2,1,0:T(8,128)S(1)}, u32[]{:S(2)}, u32[]{:S(2)}) collective-permute-start(f32[1,16,16,128]{3,2,1,0:T(8,128)S(1)} %cross_sums.9), channel_id=1, source_target_pairs={{0,16},{4,20},{8,24},{12,28},{16,0},{20,4},{24,8},{28,12},{1,17},{... | collective-permute-start | bytes 393224 | tf_op jit(solution)/shard_map/ppermute | solution.py:592
  71.0 27.7 %collective-permute-start.8 = (f32[1,16,16,128]{3,2,1,0:T(8,128)S(1)}, f32[1,16,16,128]{3,2,1,0:T(8,128)S(1)}, u32[]{:S(2)}, u32[]{:S(2)}) collective-permute-start(f32[1,16,16,128]{3,2,1,0:T(8,128)S(1)} %cross_sums.5), channel_id=1, source_target_pairs={{0,16},{4,20},{8,24},{12,28},{16,0},{20,4},{24,8},{28,12},{1,17},{... | collective-permute-start | bytes 393224 | tf_op jit(solution)/shard_map/ppermute | solution.py:592
  97.5 2.4 %collective-permute-start.33 = (f32[1,4,16,128]{3,2,1,0:T(8,128)S(1)}, f32[1,4,16,128]{3,2,1,0:T(8,128)S(1)}, u32[]{:S(2)}, u32[]{:S(2)}) collective-permute-start(f32[1,4,16,128]{3,2,1,0:T(8,128)S(1)} %get-tuple-element.91), channel_id=1, source_target_pairs={{0,4},{4,0},{8,12},{12,8},{16,20},{20,16},{24,28},{28,24},{1,5},{5... | collective-permute-start | bytes 98312 | tf_op jit(solution)/shard_map/ppermute | solution.py:592
  98.7 8.0 %collective-permute-start.34 = (f32[1,4,16,128]{3,2,1,0:T(8,128)S(1)}, f32[1,4,16,128]{3,2,1,0:T(8,128)S(1)}, u32[]{:S(2)}, u32[]{:S(2)}) collective-permute-start(f32[1,4,16,128]{3,2,1,0:T(8,128)S(1)} %get-tuple-element.92), channel_id=1, source_target_pairs={{0,8},{4,12},{8,0},{12,4},{16,24},{20,28},{24,16},{28,20},{1,9},{5... | collective-permute-start | bytes 98312 | tf_op jit(solution)/shard_map/ppermute | solution.py:592
  99.9 6.9 %collective-permute-start.35 = (f32[1,4,16,128]{3,2,1,0:T(8,128)S(1)}, f32[1,4,16,128]{3,2,1,0:T(8,128)S(1)}, u32[]{:S(2)}, u32[]{:S(2)}) collective-permute-start(f32[1,4,16,128]{3,2,1,0:T(8,128)S(1)} %get-tuple-element.93), channel_id=1, source_target_pairs={{0,12},{4,8},{8,4},{12,0},{16,28},{20,24},{24,20},{28,16},{1,13},{... | collective-permute-start | bytes 98312 | tf_op jit(solution)/shard_map/ppermute | solution.py:592
  101.0 6.5 %collective-permute-start.10 = (f32[1,4,16,128]{3,2,1,0:T(8,128)S(1)}, f32[1,4,16,128]{3,2,1,0:T(8,128)S(1)}, u32[]{:S(2)}, u32[]{:S(2)}) collective-permute-start(f32[1,4,16,128]{3,2,1,0:T(8,128)S(1)} %get-tuple-element.68), channel_id=1, source_target_pairs={{0,8},{4,12},{8,0},{12,4},{16,24},{20,28},{24,16},{28,20},{1,9},{5... | collective-permute-start | bytes 98312 | tf_op jit(solution)/shard_map/ppermute | solution.py:592
  102.1 6.5 %collective-permute-start.11 = (f32[1,4,16,128]{3,2,1,0:T(8,128)S(1)}, f32[1,4,16,128]{3,2,1,0:T(8,128)S(1)}, u32[]{:S(2)}, u32[]{:S(2)}) collective-permute-start(f32[1,4,16,128]{3,2,1,0:T(8,128)S(1)} %get-tuple-element.69), channel_id=1, source_target_pairs={{0,12},{4,8},{8,4},{12,0},{16,28},{20,24},{24,20},{28,16},{1,13},{... | collective-permute-start | bytes 98312 | tf_op jit(solution)/shard_map/ppermute | solution.py:592
  106.7 4.7 %collective-permute-start.27 = (f32[2,4,16,128]{3,2,1,0:T(8,128)S(1)}, f32[2,4,16,128]{3,2,1,0:T(8,128)S(1)}, u32[]{:S(2)}, u32[]{:S(2)}) collective-permute-start(f32[2,4,16,128]{3,2,1,0:T(8,128)S(1)} %get-tuple-element.85), channel_id=1, source_target_pairs={{0,4},{4,0},{8,12},{12,8},{16,20},{20,16},{24,28},{28,24},{1,5},{5... | collective-permute-start | bytes 196616 | tf_op jit(solution)/shard_map/ppermute | solution.py:592
  106.8 5.7 %collective-permute-start.28 = (f32[2,4,16,128]{3,2,1,0:T(8,128)S(1)}, f32[2,4,16,128]{3,2,1,0:T(8,128)S(1)}, u32[]{:S(2)}, u32[]{:S(2)}) collective-permute-start(f32[2,4,16,128]{3,2,1,0:T(8,128)S(1)} %get-tuple-element.86), channel_id=1, source_target_pairs={{0,8},{4,12},{8,0},{12,4},{16,24},{20,28},{24,16},{28,20},{1,9},{5... | collective-permute-start | bytes 196616 | tf_op jit(solution)/shard_map/ppermute | solution.py:592
  107.5 5.4 %collective-permute-start.29 = (f32[2,4,16,128]{3,2,1,0:T(8,128)S(1)}, f32[2,4,16,128]{3,2,1,0:T(8,128)S(1)}, u32[]{:S(2)}, u32[]{:S(2)}) collective-permute-start(f32[2,4,16,128]{3,2,1,0:T(8,128)S(1)} %get-tuple-element.87), channel_id=1, source_target_pairs={{0,12},{4,8},{8,4},{12,0},{16,28},{20,24},{24,20},{28,16},{1,13},{... | collective-permute-start | bytes 196616 | tf_op jit(solution)/shard_map/ppermute | solution.py:592
  108.6 4.9 %collective-permute-start.21 = (f32[2,4,16,128]{3,2,1,0:T(8,128)S(1)}, f32[2,4,16,128]{3,2,1,0:T(8,128)S(1)}, u32[]{:S(2)}, u32[]{:S(2)}) collective-permute-start(f32[2,4,16,128]{3,2,1,0:T(8,128)S(1)} %get-tuple-element.79), channel_id=1, source_target_pairs={{0,4},{4,0},{8,12},{12,8},{16,20},{20,16},{24,28},{28,24},{1,5},{5... | collective-permute-start | bytes 196616 | tf_op jit(solution)/shard_map/ppermute | solution.py:592
  109.0 1.7 %collective-permute-start.9 = (f32[1,4,16,128]{3,2,1,0:T(8,128)S(1)}, f32[1,4,16,128]{3,2,1,0:T(8,128)S(1)}, u32[]{:S(2)}, u32[]{:S(2)}) collective-permute-start(f32[1,4,16,128]{3,2,1,0:T(8,128)S(1)} %get-tuple-element.67), channel_id=1, source_target_pairs={{0,4},{4,0},{8,12},{12,8},{16,20},{20,16},{24,28},{28,24},{1,5},{5... | collective-permute-start | bytes 98312 | tf_op jit(solution)/shard_map/ppermute | solution.py:592
  110.7 5.8 %collective-permute-start.22 = (f32[2,4,16,128]{3,2,1,0:T(8,128)S(1)}, f32[2,4,16,128]{3,2,1,0:T(8,128)S(1)}, u32[]{:S(2)}, u32[]{:S(2)}) collective-permute-start(f32[2,4,16,128]{3,2,1,0:T(8,128)S(1)} %get-tuple-element.80), channel_id=1, source_target_pairs={{0,8},{4,12},{8,0},{12,4},{16,24},{20,28},{24,16},{28,20},{1,9},{5... | collective-permute-start | bytes 196616 | tf_op jit(solution)/shard_map/ppermute | solution.py:592
  111.4 5.1 %collective-permute-start.23 = (f32[2,4,16,128]{3,2,1,0:T(8,128)S(1)}, f32[2,4,16,128]{3,2,1,0:T(8,128)S(1)}, u32[]{:S(2)}, u32[]{:S(2)}) collective-permute-start(f32[2,4,16,128]{3,2,1,0:T(8,128)S(1)} %get-tuple-element.81), channel_id=1, source_target_pairs={{0,12},{4,8},{8,4},{12,0},{16,28},{20,24},{24,20},{28,16},{1,13},{... | collective-permute-start | bytes 196616 | tf_op jit(solution)/shard_map/ppermute | solution.py:592
  112.5 4.0 %collective-permute-start.15 = (f32[2,4,16,128]{3,2,1,0:T(8,128)S(1)}, f32[2,4,16,128]{3,2,1,0:T(8,128)S(1)}, u32[]{:S(2)}, u32[]{:S(2)}) collective-permute-start(f32[2,4,16,128]{3,2,1,0:T(8,128)S(1)} %get-tuple-element.73), channel_id=1, source_target_pairs={{0,4},{4,0},{8,12},{12,8},{16,20},{20,16},{24,28},{28,24},{1,5},{5... | collective-permute-start | bytes 196616 | tf_op jit(solution)/shard_map/ppermute | solution.py:592
  112.9 5.6 %collective-permute-start.16 = (f32[2,4,16,128]{3,2,1,0:T(8,128)S(1)}, f32[2,4,16,128]{3,2,1,0:T(8,128)S(1)}, u32[]{:S(2)}, u32[]{:S(2)}) collective-permute-start(f32[2,4,16,128]{3,2,1,0:T(8,128)S(1)} %get-tuple-element.74), channel_id=1, source_target_pairs={{0,8},{4,12},{8,0},{12,4},{16,24},{20,28},{24,16},{28,20},{1,9},{5... | collective-permute-start | bytes 196616 | tf_op jit(solution)/shard_map/ppermute | solution.py:592
  113.5 5.2 %collective-permute-start.17 = (f32[2,4,16,128]{3,2,1,0:T(8,128)S(1)}, f32[2,4,16,128]{3,2,1,0:T(8,128)S(1)}, u32[]{:S(2)}, u32[]{:S(2)}) collective-permute-start(f32[2,4,16,128]{3,2,1,0:T(8,128)S(1)} %get-tuple-element.75), channel_id=1, source_target_pairs={{0,12},{4,8},{8,4},{12,0},{16,28},{20,24},{24,20},{28,16},{1,13},{... | collective-permute-start | bytes 196616 | tf_op jit(solution)/shard_map/ppermute | solution.py:592

commit v3 on v2

--- a/solution.py
+++ b/solution.py
@@ -9,6 +9,7 @@
 SLICES = (1, 2, 2, 2, 1)
 CHUNKS = len(SLICES)
 PAD = 8
+EARLY = 12
 damping = 0.1
 TINY = 1e-6
 F32 = jnp.float32
@@ -70,6 +71,14 @@
     return parts[0]
 
 
+def eliminated(w, pivots):
+    row = lax.broadcasted_iota(jnp.int32, w.shape, 0)
+    for j in pivots:
+        pivot = w[j : j + 1] / w[j : j + 1, j : j + 1]
+        w = jnp.where(row == j, pivot, w - w[:, j : j + 1] * pivot)
+    return w
+
+
 def inverse_map(pairs, groups):
     number = pairs.shape[0]
     inner = number // 2
@@ -77,7 +86,7 @@
     share = DATES // (2 * groups)
     count = number // (2 * groups)
 
-    def body(pair, out, work):
+    def body(pair, work):
         h, me = half_and_member(groups)
 
         def twin(i, each):
@@ -100,23 +109,32 @@
         work[...] = jnp.zeros_like(work)
         work[:, :DATES] = normal
         work[:, DATES : DATES + number] = back
-        w = work[...]
-        row = lax.broadcasted_iota(jnp.int32, (DATES, wide), 0)
-        for j in range(DATES):
-            pivot = w[j : j + 1] / w[j : j + 1, j : j + 1]
-            w = jnp.where(row == j, pivot, w - w[:, j : j + 1] * pivot)
-        work[...] = w
-        out[...] = work[:, DATES : DATES + inner]
+        work[...] = eliminated(work[...], range(EARLY))
+
+    return pl.pallas_call(
+        body,
+        in_specs=[VMEM],
+        out_specs=VMEM,
+        out_shape=in_vmem(DATES, wide),
+        name="inverse_map",
+        compiler_params=room(2),
+    )(pairs.T)
+
+
+def inverse_rest(work, inner):
+    def body(begun, out, scratch):
+        scratch[...] = eliminated(begun[...], range(EARLY, DATES))
+        out[...] = scratch[:, DATES : DATES + inner]
 
     return pl.pallas_call(
         body,
         in_specs=[VMEM],
         out_specs=VMEM,
         out_shape=jax.ShapeDtypeStruct((DATES, inner), F32),
-        scratch_shapes=[pltpu.VMEM((DATES, wide), F32)],
-        name="inverse_map",
+        scratch_shapes=[pltpu.VMEM(work.shape, F32)],
+        name="inverse_rest",
         compiler_params=room(2),
-    )(pairs.T)
+    )(near(work))
 
 
 def edges(coh, gx, gy):
@@ -616,7 +634,8 @@
     fields = interior(coherence, grad_x, grad_y)
     r, v, u, moments = join(first, second, *fields)
     shares = summands(moments, "strip")
-    mapping = inverse_map(pairs, groups)
+    begun = inverse_map(pairs, groups)
+    mapping = inverse_rest(begun, pairs.shape[0] // 2)
     weights, keep, beside, *far = iterate(r, v, u, shares, groups, widths)
     phase = combine(r, v, u, weights)
     beside = exchange(beside, "ifg", 1)

time: 120 us -> 120 us (level)
    pallas_call x1 -> x2, Pallas kernels: 3.04 us -> 3.04 us  [the longest x1 1.71 us: inverse_rest(): pl.pallas_call(body, in_specs=[VMEM], out_specs=VMEM, out_shape=jax.Shape...]
where the time goes in v3:
time: 120 us
  waiting for transfers between devices  41.1 us (34%)
  starting transfers between devices  39 us (32%)
  Pallas kernels  38.9 us (32%)
    ppermute x34, waiting for transfers between devices, exchange(): return lax.ppermute(x, axis, [(i, i ^ mask) for i in range(size)])  41.1 us
    ppermute x34, starting transfers between devices, exchange(): return lax.ppermute(x, axis, [(i, i ^ mask) for i in range(size)])  35.4 us
    pallas_call x10, Pallas kernels, half_sums(): pl.pallas_call(body, in_specs=[SMEM] + [VMEM] * len(args), out_specs=[VME...  14.6 us
    pallas_call x1, Pallas kernels, interior(): pl.pallas_call(body, in_specs=[ANY] * 3, out_specs=[VMEM] * 7, out_shape=...  13 us
    ppermute x2, starting transfers between devices, on_device(): lax.ppermute(x, 'strip', [p for i in range(at, strips - 1, 2) for p in ((...  3.69 us
  transfers between devices with their start and end apart: 36, of which 10 were waited for; matrix products, arithmetic and copies ran while one was open for 0% of the time, Pallas kernels for 27%

profile of v3, /device:TPU:0, one launch (start us, length us, event | category | flops | bytes accessed | tf_op | source)
XLA Modules:
  0.0 119.8 jit_solution(4014676788779499951)
XLA Ops:
  0.6 2.2 %edges.1 = (f32[6,8,1024]{2,1,0:T(8,128)S(1)}, f32[6,8,1024]{2,1,0:T(8,128)S(1)}) custom-call(f32[8,64,1024]{2,1,0:T(8,128)} %c_hbm.1, f32[8,64,1024]{2,1,0:T(8,128)} %x_hbm.1, f32[8,64,1024]{2,1,0:T(8,128)} %y_hbm.1, f32[8,64,1024]{2,1,0:T(8,128)} %c_hbm.1, f32[8,64,1024]{2,1,0:T(8,128)} %x_hbm.1, f32[8,64,1024]{2,1,0:T(8,128)} %y_hbm.1), custom_call_target="tpu_custom_call" | custom-call | tf_op jit(solution)/shard_map/edges/pallas_call | solution.py:177
  2.9 3.0 %collective-permute-start = (f32[6,8,1024]{2,1,0:T(8,128)S(1)}, f32[6,8,1024]{2,1,0:T(8,128)S(1)}, u32[]{:S(2)}, u32[]{:S(2)}) collective-permute-start(f32[6,8,1024]{2,1,0:T(8,128)S(1)} %get-tuple-element.48), channel_id=1, source_target_pairs={{0,1},{1,0},{2,3},{3,2},{4,5},{5,4},{6,7},{7,6},{8,9},{9,8},{10,11... | collective-permute-start | bytes 589832 | tf_op jit(solution)/shard_map/ppermute | solution.py:631
  5.9 0.7 collective-permute-start.1
  6.6 13.0 %interior.1 = (f32[64,8,1024]{2,1,0:T(8,128)S(1)}, f32[64,8,1024]{2,1,0:T(8,128)S(1)}, f32[64,8,1024]{2,1,0:T(8,128)S(1)}, f32[64,8,1024]{2,1,0:T(8,128)S(1)}, f...) custom-call(f32[8,64,1024]{2,1,0:T(8,128)} %c_hbm.1, f32[8,64,1024]{2,1,0:T(8,128)} %x_hbm.1, ...), custom_call_target="tpu_custom_call" | custom-call | tf_op jit(solution)/shard_map/interior/pallas_call | solution.py:302
  19.6 0.0 collective-permute-done.got_first
  19.6 0.9 join.1
  20.5 4.2 %collective-permute-start.2 = (f32[8,128]{1,0:T(8,128)S(1)}, f32[8,128]{1,0:T(8,128)S(1)}, u32[]{:S(2)}, u32[]{:S(2)}) collective-permute-start(f32[8,128]{1,0:T(8,128)S(1)} %get-tuple-element.60.refs_3_), channel_id=1, source_target_pairs={{0,1},{1,0},{2,3},{3,2},{4,5},{5,4},{6,7},{7,6},{8,9},{9,8},{10,11... | collective-permute-start | bytes 12296 | tf_op jit(solution)/shard_map/ppermute | solution.py:610
  24.7 0.0 collective-permute-start.3
  24.7 1.5 %collective-permute-start.4 = (f32[8,128]{1,0:T(8,128)S(1)}, f32[8,128]{1,0:T(8,128)S(1)}, u32[]{:S(2)}, u32[]{:S(2)}) collective-permute-start(f32[8,128]{1,0:T(8,128)S(1)} %get-tuple-element.60.refs_3_), channel_id=1, source_target_pairs={{0,3},{1,2},{2,1},{3,0},{4,7},{5,6},{6,5},{7,4},{8,11},{9,10},{10,... | collective-permute-start | bytes 12296 | tf_op jit(solution)/shard_map/ppermute | solution.py:610
  26.2 0.0 collective-permute-done.2.refs_4_
  26.3 2.0 %collective-permute-done.3.refs_5_ = f32[8,128]{1,0:T(8,128)S(1)} collective-permute-done((f32[8,128]{1,0:T(8,128)S(1)}, f32[8,128]{1,0:T(8,128)S(1)}, u32[]{:S(2)}, u32[]{:S(2)}) %collective-permute-start.3) | collective-permute-done | bytes 4128 | tf_op jit(solution)/shard_map/ppermute | solution.py:610
  28.3 0.9 collective-permute-done.4.refs_6_
  29.2 1.9 %iterate.1 = (f32[8,128]{1,0:T(8,128)S(1)}, f32[8,8,16,128]{3,2,1,0:T(8,128)S(1)}, f32[8,8,16,128]{3,2,1,0:T(8,128)S(1)}, f32[1,8,16,128]{3,2,1,0:T(8,128)S(1)},...) custom-call(f32[64,8,1024]{2,1,0:T(8,128)S(1)} %get-tuple-element.57, ...), custom_call_target="tpu_custom_call" | custom-call | tf_op jit(solution)/shard_map/iterate/pallas_call | solution.py:465
  31.1 0.1 collective-permute-start.5
  31.2 1.6 %collective-permute-start.24 = (f32[2,8,16,128]{3,2,1,0:T(8,128)S(1)}, f32[2,8,16,128]{3,2,1,0:T(8,128)S(1)}, u32[]{:S(2)}, u32[]{:S(2)}) collective-permute-start(f32[2,8,16,128]{3,2,1,0:T(8,128)S(1)} %get-tuple-element.82), channel_id=1, source_target_pairs={{0,8},{4,12},{8,0},{12,4},{16,24},{20,28},{24,16},{28,20},{1,9},{5... | collective-permute-start | bytes 393224 | tf_op jit(solution)/shard_map/ppermute | solution.py:610
  32.9 0.2 collective-permute-start.25
  33.1 1.6 %collective-permute-start.18 = (f32[2,8,16,128]{3,2,1,0:T(8,128)S(1)}, f32[2,8,16,128]{3,2,1,0:T(8,128)S(1)}, u32[]{:S(2)}, u32[]{:S(2)}) collective-permute-start(f32[2,8,16,128]{3,2,1,0:T(8,128)S(1)} %get-tuple-element.76), channel_id=1, source_target_pairs={{0,8},{4,12},{8,0},{12,4},{16,24},{20,28},{24,16},{28,20},{1,9},{5... | collective-permute-start | bytes 393224 | tf_op jit(solution)/shard_map/ppermute | solution.py:610
  34.7 0.1 collective-permute-start.19
  34.8 2.9 %collective-permute-done.24.refs_2_ = f32[2,8,16,128]{3,2,1,0:T(8,128)S(1)} collective-permute-done((f32[2,8,16,128]{3,2,1,0:T(8,128)S(1)}, f32[2,8,16,128]{3,2,1,0:T(8,128)S(1)}, u32[]{:S(2)}, u32[]{:S(2)}) %collective-permute-start.24) | collective-permute-done | bytes 131104 | tf_op jit(solution)/shard_map/ppermute | solution.py:610
  37.7 1.6 %collective-permute-start.12 = (f32[2,8,16,128]{3,2,1,0:T(8,128)S(1)}, f32[2,8,16,128]{3,2,1,0:T(8,128)S(1)}, u32[]{:S(2)}, u32[]{:S(2)}) collective-permute-start(f32[2,8,16,128]{3,2,1,0:T(8,128)S(1)} %get-tuple-element.70), channel_id=1, source_target_pairs={{0,8},{4,12},{8,0},{12,4},{16,24},{20,28},{24,16},{28,20},{1,9},{5... | collective-permute-start | bytes 393224 | tf_op jit(solution)/shard_map/ppermute | solution.py:610
  39.2 0.3 collective-permute-done.25.refs_3_
  39.6 1.9 %collective-permute-start.13 = (f32[2,8,16,128]{3,2,1,0:T(8,128)S(1)}, f32[2,8,16,128]{3,2,1,0:T(8,128)S(1)}, u32[]{:S(2)}, u32[]{:S(2)}) collective-permute-start(f32[2,8,16,128]{3,2,1,0:T(8,128)S(1)} %get-tuple-element.71), channel_id=1, source_target_pairs={{0,12},{4,8},{8,4},{12,0},{16,28},{20,24},{24,20},{28,16},{1,13},{... | collective-permute-start | bytes 393224 | tf_op jit(solution)/shard_map/ppermute | solution.py:610
  41.5 1.8 %collective-permute-done.18.refs_2_ = f32[2,8,16,128]{3,2,1,0:T(8,128)S(1)} collective-permute-done((f32[2,8,16,128]{3,2,1,0:T(8,128)S(1)}, f32[2,8,16,128]{3,2,1,0:T(8,128)S(1)}, u32[]{:S(2)}, u32[]{:S(2)}) %collective-permute-start.18) | collective-permute-done | bytes 131104 | tf_op jit(solution)/shard_map/ppermute | solution.py:610
  43.3 1.6 %collective-permute-start.30 = (f32[1,8,16,128]{3,2,1,0:T(8,128)S(1)}, f32[1,8,16,128]{3,2,1,0:T(8,128)S(1)}, u32[]{:S(2)}, u32[]{:S(2)}) collective-permute-start(f32[1,8,16,128]{3,2,1,0:T(8,128)S(1)} %get-tuple-element.88), channel_id=1, source_target_pairs={{0,8},{4,12},{8,0},{12,4},{16,24},{20,28},{24,16},{28,20},{1,9},{5... | collective-permute-start | bytes 196616 | tf_op jit(solution)/shard_map/ppermute | solution.py:610
  44.9 1.3 %inverse_map.1.begun = f32[32,128]{1,0:T(8,128)S(1)} custom-call(s32[2,64]{1,0:T(2,128)S(1)} %bitcast.1), custom_call_target="tpu_custom_call" | custom-call | tf_op jit(solution)/shard_map/inverse_map/pallas_call | solution.py:114
  46.2 1.7 %inverse_rest.1.map_ref = f32[32,32]{1,0:T(8,128)S(1)} custom-call(f32[32,128]{1,0:T(8,128)S(1)} %inverse_map.1.begun), custom_call_target="tpu_custom_call" | custom-call | tf_op jit(solution)/shard_map/inverse_rest/pallas_call | solution.py:129
  47.9 1.7 %cross_sums.8 = f32[2,16,16,128]{3,2,1,0:T(8,128)S(1)} custom-call(f32[32,32]{1,0:T(8,128)S(1)} %inverse_rest.1.map_ref, f32[8,8,16,128]{3,2,1,0:T(8,128)S(1)} %get-tuple-element.62.refs_0_, f32[8,8,16,128]{3,2,1,0:T(8,128)S(1)} %collective-permute-done.5.refs_1_, f32[2,8,16,128]{3,2,1,0:T(8,128)S(1)} %collective-permute-done.24.refs_2_, ...), custom_call_target="tpu_custom_call" | custom-call | tf_op jit(solution)/shard_map/cross_sums/pallas_call | solution.py:570
  49.6 2.7 %collective-permute-start.26 = (f32[2,16,16,128]{3,2,1,0:T(8,128)S(1)}, f32[2,16,16,128]{3,2,1,0:T(8,128)S(1)}, u32[]{:S(2)}, u32[]{:S(2)}) collective-permute-start(f32[2,16,16,128]{3,2,1,0:T(8,128)S(1)} %cross_sums.8), channel_id=1, source_target_pairs={{0,16},{4,20},{8,24},{12,28},{16,0},{20,4},{24,8},{28,12},{1,17},{... | collective-permute-start | bytes 786440 | tf_op jit(solution)/shard_map/ppermute | solution.py:610
  52.2 1.6 %cross_sums.7 = f32[2,16,16,128]{3,2,1,0:T(8,128)S(1)} custom-call(f32[32,32]{1,0:T(8,128)S(1)} %inverse_rest.1.map_ref, f32[8,8,16,128]{3,2,1,0:T(8,128)S(1)} %get-tuple-element.62.refs_0_, f32[8,8,16,128]{3,2,1,0:T(8,128)S(1)} %collective-permute-done.5.refs_1_, f32[2,8,16,128]{3,2,1,0:T(8,128)S(1)} %collective-permute-done.18.refs_2_, ...), custom_call_target="tpu_custom_call" | custom-call | tf_op jit(solution)/shard_map/cross_sums/pallas_call | solution.py:570
  53.9 0.4 collective-permute-start.20
  54.3 0.5 collective-permute-start.6
  54.8 1.6 %cross_sums.6 = f32[2,16,16,128]{3,2,1,0:T(8,128)S(1)} custom-call(f32[32,32]{1,0:T(8,128)S(1)} %inverse_rest.1.map_ref, f32[8,8,16,128]{3,2,1,0:T(8,128)S(1)} %get-tuple-element.62.refs_0_, f32[8,8,16,128]{3,2,1,0:T(8,128)S(1)} %collective-permute-done.5.refs_1_, f32[2,8,16,128]{3,2,1,0:T(8,128)S(1)} %collective-permute-done.12.refs_2_, ...), custom_call_target="tpu_custom_call" | custom-call | tf_op jit(solution)/shard_map/cross_sums/pallas_call | solution.py:570
  56.4 1.0 collective-permute-start.7
  57.4 2.6 %collective-permute-start.14 = (f32[2,16,16,128]{3,2,1,0:T(8,128)S(1)}, f32[2,16,16,128]{3,2,1,0:T(8,128)S(1)}, u32[]{:S(2)}, u32[]{:S(2)}) collective-permute-start(f32[2,16,16,128]{3,2,1,0:T(8,128)S(1)} %cross_sums.6), channel_id=1, source_target_pairs={{0,16},{4,20},{8,24},{12,28},{16,0},{20,4},{24,8},{28,12},{1,17},{... | collective-permute-start | bytes 786440 | tf_op jit(solution)/shard_map/ppermute | solution.py:610
  59.9 1.2 %cross_sums.9 = f32[1,16,16,128]{3,2,1,0:T(8,128)S(1)} custom-call(f32[32,32]{1,0:T(8,128)S(1)} %inverse_rest.1.map_ref, f32[8,8,16,128]{3,2,1,0:T(8,128)S(1)} %get-tuple-element.62.refs_0_, f32[8,8,16,128]{3,2,1,0:T(8,128)S(1)} %collective-permute-done.5.refs_1_, f32[1,8,16,128]{3,2,1,0:T(8,128)S(1)} %collective-permute-done.30.refs_2_, ...), custom_call_target="tpu_custom_call" | custom-call | tf_op jit(solution)/shard_map/cross_sums/pallas_call | solution.py:570
  61.2 4.8 %collective-permute-done.6.refs_2_ = f32[1,8,16,128]{3,2,1,0:T(8,128)S(1)} collective-permute-done((f32[1,8,16,128]{3,2,1,0:T(8,128)S(1)}, f32[1,8,16,128]{3,2,1,0:T(8,128)S(1)}, u32[]{:S(2)}, u32[]{:S(2)}) %collective-permute-start.6) | collective-permute-done | bytes 65568 | tf_op jit(solution)/shard_map/ppermute | solution.py:610
  66.0 3.8 %collective-permute-start.32 = (f32[1,16,16,128]{3,2,1,0:T(8,128)S(1)}, f32[1,16,16,128]{3,2,1,0:T(8,128)S(1)}, u32[]{:S(2)}, u32[]{:S(2)}) collective-permute-start(f32[1,16,16,128]{3,2,1,0:T(8,128)S(1)} %cross_sums.9), channel_id=1, source_target_pairs={{0,16},{4,20},{8,24},{12,28},{16,0},{20,4},{24,8},{28,12},{1,17},{... | collective-permute-start | bytes 393224 | tf_op jit(solution)/shard_map/ppermute | solution.py:610
  69.8 1.2 %cross_sums.5 = f32[1,16,16,128]{3,2,1,0:T(8,128)S(1)} custom-call(f32[32,32]{1,0:T(8,128)S(1)} %inverse_rest.1.map_ref, f32[8,8,16,128]{3,2,1,0:T(8,128)S(1)} %get-tuple-element.62.refs_0_, f32[8,8,16,128]{3,2,1,0:T(8,128)S(1)} %collective-permute-done.5.refs_1_, f32[1,8,16,128]{3,2,1,0:T(8,128)S(1)} %collective-permute-done.6.refs_2_, ...), custom_call_target="tpu_custom_call" | custom-call | tf_op jit(solution)/shard_map/cross_sums/pallas_call | solution.py:570
  71.0 0.4 collective-permute-start.8
  71.4 24.9 %collective-permute-done.32.refs_4_ = f32[1,16,16,128]{3,2,1,0:T(8,128)S(1)} collective-permute-done((f32[1,16,16,128]{3,2,1,0:T(8,128)S(1)}, f32[1,16,16,128]{3,2,1,0:T(8,128)S(1)}, u32[]{:S(2)}, u32[]{:S(2)}) %collective-permute-start.32) | collective-permute-done | bytes 131104 | tf_op jit(solution)/shard_map/ppermute | solution.py:610
  96.3 1.2 %own_sums.9 = (f32[1,4,16,128]{3,2,1,0:T(8,128)S(1)}, f32[1,4,16,128]{3,2,1,0:T(8,128)S(1)}, f32[1,4,16,128]{3,2,1,0:T(8,128)S(1)}, f32[1,4,16,128]{3,2,1,0:T(8,128)S(1)}) custom-call(f32[32,32]{1,0:T(8,128)S(1)} %inverse_rest.1.map_ref, f32[8,8,16,128]{3,2,1,0:T(8,128)S(1)} %get-tuple-element.62.refs_0_, ...), custom_call_target="tpu_custom_call" | custom-call | tf_op jit(solution)/shard_map/own_sums/pallas_call | solution.py:570
  97.5 0.1 collective-permute-start.33
  97.6 1.1 collective-permute-done.8.refs_4_
  98.7 1.2 %own_sums.5 = (f32[1,4,16,128]{3,2,1,0:T(8,128)S(1)}, f32[1,4,16,128]{3,2,1,0:T(8,128)S(1)}, f32[1,4,16,128]{3,2,1,0:T(8,128)S(1)}, f32[1,4,16,128]{3,2,1,0:T(8,128)S(1)}) custom-call(f32[32,32]{1,0:T(8,128)S(1)} %inverse_rest.1.map_ref, f32[8,8,16,128]{3,2,1,0:T(8,128)S(1)} %get-tuple-element.62.refs_0_, ...), custom_call_target="tpu_custom_call" | custom-call | tf_op jit(solution)/shard_map/own_sums/pallas_call | solution.py:570
  99.9 1.1 collective-permute-start.35
  101.0 1.1 collective-permute-start.10
  102.1 1.4 %collective-permute-start.11 = (f32[1,4,16,128]{3,2,1,0:T(8,128)S(1)}, f32[1,4,16,128]{3,2,1,0:T(8,128)S(1)}, u32[]{:S(2)}, u32[]{:S(2)}) collective-permute-start(f32[1,4,16,128]{3,2,1,0:T(8,128)S(1)} %get-tuple-element.69), channel_id=1, source_target_pairs={{0,12},{4,8},{8,4},{12,0},{16,28},{20,24},{24,20},{28,16},{1,13},{... | collective-permute-start | bytes 98312 | tf_op jit(solution)/shard_map/ppermute | solution.py:610
  103.5 1.6 %own_sums.8 = (f32[2,4,16,128]{3,2,1,0:T(8,128)S(1)}, f32[2,4,16,128]{3,2,1,0:T(8,128)S(1)}, f32[2,4,16,128]{3,2,1,0:T(8,128)S(1)}, f32[2,4,16,128]{3,2,1,0:T(8,128)S(1)}) custom-call(f32[32,32]{1,0:T(8,128)S(1)} %inverse_rest.1.map_ref, f32[8,8,16,128]{3,2,1,0:T(8,128)S(1)} %get-tuple-element.62.refs_0_, ...), custom_call_target="tpu_custom_call" | custom-call | tf_op jit(solution)/shard_map/own_sums/pallas_call | solution.py:570
  105.1 1.6 %own_sums.7 = (f32[2,4,16,128]{3,2,1,0:T(8,128)S(1)}, f32[2,4,16,128]{3,2,1,0:T(8,128)S(1)}, f32[2,4,16,128]{3,2,1,0:T(8,128)S(1)}, f32[2,4,16,128]{3,2,1,0:T(8,128)S(1)}) custom-call(f32[32,32]{1,0:T(8,128)S(1)} %inverse_rest.1.map_ref, f32[8,8,16,128]{3,2,1,0:T(8,128)S(1)} %get-tuple-element.62.refs_0_, ...), custom_call_target="tpu_custom_call" | custom-call | tf_op jit(solution)/shard_map/own_sums/pallas_call | solution.py:570
  106.7 0.1 collective-permute-start.27
  106.8 0.7 collective-permute-start.28
  107.5 1.1 collective-permute-start.29
  108.6 0.4 collective-permute-start.21
  109.0 0.1 collective-permute-start.9
  109.1 1.6 %own_sums.6 = (f32[2,4,16,128]{3,2,1,0:T(8,128)S(1)}, f32[2,4,16,128]{3,2,1,0:T(8,128)S(1)}, f32[2,4,16,128]{3,2,1,0:T(8,128)S(1)}, f32[2,4,16,128]{3,2,1,0:T(8,128)S(1)}) custom-call(f32[32,32]{1,0:T(8,128)S(1)} %inverse_rest.1.map_ref, f32[8,8,16,128]{3,2,1,0:T(8,128)S(1)} %get-tuple-element.62.refs_0_, ...), custom_call_target="tpu_custom_call" | custom-call | tf_op jit(solution)/shard_map/own_sums/pallas_call | solution.py:570
  110.7 0.7 collective-permute-start.22
  111.4 1.1 collective-permute-start.23
  112.5 0.4 collective-permute-start.15
  112.9 0.6 collective-permute-start.16
  113.5 0.8 collective-permute-start.17
  114.4 2.1 %combine.1 = f32[8,64,1024]{2,1,0:T(8,128)} custom-call(f32[64,8,1024]{2,1,0:T(8,128)S(1)} %get-tuple-element.57.refs_0_.r_ref, f32[64,8,1024]{2,1,0:T(8,128)S(1)} %get-tuple-element.58.refs_1_.v_ref, f32[64,8,1024]{2,1,0:T(8,128)S(1)} %get-tuple-element.59.refs_2_.u_ref, f32[8,128]{1,0:T(8,128)S(1)} %get-tuple-element.61.weights_ref), custom_call_target="tpu_custom_call" | custom-call | tf_op jit(solution)/shard_map/combine/pallas_call | solution.py:502
  116.5 2.0 %collective-permute-done.16.refs_6_ = f32[2,4,16,128]{3,2,1,0:T(8,128)S(1)} collective-permute-done((f32[2,4,16,128]{3,2,1,0:T(8,128)S(1)}, f32[2,4,16,128]{3,2,1,0:T(8,128)S(1)}, u32[]{:S(2)}, u32[]{:S(2)}) %collective-permute-start.16) | collective-permute-done | bytes 65568 | tf_op jit(solution)/shard_map/ppermute | solution.py:610
  118.6 0.2 collective-permute-done.17.refs_7_
  118.7 1.1 assemble.1
  (28 shorter events, 0.1 us)
Async XLA Ops:
  2.9 16.7 %collective-permute-start = (f32[6,8,1024]{2,1,0:T(8,128)S(1)}, f32[6,8,1024]{2,1,0:T(8,128)S(1)}, u32[]{:S(2)}, u32[]{:S(2)}) collective-permute-start(f32[6,8,1024]{2,1,0:T(8,128)S(1)} %get-tuple-element.48), channel_id=1, source_target_pairs={{0,1},{1,0},{2,3},{3,2},{4,5},{5,4},{6,7},{7,6},{8,9},{9,8},{10,11... | collective-permute-start | bytes 589832 | tf_op jit(solution)/shard_map/ppermute | solution.py:631
  5.9 13.7 %collective-permute-start.1 = (f32[6,8,1024]{2,1,0:T(8,128)S(1)}, f32[6,8,1024]{2,1,0:T(8,128)S(1)}, u32[]{:S(2)}, u32[]{:S(2)}) collective-permute-start(f32[6,8,1024]{2,1,0:T(8,128)S(1)} %get-tuple-element.49), channel_id=1, source_target_pairs={{1,2},{2,1},{5,6},{6,5},{9,10},{10,9},{13,14},{14,13},{17,18},{18,... | collective-permute-start | bytes 589832 | tf_op jit(solution)/shard_map/ppermute | solution.py:631
  20.5 5.8 %collective-permute-start.2 = (f32[8,128]{1,0:T(8,128)S(1)}, f32[8,128]{1,0:T(8,128)S(1)}, u32[]{:S(2)}, u32[]{:S(2)}) collective-permute-start(f32[8,128]{1,0:T(8,128)S(1)} %get-tuple-element.60.refs_3_), channel_id=1, source_target_pairs={{0,1},{1,0},{2,3},{3,2},{4,5},{5,4},{6,7},{7,6},{8,9},{9,8},{10,11... | collective-permute-start | bytes 12296 | tf_op jit(solution)/shard_map/ppermute | solution.py:610
  24.7 3.6 %collective-permute-start.3 = (f32[8,128]{1,0:T(8,128)S(1)}, f32[8,128]{1,0:T(8,128)S(1)}, u32[]{:S(2)}, u32[]{:S(2)}) collective-permute-start(f32[8,128]{1,0:T(8,128)S(1)} %get-tuple-element.60.refs_3_), channel_id=1, source_target_pairs={{0,2},{1,3},{2,0},{3,1},{4,6},{5,7},{6,4},{7,5},{8,10},{9,11},{10,... | collective-permute-start | bytes 12296 | tf_op jit(solution)/shard_map/ppermute | solution.py:610
  24.7 4.5 %collective-permute-start.4 = (f32[8,128]{1,0:T(8,128)S(1)}, f32[8,128]{1,0:T(8,128)S(1)}, u32[]{:S(2)}, u32[]{:S(2)}) collective-permute-start(f32[8,128]{1,0:T(8,128)S(1)} %get-tuple-element.60.refs_3_), channel_id=1, source_target_pairs={{0,3},{1,2},{2,1},{3,0},{4,7},{5,6},{6,5},{7,4},{8,11},{9,10},{10,... | collective-permute-start | bytes 12296 | tf_op jit(solution)/shard_map/ppermute | solution.py:610
  29.2 15.7 %copy-start = (s32[64,2]{0,1:T(2,128)S(1)}, s32[64,2]{0,1:T(2,128)}, u32[]{:S(2)}) copy-start(s32[64,2]{0,1:T(2,128)} %param.7) | copy-start | bytes 1540
  31.1 13.7 %collective-permute-start.5 = (f32[8,8,16,128]{3,2,1,0:T(8,128)S(1)}, f32[8,8,16,128]{3,2,1,0:T(8,128)S(1)}, u32[]{:S(2)}, u32[]{:S(2)}) collective-permute-start(f32[8,8,16,128]{3,2,1,0:T(8,128)S(1)} %get-tuple-element.63), channel_id=1, source_target_pairs={{0,4},{4,0},{8,12},{12,8},{16,20},{20,16},{24,28},{28,24},{1,5},{5... | collective-permute-start | bytes 1572872 | tf_op jit(solution)/shard_map/ppermute | solution.py:610
  31.2 6.4 %collective-permute-start.24 = (f32[2,8,16,128]{3,2,1,0:T(8,128)S(1)}, f32[2,8,16,128]{3,2,1,0:T(8,128)S(1)}, u32[]{:S(2)}, u32[]{:S(2)}) collective-permute-start(f32[2,8,16,128]{3,2,1,0:T(8,128)S(1)} %get-tuple-element.82), channel_id=1, source_target_pairs={{0,8},{4,12},{8,0},{12,4},{16,24},{20,28},{24,16},{28,20},{1,9},{5... | collective-permute-start | bytes 393224 | tf_op jit(solution)/shard_map/ppermute | solution.py:610
  32.9 6.7 %collective-permute-start.25 = (f32[2,8,16,128]{3,2,1,0:T(8,128)S(1)}, f32[2,8,16,128]{3,2,1,0:T(8,128)S(1)}, u32[]{:S(2)}, u32[]{:S(2)}) collective-permute-start(f32[2,8,16,128]{3,2,1,0:T(8,128)S(1)} %get-tuple-element.83), channel_id=1, source_target_pairs={{0,12},{4,8},{8,4},{12,0},{16,28},{20,24},{24,20},{28,16},{1,13},{... | collective-permute-start | bytes 393224 | tf_op jit(solution)/shard_map/ppermute | solution.py:610
  33.1 10.2 %collective-permute-start.18 = (f32[2,8,16,128]{3,2,1,0:T(8,128)S(1)}, f32[2,8,16,128]{3,2,1,0:T(8,128)S(1)}, u32[]{:S(2)}, u32[]{:S(2)}) collective-permute-start(f32[2,8,16,128]{3,2,1,0:T(8,128)S(1)} %get-tuple-element.76), channel_id=1, source_target_pairs={{0,8},{4,12},{8,0},{12,4},{16,24},{20,28},{24,16},{28,20},{1,9},{5... | collective-permute-start | bytes 393224 | tf_op jit(solution)/shard_map/ppermute | solution.py:610
  34.7 14.9 %collective-permute-start.19 = (f32[2,8,16,128]{3,2,1,0:T(8,128)S(1)}, f32[2,8,16,128]{3,2,1,0:T(8,128)S(1)}, u32[]{:S(2)}, u32[]{:S(2)}) collective-permute-start(f32[2,8,16,128]{3,2,1,0:T(8,128)S(1)} %get-tuple-element.77), channel_id=1, source_target_pairs={{0,12},{4,8},{8,4},{12,0},{16,28},{20,24},{24,20},{28,16},{1,13},{... | collective-permute-start | bytes 393224 | tf_op jit(solution)/shard_map/ppermute | solution.py:610
  37.7 16.2 %collective-permute-start.12 = (f32[2,8,16,128]{3,2,1,0:T(8,128)S(1)}, f32[2,8,16,128]{3,2,1,0:T(8,128)S(1)}, u32[]{:S(2)}, u32[]{:S(2)}) collective-permute-start(f32[2,8,16,128]{3,2,1,0:T(8,128)S(1)} %get-tuple-element.70), channel_id=1, source_target_pairs={{0,8},{4,12},{8,0},{12,4},{16,24},{20,28},{24,16},{28,20},{1,9},{5... | collective-permute-start | bytes 393224 | tf_op jit(solution)/shard_map/ppermute | solution.py:610
  39.6 14.7 %collective-permute-start.13 = (f32[2,8,16,128]{3,2,1,0:T(8,128)S(1)}, f32[2,8,16,128]{3,2,1,0:T(8,128)S(1)}, u32[]{:S(2)}, u32[]{:S(2)}) collective-permute-start(f32[2,8,16,128]{3,2,1,0:T(8,128)S(1)} %get-tuple-element.71), channel_id=1, source_target_pairs={{0,12},{4,8},{8,4},{12,0},{16,28},{20,24},{24,20},{28,16},{1,13},{... | collective-permute-start | bytes 393224 | tf_op jit(solution)/shard_map/ppermute | solution.py:610
  43.3 13.1 %collective-permute-start.30 = (f32[1,8,16,128]{3,2,1,0:T(8,128)S(1)}, f32[1,8,16,128]{3,2,1,0:T(8,128)S(1)}, u32[]{:S(2)}, u32[]{:S(2)}) collective-permute-start(f32[1,8,16,128]{3,2,1,0:T(8,128)S(1)} %get-tuple-element.88), channel_id=1, source_target_pairs={{0,8},{4,12},{8,0},{12,4},{16,24},{20,28},{24,16},{28,20},{1,9},{5... | collective-permute-start | bytes 196616 | tf_op jit(solution)/shard_map/ppermute | solution.py:610
  44.9 12.5 %collective-permute-start.31 = (f32[1,8,16,128]{3,2,1,0:T(8,128)S(1)}, f32[1,8,16,128]{3,2,1,0:T(8,128)S(1)}, u32[]{:S(2)}, u32[]{:S(2)}) collective-permute-start(f32[1,8,16,128]{3,2,1,0:T(8,128)S(1)} %get-tuple-element.89), channel_id=1, source_target_pairs={{0,12},{4,8},{8,4},{12,0},{16,28},{20,24},{24,20},{28,16},{1,13},{... | collective-permute-start | bytes 196616 | tf_op jit(solution)/shard_map/ppermute | solution.py:610
  49.6 51.4 %collective-permute-start.26 = (f32[2,16,16,128]{3,2,1,0:T(8,128)S(1)}, f32[2,16,16,128]{3,2,1,0:T(8,128)S(1)}, u32[]{:S(2)}, u32[]{:S(2)}) collective-permute-start(f32[2,16,16,128]{3,2,1,0:T(8,128)S(1)} %cross_sums.8), channel_id=1, source_target_pairs={{0,16},{4,20},{8,24},{12,28},{16,0},{20,4},{24,8},{28,12},{1,17},{... | collective-permute-start | bytes 786440 | tf_op jit(solution)/shard_map/ppermute | solution.py:610
  53.9 48.2 %collective-permute-start.20 = (f32[2,16,16,128]{3,2,1,0:T(8,128)S(1)}, f32[2,16,16,128]{3,2,1,0:T(8,128)S(1)}, u32[]{:S(2)}, u32[]{:S(2)}) collective-permute-start(f32[2,16,16,128]{3,2,1,0:T(8,128)S(1)} %cross_sums.7), channel_id=1, source_target_pairs={{0,16},{4,20},{8,24},{12,28},{16,0},{20,4},{24,8},{28,12},{1,17},{... | collective-permute-start | bytes 786440 | tf_op jit(solution)/shard_map/ppermute | solution.py:610
  54.3 11.7 %collective-permute-start.6 = (f32[1,8,16,128]{3,2,1,0:T(8,128)S(1)}, f32[1,8,16,128]{3,2,1,0:T(8,128)S(1)}, u32[]{:S(2)}, u32[]{:S(2)}) collective-permute-start(f32[1,8,16,128]{3,2,1,0:T(8,128)S(1)} %get-tuple-element.64), channel_id=1, source_target_pairs={{0,8},{4,12},{8,0},{12,4},{16,24},{20,28},{24,16},{28,20},{1,9},{5... | collective-permute-start | bytes 196616 | tf_op jit(solution)/shard_map/ppermute | solution.py:610
  56.4 13.4 %collective-permute-start.7 = (f32[1,8,16,128]{3,2,1,0:T(8,128)S(1)}, f32[1,8,16,128]{3,2,1,0:T(8,128)S(1)}, u32[]{:S(2)}, u32[]{:S(2)}) collective-permute-start(f32[1,8,16,128]{3,2,1,0:T(8,128)S(1)} %get-tuple-element.65), channel_id=1, source_target_pairs={{0,12},{4,8},{8,4},{12,0},{16,28},{20,24},{24,20},{28,16},{1,13},{... | collective-permute-start | bytes 196616 | tf_op jit(solution)/shard_map/ppermute | solution.py:610
  57.4 51.6 %collective-permute-start.14 = (f32[2,16,16,128]{3,2,1,0:T(8,128)S(1)}, f32[2,16,16,128]{3,2,1,0:T(8,128)S(1)}, u32[]{:S(2)}, u32[]{:S(2)}) collective-permute-start(f32[2,16,16,128]{3,2,1,0:T(8,128)S(1)} %cross_sums.6), channel_id=1, source_target_pairs={{0,16},{4,20},{8,24},{12,28},{16,0},{20,4},{24,8},{28,12},{1,17},{... | collective-permute-start | bytes 786440 | tf_op jit(solution)/shard_map/ppermute | solution.py:610
  66.0 30.3 %collective-permute-start.32 = (f32[1,16,16,128]{3,2,1,0:T(8,128)S(1)}, f32[1,16,16,128]{3,2,1,0:T(8,128)S(1)}, u32[]{:S(2)}, u32[]{:S(2)}) collective-permute-start(f32[1,16,16,128]{3,2,1,0:T(8,128)S(1)} %cross_sums.9), channel_id=1, source_target_pairs={{0,16},{4,20},{8,24},{12,28},{16,0},{20,4},{24,8},{28,12},{1,17},{... | collective-permute-start | bytes 393224 | tf_op jit(solution)/shard_map/ppermute | solution.py:610
  71.0 27.7 %collective-permute-start.8 = (f32[1,16,16,128]{3,2,1,0:T(8,128)S(1)}, f32[1,16,16,128]{3,2,1,0:T(8,128)S(1)}, u32[]{:S(2)}, u32[]{:S(2)}) collective-permute-start(f32[1,16,16,128]{3,2,1,0:T(8,128)S(1)} %cross_sums.5), channel_id=1, source_target_pairs={{0,16},{4,20},{8,24},{12,28},{16,0},{20,4},{24,8},{28,12},{1,17},{... | collective-permute-start | bytes 393224 | tf_op jit(solution)/shard_map/ppermute | solution.py:610
  97.5 2.4 %collective-permute-start.33 = (f32[1,4,16,128]{3,2,1,0:T(8,128)S(1)}, f32[1,4,16,128]{3,2,1,0:T(8,128)S(1)}, u32[]{:S(2)}, u32[]{:S(2)}) collective-permute-start(f32[1,4,16,128]{3,2,1,0:T(8,128)S(1)} %get-tuple-element.91), channel_id=1, source_target_pairs={{0,4},{4,0},{8,12},{12,8},{16,20},{20,16},{24,28},{28,24},{1,5},{5... | collective-permute-start | bytes 98312 | tf_op jit(solution)/shard_map/ppermute | solution.py:610
  98.7 8.0 %collective-permute-start.34 = (f32[1,4,16,128]{3,2,1,0:T(8,128)S(1)}, f32[1,4,16,128]{3,2,1,0:T(8,128)S(1)}, u32[]{:S(2)}, u32[]{:S(2)}) collective-permute-start(f32[1,4,16,128]{3,2,1,0:T(8,128)S(1)} %get-tuple-element.92), channel_id=1, source_target_pairs={{0,8},{4,12},{8,0},{12,4},{16,24},{20,28},{24,16},{28,20},{1,9},{5... | collective-permute-start | bytes 98312 | tf_op jit(solution)/shard_map/ppermute | solution.py:610
  99.9 6.9 %collective-permute-start.35 = (f32[1,4,16,128]{3,2,1,0:T(8,128)S(1)}, f32[1,4,16,128]{3,2,1,0:T(8,128)S(1)}, u32[]{:S(2)}, u32[]{:S(2)}) collective-permute-start(f32[1,4,16,128]{3,2,1,0:T(8,128)S(1)} %get-tuple-element.93), channel_id=1, source_target_pairs={{0,12},{4,8},{8,4},{12,0},{16,28},{20,24},{24,20},{28,16},{1,13},{... | collective-permute-start | bytes 98312 | tf_op jit(solution)/shard_map/ppermute | solution.py:610
  101.0 6.5 %collective-permute-start.10 = (f32[1,4,16,128]{3,2,1,0:T(8,128)S(1)}, f32[1,4,16,128]{3,2,1,0:T(8,128)S(1)}, u32[]{:S(2)}, u32[]{:S(2)}) collective-permute-start(f32[1,4,16,128]{3,2,1,0:T(8,128)S(1)} %get-tuple-element.68), channel_id=1, source_target_pairs={{0,8},{4,12},{8,0},{12,4},{16,24},{20,28},{24,16},{28,20},{1,9},{5... | collective-permute-start | bytes 98312 | tf_op jit(solution)/shard_map/ppermute | solution.py:610
  102.1 6.5 %collective-permute-start.11 = (f32[1,4,16,128]{3,2,1,0:T(8,128)S(1)}, f32[1,4,16,128]{3,2,1,0:T(8,128)S(1)}, u32[]{:S(2)}, u32[]{:S(2)}) collective-permute-start(f32[1,4,16,128]{3,2,1,0:T(8,128)S(1)} %get-tuple-element.69), channel_id=1, source_target_pairs={{0,12},{4,8},{8,4},{12,0},{16,28},{20,24},{24,20},{28,16},{1,13},{... | collective-permute-start | bytes 98312 | tf_op jit(solution)/shard_map/ppermute | solution.py:610
  106.7 4.7 %collective-permute-start.27 = (f32[2,4,16,128]{3,2,1,0:T(8,128)S(1)}, f32[2,4,16,128]{3,2,1,0:T(8,128)S(1)}, u32[]{:S(2)}, u32[]{:S(2)}) collective-permute-start(f32[2,4,16,128]{3,2,1,0:T(8,128)S(1)} %get-tuple-element.85), channel_id=1, source_target_pairs={{0,4},{4,0},{8,12},{12,8},{16,20},{20,16},{24,28},{28,24},{1,5},{5... | collective-permute-start | bytes 196616 | tf_op jit(solution)/shard_map/ppermute | solution.py:610
  106.8 5.7 %collective-permute-start.28 = (f32[2,4,16,128]{3,2,1,0:T(8,128)S(1)}, f32[2,4,16,128]{3,2,1,0:T(8,128)S(1)}, u32[]{:S(2)}, u32[]{:S(2)}) collective-permute-start(f32[2,4,16,128]{3,2,1,0:T(8,128)S(1)} %get-tuple-element.86), channel_id=1, source_target_pairs={{0,8},{4,12},{8,0},{12,4},{16,24},{20,28},{24,16},{28,20},{1,9},{5... | collective-permute-start | bytes 196616 | tf_op jit(solution)/shard_map/ppermute | solution.py:610
  107.5 5.4 %collective-permute-start.29 = (f32[2,4,16,128]{3,2,1,0:T(8,128)S(1)}, f32[2,4,16,128]{3,2,1,0:T(8,128)S(1)}, u32[]{:S(2)}, u32[]{:S(2)}) collective-permute-start(f32[2,4,16,128]{3,2,1,0:T(8,128)S(1)} %get-tuple-element.87), channel_id=1, source_target_pairs={{0,12},{4,8},{8,4},{12,0},{16,28},{20,24},{24,20},{28,16},{1,13},{... | collective-permute-start | bytes 196616 | tf_op jit(solution)/shard_map/ppermute | solution.py:610
  108.6 4.9 %collective-permute-start.21 = (f32[2,4,16,128]{3,2,1,0:T(8,128)S(1)}, f32[2,4,16,128]{3,2,1,0:T(8,128)S(1)}, u32[]{:S(2)}, u32[]{:S(2)}) collective-permute-start(f32[2,4,16,128]{3,2,1,0:T(8,128)S(1)} %get-tuple-element.79), channel_id=1, source_target_pairs={{0,4},{4,0},{8,12},{12,8},{16,20},{20,16},{24,28},{28,24},{1,5},{5... | collective-permute-start | bytes 196616 | tf_op jit(solution)/shard_map/ppermute | solution.py:610
  109.0 1.7 %collective-permute-start.9 = (f32[1,4,16,128]{3,2,1,0:T(8,128)S(1)}, f32[1,4,16,128]{3,2,1,0:T(8,128)S(1)}, u32[]{:S(2)}, u32[]{:S(2)}) collective-permute-start(f32[1,4,16,128]{3,2,1,0:T(8,128)S(1)} %get-tuple-element.67), channel_id=1, source_target_pairs={{0,4},{4,0},{8,12},{12,8},{16,20},{20,16},{24,28},{28,24},{1,5},{5... | collective-permute-start | bytes 98312 | tf_op jit(solution)/shard_map/ppermute | solution.py:610
  110.7 5.8 %collective-permute-start.22 = (f32[2,4,16,128]{3,2,1,0:T(8,128)S(1)}, f32[2,4,16,128]{3,2,1,0:T(8,128)S(1)}, u32[]{:S(2)}, u32[]{:S(2)}) collective-permute-start(f32[2,4,16,128]{3,2,1,0:T(8,128)S(1)} %get-tuple-element.80), channel_id=1, source_target_pairs={{0,8},{4,12},{8,0},{12,4},{16,24},{20,28},{24,16},{28,20},{1,9},{5... | collective-permute-start | bytes 196616 | tf_op jit(solution)/shard_map/ppermute | solution.py:610
  111.4 5.1 %collective-permute-start.23 = (f32[2,4,16,128]{3,2,1,0:T(8,128)S(1)}, f32[2,4,16,128]{3,2,1,0:T(8,128)S(1)}, u32[]{:S(2)}, u32[]{:S(2)}) collective-permute-start(f32[2,4,16,128]{3,2,1,0:T(8,128)S(1)} %get-tuple-element.81), channel_id=1, source_target_pairs={{0,12},{4,8},{8,4},{12,0},{16,28},{20,24},{24,20},{28,16},{1,13},{... | collective-permute-start | bytes 196616 | tf_op jit(solution)/shard_map/ppermute | solution.py:610
  112.5 4.0 %collective-permute-start.15 = (f32[2,4,16,128]{3,2,1,0:T(8,128)S(1)}, f32[2,4,16,128]{3,2,1,0:T(8,128)S(1)}, u32[]{:S(2)}, u32[]{:S(2)}) collective-permute-start(f32[2,4,16,128]{3,2,1,0:T(8,128)S(1)} %get-tuple-element.73), channel_id=1, source_target_pairs={{0,4},{4,0},{8,12},{12,8},{16,20},{20,16},{24,28},{28,24},{1,5},{5... | collective-permute-start | bytes 196616 | tf_op jit(solution)/shard_map/ppermute | solution.py:610
  112.9 5.6 %collective-permute-start.16 = (f32[2,4,16,128]{3,2,1,0:T(8,128)S(1)}, f32[2,4,16,128]{3,2,1,0:T(8,128)S(1)}, u32[]{:S(2)}, u32[]{:S(2)}) collective-permute-start(f32[2,4,16,128]{3,2,1,0:T(8,128)S(1)} %get-tuple-element.74), channel_id=1, source_target_pairs={{0,8},{4,12},{8,0},{12,4},{16,24},{20,28},{24,16},{28,20},{1,9},{5... | collective-permute-start | bytes 196616 | tf_op jit(solution)/shard_map/ppermute | solution.py:610
  113.5 5.2 %collective-permute-start.17 = (f32[2,4,16,128]{3,2,1,0:T(8,128)S(1)}, f32[2,4,16,128]{3,2,1,0:T(8,128)S(1)}, u32[]{:S(2)}, u32[]{:S(2)}) collective-permute-start(f32[2,4,16,128]{3,2,1,0:T(8,128)S(1)} %get-tuple-element.75), channel_id=1, source_target_pairs={{0,12},{4,8},{8,4},{12,0},{16,28},{20,24},{24,20},{28,16},{1,13},{... | collective-permute-start | bytes 196616 | tf_op jit(solution)/shard_map/ppermute | solution.py:610

commit v4 on v3

--- a/solution.py
+++ b/solution.py
@@ -9,7 +9,7 @@
 SLICES = (1, 2, 2, 2, 1)
 CHUNKS = len(SLICES)
 PAD = 8
-EARLY = 12
+EARLY = 18
 damping = 0.1
 TINY = 1e-6
 F32 = jnp.float32
@@ -151,12 +151,10 @@
 
         def send(down, up):
             for k in range(count):
-                c, y = (cb[k], yb[k])
-                r = partial_rhs(c, xb[k], y)
+                c, x, y = (jnp.where(row < 4, t[k], b[k]) for t, b in ((ct, cb), (xt, xb), (yt, yb)))
+                r = partial_rhs(c, x, y)
                 for i, x in enumerate((r[6:7], r[7:8], y[7:8], c[6:7], c[7:8])):
                     down[i, k : k + 1, :] = x
-                c = ct[k]
-                r = partial_rhs(c, xt[k], yt[k])
                 for i in range(3):
                     up[i, k : k + 1, :] = r[i : i + 1]
                     up[3 + i, k : k + 1, :] = c[i : i + 1]
@@ -539,7 +537,7 @@
             for (b, a), x in zip(spots, acc):
                 out[b, d, a : a + 8, :] = x
 
-        per = min(4 if len(spots) <= 2 else 2, share)
+        per = min(4, share)
 
         def step_of(first, out, begin):
             def step(i, _):

time: 120 us -> 119 us (level)
  no operation moved by 1% of the time
where the time goes in v4:
time: 119 us
  waiting for transfers between devices  41.2 us (35%)
  starting transfers between devices  39.1 us (33%)
  Pallas kernels  38.1 us (32%)
    ppermute x34, waiting for transfers between devices, exchange(): return lax.ppermute(x, axis, [(i, i ^ mask) for i in range(size)])  41.2 us
    ppermute x34, starting transfers between devices, exchange(): return lax.ppermute(x, axis, [(i, i ^ mask) for i in range(size)])  35.4 us
    pallas_call x10, Pallas kernels, half_sums(): pl.pallas_call(body, in_specs=[SMEM] + [VMEM] * len(args), out_specs=[VME...  14.2 us
    pallas_call x1, Pallas kernels, interior(): pl.pallas_call(body, in_specs=[ANY] * 3, out_specs=[VMEM] * 7, out_shape=...  13.2 us
    ppermute x2, starting transfers between devices, on_device(): lax.ppermute(x, 'strip', [p for i in range(at, strips - 1, 2) for p in ((...  3.69 us
  transfers between devices with their start and end apart: 36, of which 10 were waited for; matrix products, arithmetic and copies ran while one was open for 0% of the time, Pallas kernels for 27%

profile of v4, /device:TPU:0, one launch (start us, length us, event | category | flops | bytes accessed | tf_op | source)
XLA Modules:
  0.0 119.2 jit_solution(18247722131761802860)
XLA Ops:
  0.6 1.7 %edges.1 = (f32[6,8,1024]{2,1,0:T(8,128)S(1)}, f32[6,8,1024]{2,1,0:T(8,128)S(1)}) custom-call(f32[8,64,1024]{2,1,0:T(8,128)} %c_hbm.1, f32[8,64,1024]{2,1,0:T(8,128)} %x_hbm.1, f32[8,64,1024]{2,1,0:T(8,128)} %y_hbm.1, f32[8,64,1024]{2,1,0:T(8,128)} %c_hbm.1, f32[8,64,1024]{2,1,0:T(8,128)} %x_hbm.1, f32[8,64,1024]{2,1,0:T(8,128)} %y_hbm.1), custom_call_target="tpu_custom_call" | custom-call | tf_op jit(solution)/shard_map/edges/pallas_call | solution.py:175
  2.3 3.0 %collective-permute-start = (f32[6,8,1024]{2,1,0:T(8,128)S(1)}, f32[6,8,1024]{2,1,0:T(8,128)S(1)}, u32[]{:S(2)}, u32[]{:S(2)}) collective-permute-start(f32[6,8,1024]{2,1,0:T(8,128)S(1)} %get-tuple-element.48), channel_id=1, source_target_pairs={{0,1},{1,0},{2,3},{3,2},{4,5},{5,4},{6,7},{7,6},{8,9},{9,8},{10,11... | collective-permute-start | bytes 589832 | tf_op jit(solution)/shard_map/ppermute | solution.py:629
  5.3 0.7 collective-permute-start.1
  6.0 13.2 %interior.1 = (f32[64,8,1024]{2,1,0:T(8,128)S(1)}, f32[64,8,1024]{2,1,0:T(8,128)S(1)}, f32[64,8,1024]{2,1,0:T(8,128)S(1)}, f32[64,8,1024]{2,1,0:T(8,128)S(1)}, f...) custom-call(f32[8,64,1024]{2,1,0:T(8,128)} %c_hbm.1, f32[8,64,1024]{2,1,0:T(8,128)} %x_hbm.1, ...), custom_call_target="tpu_custom_call" | custom-call | tf_op jit(solution)/shard_map/interior/pallas_call | solution.py:300
  19.2 0.0 collective-permute-done.got_first
  19.2 0.0 collective-permute-done.1.got_second
  19.2 0.9 join.1
  20.1 4.2 %collective-permute-start.2 = (f32[8,128]{1,0:T(8,128)S(1)}, f32[8,128]{1,0:T(8,128)S(1)}, u32[]{:S(2)}, u32[]{:S(2)}) collective-permute-start(f32[8,128]{1,0:T(8,128)S(1)} %get-tuple-element.60.refs_3_), channel_id=1, source_target_pairs={{0,1},{1,0},{2,3},{3,2},{4,5},{5,4},{6,7},{7,6},{8,9},{9,8},{10,11... | collective-permute-start | bytes 12296 | tf_op jit(solution)/shard_map/ppermute | solution.py:608
  24.3 1.5 %collective-permute-start.4 = (f32[8,128]{1,0:T(8,128)S(1)}, f32[8,128]{1,0:T(8,128)S(1)}, u32[]{:S(2)}, u32[]{:S(2)}) collective-permute-start(f32[8,128]{1,0:T(8,128)S(1)} %get-tuple-element.60.refs_3_), channel_id=1, source_target_pairs={{0,3},{1,2},{2,1},{3,0},{4,7},{5,6},{6,5},{7,4},{8,11},{9,10},{10,... | collective-permute-start | bytes 12296 | tf_op jit(solution)/shard_map/ppermute | solution.py:608
  25.8 0.0 collective-permute-done.2.refs_4_
  25.9 2.0 %collective-permute-done.3.refs_5_ = f32[8,128]{1,0:T(8,128)S(1)} collective-permute-done((f32[8,128]{1,0:T(8,128)S(1)}, f32[8,128]{1,0:T(8,128)S(1)}, u32[]{:S(2)}, u32[]{:S(2)}) %collective-permute-start.3) | collective-permute-done | bytes 4128 | tf_op jit(solution)/shard_map/ppermute | solution.py:608
  27.9 0.9 collective-permute-done.4.refs_6_
  28.8 1.9 %iterate.1 = (f32[8,128]{1,0:T(8,128)S(1)}, f32[8,8,16,128]{3,2,1,0:T(8,128)S(1)}, f32[8,8,16,128]{3,2,1,0:T(8,128)S(1)}, f32[1,8,16,128]{3,2,1,0:T(8,128)S(1)},...) custom-call(f32[64,8,1024]{2,1,0:T(8,128)S(1)} %get-tuple-element.57, ...), custom_call_target="tpu_custom_call" | custom-call | tf_op jit(solution)/shard_map/iterate/pallas_call | solution.py:463
  30.8 0.1 collective-permute-start.5
  30.8 1.6 %collective-permute-start.24 = (f32[2,8,16,128]{3,2,1,0:T(8,128)S(1)}, f32[2,8,16,128]{3,2,1,0:T(8,128)S(1)}, u32[]{:S(2)}, u32[]{:S(2)}) collective-permute-start(f32[2,8,16,128]{3,2,1,0:T(8,128)S(1)} %get-tuple-element.82), channel_id=1, source_target_pairs={{0,8},{4,12},{8,0},{12,4},{16,24},{20,28},{24,16},{28,20},{1,9},{5... | collective-permute-start | bytes 393224 | tf_op jit(solution)/shard_map/ppermute | solution.py:608
  32.5 0.2 collective-permute-start.25
  32.7 1.6 %collective-permute-start.18 = (f32[2,8,16,128]{3,2,1,0:T(8,128)S(1)}, f32[2,8,16,128]{3,2,1,0:T(8,128)S(1)}, u32[]{:S(2)}, u32[]{:S(2)}) collective-permute-start(f32[2,8,16,128]{3,2,1,0:T(8,128)S(1)} %get-tuple-element.76), channel_id=1, source_target_pairs={{0,8},{4,12},{8,0},{12,4},{16,24},{20,28},{24,16},{28,20},{1,9},{5... | collective-permute-start | bytes 393224 | tf_op jit(solution)/shard_map/ppermute | solution.py:608
  34.3 0.1 collective-permute-start.19
  34.4 2.9 %collective-permute-done.24.refs_2_ = f32[2,8,16,128]{3,2,1,0:T(8,128)S(1)} collective-permute-done((f32[2,8,16,128]{3,2,1,0:T(8,128)S(1)}, f32[2,8,16,128]{3,2,1,0:T(8,128)S(1)}, u32[]{:S(2)}, u32[]{:S(2)}) %collective-permute-start.24) | collective-permute-done | bytes 131104 | tf_op jit(solution)/shard_map/ppermute | solution.py:608
  37.3 1.6 %collective-permute-start.12 = (f32[2,8,16,128]{3,2,1,0:T(8,128)S(1)}, f32[2,8,16,128]{3,2,1,0:T(8,128)S(1)}, u32[]{:S(2)}, u32[]{:S(2)}) collective-permute-start(f32[2,8,16,128]{3,2,1,0:T(8,128)S(1)} %get-tuple-element.70), channel_id=1, source_target_pairs={{0,8},{4,12},{8,0},{12,4},{16,24},{20,28},{24,16},{28,20},{1,9},{5... | collective-permute-start | bytes 393224 | tf_op jit(solution)/shard_map/ppermute | solution.py:608
  38.8 0.3 collective-permute-done.25.refs_3_
  39.2 1.9 %collective-permute-start.13 = (f32[2,8,16,128]{3,2,1,0:T(8,128)S(1)}, f32[2,8,16,128]{3,2,1,0:T(8,128)S(1)}, u32[]{:S(2)}, u32[]{:S(2)}) collective-permute-start(f32[2,8,16,128]{3,2,1,0:T(8,128)S(1)} %get-tuple-element.71), channel_id=1, source_target_pairs={{0,12},{4,8},{8,4},{12,0},{16,28},{20,24},{24,20},{28,16},{1,13},{... | collective-permute-start | bytes 393224 | tf_op jit(solution)/shard_map/ppermute | solution.py:608
  41.1 1.8 %collective-permute-done.18.refs_2_ = f32[2,8,16,128]{3,2,1,0:T(8,128)S(1)} collective-permute-done((f32[2,8,16,128]{3,2,1,0:T(8,128)S(1)}, f32[2,8,16,128]{3,2,1,0:T(8,128)S(1)}, u32[]{:S(2)}, u32[]{:S(2)}) %collective-permute-start.18) | collective-permute-done | bytes 131104 | tf_op jit(solution)/shard_map/ppermute | solution.py:608
  42.9 1.6 %collective-permute-start.30 = (f32[1,8,16,128]{3,2,1,0:T(8,128)S(1)}, f32[1,8,16,128]{3,2,1,0:T(8,128)S(1)}, u32[]{:S(2)}, u32[]{:S(2)}) collective-permute-start(f32[1,8,16,128]{3,2,1,0:T(8,128)S(1)} %get-tuple-element.88), channel_id=1, source_target_pairs={{0,8},{4,12},{8,0},{12,4},{16,24},{20,28},{24,16},{28,20},{1,9},{5... | collective-permute-start | bytes 196616 | tf_op jit(solution)/shard_map/ppermute | solution.py:608
  44.5 1.8 %inverse_map.1.begun = f32[32,128]{1,0:T(8,128)S(1)} custom-call(s32[2,64]{1,0:T(2,128)S(1)} %bitcast.1), custom_call_target="tpu_custom_call" | custom-call | tf_op jit(solution)/shard_map/inverse_map/pallas_call | solution.py:114
  46.3 1.2 %inverse_rest.1.map_ref = f32[32,32]{1,0:T(8,128)S(1)} custom-call(f32[32,128]{1,0:T(8,128)S(1)} %inverse_map.1.begun), custom_call_target="tpu_custom_call" | custom-call | tf_op jit(solution)/shard_map/inverse_rest/pallas_call | solution.py:129
  47.5 1.6 %cross_sums.8 = f32[2,16,16,128]{3,2,1,0:T(8,128)S(1)} custom-call(f32[32,32]{1,0:T(8,128)S(1)} %inverse_rest.1.map_ref, f32[8,8,16,128]{3,2,1,0:T(8,128)S(1)} %get-tuple-element.62.refs_0_, f32[8,8,16,128]{3,2,1,0:T(8,128)S(1)} %collective-permute-done.5.refs_1_, f32[2,8,16,128]{3,2,1,0:T(8,128)S(1)} %collective-permute-done.24.refs_2_, ...), custom_call_target="tpu_custom_call" | custom-call | tf_op jit(solution)/shard_map/cross_sums/pallas_call | solution.py:568
  49.1 2.7 %collective-permute-start.26 = (f32[2,16,16,128]{3,2,1,0:T(8,128)S(1)}, f32[2,16,16,128]{3,2,1,0:T(8,128)S(1)}, u32[]{:S(2)}, u32[]{:S(2)}) collective-permute-start(f32[2,16,16,128]{3,2,1,0:T(8,128)S(1)} %cross_sums.8), channel_id=1, source_target_pairs={{0,16},{4,20},{8,24},{12,28},{16,0},{20,4},{24,8},{28,12},{1,17},{... | collective-permute-start | bytes 786440 | tf_op jit(solution)/shard_map/ppermute | solution.py:608
  51.8 1.6 %cross_sums.7 = f32[2,16,16,128]{3,2,1,0:T(8,128)S(1)} custom-call(f32[32,32]{1,0:T(8,128)S(1)} %inverse_rest.1.map_ref, f32[8,8,16,128]{3,2,1,0:T(8,128)S(1)} %get-tuple-element.62.refs_0_, f32[8,8,16,128]{3,2,1,0:T(8,128)S(1)} %collective-permute-done.5.refs_1_, f32[2,8,16,128]{3,2,1,0:T(8,128)S(1)} %collective-permute-done.18.refs_2_, ...), custom_call_target="tpu_custom_call" | custom-call | tf_op jit(solution)/shard_map/cross_sums/pallas_call | solution.py:568
  53.3 0.4 collective-permute-start.20
  53.8 0.5 collective-permute-start.6
  54.2 1.5 %cross_sums.6 = f32[2,16,16,128]{3,2,1,0:T(8,128)S(1)} custom-call(f32[32,32]{1,0:T(8,128)S(1)} %inverse_rest.1.map_ref, f32[8,8,16,128]{3,2,1,0:T(8,128)S(1)} %get-tuple-element.62.refs_0_, f32[8,8,16,128]{3,2,1,0:T(8,128)S(1)} %collective-permute-done.5.refs_1_, f32[2,8,16,128]{3,2,1,0:T(8,128)S(1)} %collective-permute-done.12.refs_2_, ...), custom_call_target="tpu_custom_call" | custom-call | tf_op jit(solution)/shard_map/cross_sums/pallas_call | solution.py:568
  55.7 1.0 collective-permute-start.7
  56.7 2.6 %collective-permute-start.14 = (f32[2,16,16,128]{3,2,1,0:T(8,128)S(1)}, f32[2,16,16,128]{3,2,1,0:T(8,128)S(1)}, u32[]{:S(2)}, u32[]{:S(2)}) collective-permute-start(f32[2,16,16,128]{3,2,1,0:T(8,128)S(1)} %cross_sums.6), channel_id=1, source_target_pairs={{0,16},{4,20},{8,24},{12,28},{16,0},{20,4},{24,8},{28,12},{1,17},{... | collective-permute-start | bytes 786440 | tf_op jit(solution)/shard_map/ppermute | solution.py:608
  59.3 1.2 %cross_sums.9 = f32[1,16,16,128]{3,2,1,0:T(8,128)S(1)} custom-call(f32[32,32]{1,0:T(8,128)S(1)} %inverse_rest.1.map_ref, f32[8,8,16,128]{3,2,1,0:T(8,128)S(1)} %get-tuple-element.62.refs_0_, f32[8,8,16,128]{3,2,1,0:T(8,128)S(1)} %collective-permute-done.5.refs_1_, f32[1,8,16,128]{3,2,1,0:T(8,128)S(1)} %collective-permute-done.30.refs_2_, ...), custom_call_target="tpu_custom_call" | custom-call | tf_op jit(solution)/shard_map/cross_sums/pallas_call | solution.py:568
  60.5 5.1 %collective-permute-done.6.refs_2_ = f32[1,8,16,128]{3,2,1,0:T(8,128)S(1)} collective-permute-done((f32[1,8,16,128]{3,2,1,0:T(8,128)S(1)}, f32[1,8,16,128]{3,2,1,0:T(8,128)S(1)}, u32[]{:S(2)}, u32[]{:S(2)}) %collective-permute-start.6) | collective-permute-done | bytes 65568 | tf_op jit(solution)/shard_map/ppermute | solution.py:608
  65.6 3.8 %collective-permute-start.32 = (f32[1,16,16,128]{3,2,1,0:T(8,128)S(1)}, f32[1,16,16,128]{3,2,1,0:T(8,128)S(1)}, u32[]{:S(2)}, u32[]{:S(2)}) collective-permute-start(f32[1,16,16,128]{3,2,1,0:T(8,128)S(1)} %cross_sums.9), channel_id=1, source_target_pairs={{0,16},{4,20},{8,24},{12,28},{16,0},{20,4},{24,8},{28,12},{1,17},{... | collective-permute-start | bytes 393224 | tf_op jit(solution)/shard_map/ppermute | solution.py:608
  69.4 1.2 %cross_sums.5 = f32[1,16,16,128]{3,2,1,0:T(8,128)S(1)} custom-call(f32[32,32]{1,0:T(8,128)S(1)} %inverse_rest.1.map_ref, f32[8,8,16,128]{3,2,1,0:T(8,128)S(1)} %get-tuple-element.62.refs_0_, f32[8,8,16,128]{3,2,1,0:T(8,128)S(1)} %collective-permute-done.5.refs_1_, f32[1,8,16,128]{3,2,1,0:T(8,128)S(1)} %collective-permute-done.6.refs_2_, ...), custom_call_target="tpu_custom_call" | custom-call | tf_op jit(solution)/shard_map/cross_sums/pallas_call | solution.py:568
  70.6 0.4 collective-permute-start.8
  71.0 24.8 %collective-permute-done.32.refs_4_ = f32[1,16,16,128]{3,2,1,0:T(8,128)S(1)} collective-permute-done((f32[1,16,16,128]{3,2,1,0:T(8,128)S(1)}, f32[1,16,16,128]{3,2,1,0:T(8,128)S(1)}, u32[]{:S(2)}, u32[]{:S(2)}) %collective-permute-start.32) | collective-permute-done | bytes 131104 | tf_op jit(solution)/shard_map/ppermute | solution.py:608
  95.8 1.2 %own_sums.9 = (f32[1,4,16,128]{3,2,1,0:T(8,128)S(1)}, f32[1,4,16,128]{3,2,1,0:T(8,128)S(1)}, f32[1,4,16,128]{3,2,1,0:T(8,128)S(1)}, f32[1,4,16,128]{3,2,1,0:T(8,128)S(1)}) custom-call(f32[32,32]{1,0:T(8,128)S(1)} %inverse_rest.1.map_ref, f32[8,8,16,128]{3,2,1,0:T(8,128)S(1)} %get-tuple-element.62.refs_0_, ...), custom_call_target="tpu_custom_call" | custom-call | tf_op jit(solution)/shard_map/own_sums/pallas_call | solution.py:568
  97.0 0.1 collective-permute-start.33
  97.1 1.1 collective-permute-done.8.refs_4_
  98.2 1.2 %own_sums.5 = (f32[1,4,16,128]{3,2,1,0:T(8,128)S(1)}, f32[1,4,16,128]{3,2,1,0:T(8,128)S(1)}, f32[1,4,16,128]{3,2,1,0:T(8,128)S(1)}, f32[1,4,16,128]{3,2,1,0:T(8,128)S(1)}) custom-call(f32[32,32]{1,0:T(8,128)S(1)} %inverse_rest.1.map_ref, f32[8,8,16,128]{3,2,1,0:T(8,128)S(1)} %get-tuple-element.62.refs_0_, ...), custom_call_target="tpu_custom_call" | custom-call | tf_op jit(solution)/shard_map/own_sums/pallas_call | solution.py:568
  99.4 1.1 collective-permute-start.35
  100.6 1.1 collective-permute-start.10
  101.6 1.4 %collective-permute-start.11 = (f32[1,4,16,128]{3,2,1,0:T(8,128)S(1)}, f32[1,4,16,128]{3,2,1,0:T(8,128)S(1)}, u32[]{:S(2)}, u32[]{:S(2)}) collective-permute-start(f32[1,4,16,128]{3,2,1,0:T(8,128)S(1)} %get-tuple-element.69), channel_id=1, source_target_pairs={{0,12},{4,8},{8,4},{12,0},{16,28},{20,24},{24,20},{28,16},{1,13},{... | collective-permute-start | bytes 98312 | tf_op jit(solution)/shard_map/ppermute | solution.py:608
  103.0 1.5 %own_sums.8 = (f32[2,4,16,128]{3,2,1,0:T(8,128)S(1)}, f32[2,4,16,128]{3,2,1,0:T(8,128)S(1)}, f32[2,4,16,128]{3,2,1,0:T(8,128)S(1)}, f32[2,4,16,128]{3,2,1,0:T(8,128)S(1)}) custom-call(f32[32,32]{1,0:T(8,128)S(1)} %inverse_rest.1.map_ref, f32[8,8,16,128]{3,2,1,0:T(8,128)S(1)} %get-tuple-element.62.refs_0_, ...), custom_call_target="tpu_custom_call" | custom-call | tf_op jit(solution)/shard_map/own_sums/pallas_call | solution.py:568
  104.5 1.5 %own_sums.7 = (f32[2,4,16,128]{3,2,1,0:T(8,128)S(1)}, f32[2,4,16,128]{3,2,1,0:T(8,128)S(1)}, f32[2,4,16,128]{3,2,1,0:T(8,128)S(1)}, f32[2,4,16,128]{3,2,1,0:T(8,128)S(1)}) custom-call(f32[32,32]{1,0:T(8,128)S(1)} %inverse_rest.1.map_ref, f32[8,8,16,128]{3,2,1,0:T(8,128)S(1)} %get-tuple-element.62.refs_0_, ...), custom_call_target="tpu_custom_call" | custom-call | tf_op jit(solution)/shard_map/own_sums/pallas_call | solution.py:568
  106.1 0.1 collective-permute-start.27
  106.2 0.7 collective-permute-start.28
  106.9 1.1 collective-permute-start.29
  108.0 0.4 collective-permute-start.21
  108.4 0.1 collective-permute-start.9
  108.5 1.5 %own_sums.6 = (f32[2,4,16,128]{3,2,1,0:T(8,128)S(1)}, f32[2,4,16,128]{3,2,1,0:T(8,128)S(1)}, f32[2,4,16,128]{3,2,1,0:T(8,128)S(1)}, f32[2,4,16,128]{3,2,1,0:T(8,128)S(1)}) custom-call(f32[32,32]{1,0:T(8,128)S(1)} %inverse_rest.1.map_ref, f32[8,8,16,128]{3,2,1,0:T(8,128)S(1)} %get-tuple-element.62.refs_0_, ...), custom_call_target="tpu_custom_call" | custom-call | tf_op jit(solution)/shard_map/own_sums/pallas_call | solution.py:568
  110.1 0.7 collective-permute-start.22
  110.7 1.1 collective-permute-start.23
  111.8 0.4 collective-permute-start.15
  112.3 0.6 collective-permute-start.16
  112.9 0.8 collective-permute-start.17
  113.7 2.1 %combine.1 = f32[8,64,1024]{2,1,0:T(8,128)} custom-call(f32[64,8,1024]{2,1,0:T(8,128)S(1)} %get-tuple-element.57.refs_0_.r_ref, f32[64,8,1024]{2,1,0:T(8,128)S(1)} %get-tuple-element.58.refs_1_.v_ref, f32[64,8,1024]{2,1,0:T(8,128)S(1)} %get-tuple-element.59.refs_2_.u_ref, f32[8,128]{1,0:T(8,128)S(1)} %get-tuple-element.61.weights_ref), custom_call_target="tpu_custom_call" | custom-call | tf_op jit(solution)/shard_map/combine/pallas_call | solution.py:500
  115.9 2.0 %collective-permute-done.16.refs_6_ = f32[2,4,16,128]{3,2,1,0:T(8,128)S(1)} collective-permute-done((f32[2,4,16,128]{3,2,1,0:T(8,128)S(1)}, f32[2,4,16,128]{3,2,1,0:T(8,128)S(1)}, u32[]{:S(2)}, u32[]{:S(2)}) %collective-permute-start.16) | collective-permute-done | bytes 65568 | tf_op jit(solution)/shard_map/ppermute | solution.py:608
  117.9 0.2 collective-permute-done.17.refs_7_
  118.1 1.1 assemble.1
  (28 shorter events, 0.1 us)
Async XLA Ops:
  2.3 16.9 %collective-permute-start = (f32[6,8,1024]{2,1,0:T(8,128)S(1)}, f32[6,8,1024]{2,1,0:T(8,128)S(1)}, u32[]{:S(2)}, u32[]{:S(2)}) collective-permute-start(f32[6,8,1024]{2,1,0:T(8,128)S(1)} %get-tuple-element.48), channel_id=1, source_target_pairs={{0,1},{1,0},{2,3},{3,2},{4,5},{5,4},{6,7},{7,6},{8,9},{9,8},{10,11... | collective-permute-start | bytes 589832 | tf_op jit(solution)/shard_map/ppermute | solution.py:629
  5.3 13.8 %collective-permute-start.1 = (f32[6,8,1024]{2,1,0:T(8,128)S(1)}, f32[6,8,1024]{2,1,0:T(8,128)S(1)}, u32[]{:S(2)}, u32[]{:S(2)}) collective-permute-start(f32[6,8,1024]{2,1,0:T(8,128)S(1)} %get-tuple-element.49), channel_id=1, source_target_pairs={{1,2},{2,1},{5,6},{6,5},{9,10},{10,9},{13,14},{14,13},{17,18},{18,... | collective-permute-start | bytes 589832 | tf_op jit(solution)/shard_map/ppermute | solution.py:629
  20.1 5.8 %collective-permute-start.2 = (f32[8,128]{1,0:T(8,128)S(1)}, f32[8,128]{1,0:T(8,128)S(1)}, u32[]{:S(2)}, u32[]{:S(2)}) collective-permute-start(f32[8,128]{1,0:T(8,128)S(1)} %get-tuple-element.60.refs_3_), channel_id=1, source_target_pairs={{0,1},{1,0},{2,3},{3,2},{4,5},{5,4},{6,7},{7,6},{8,9},{9,8},{10,11... | collective-permute-start | bytes 12296 | tf_op jit(solution)/shard_map/ppermute | solution.py:608
  24.3 3.6 %collective-permute-start.3 = (f32[8,128]{1,0:T(8,128)S(1)}, f32[8,128]{1,0:T(8,128)S(1)}, u32[]{:S(2)}, u32[]{:S(2)}) collective-permute-start(f32[8,128]{1,0:T(8,128)S(1)} %get-tuple-element.60.refs_3_), channel_id=1, source_target_pairs={{0,2},{1,3},{2,0},{3,1},{4,6},{5,7},{6,4},{7,5},{8,10},{9,11},{10,... | collective-permute-start | bytes 12296 | tf_op jit(solution)/shard_map/ppermute | solution.py:608
  24.3 4.5 %collective-permute-start.4 = (f32[8,128]{1,0:T(8,128)S(1)}, f32[8,128]{1,0:T(8,128)S(1)}, u32[]{:S(2)}, u32[]{:S(2)}) collective-permute-start(f32[8,128]{1,0:T(8,128)S(1)} %get-tuple-element.60.refs_3_), channel_id=1, source_target_pairs={{0,3},{1,2},{2,1},{3,0},{4,7},{5,6},{6,5},{7,4},{8,11},{9,10},{10,... | collective-permute-start | bytes 12296 | tf_op jit(solution)/shard_map/ppermute | solution.py:608
  28.8 15.7 %copy-start = (s32[64,2]{0,1:T(2,128)S(1)}, s32[64,2]{0,1:T(2,128)}, u32[]{:S(2)}) copy-start(s32[64,2]{0,1:T(2,128)} %param.7) | copy-start | bytes 1540
  30.8 13.7 %collective-permute-start.5 = (f32[8,8,16,128]{3,2,1,0:T(8,128)S(1)}, f32[8,8,16,128]{3,2,1,0:T(8,128)S(1)}, u32[]{:S(2)}, u32[]{:S(2)}) collective-permute-start(f32[8,8,16,128]{3,2,1,0:T(8,128)S(1)} %get-tuple-element.63), channel_id=1, source_target_pairs={{0,4},{4,0},{8,12},{12,8},{16,20},{20,16},{24,28},{28,24},{1,5},{5... | collective-permute-start | bytes 1572872 | tf_op jit(solution)/shard_map/ppermute | solution.py:608
  30.8 6.4 %collective-permute-start.24 = (f32[2,8,16,128]{3,2,1,0:T(8,128)S(1)}, f32[2,8,16,128]{3,2,1,0:T(8,128)S(1)}, u32[]{:S(2)}, u32[]{:S(2)}) collective-permute-start(f32[2,8,16,128]{3,2,1,0:T(8,128)S(1)} %get-tuple-element.82), channel_id=1, source_target_pairs={{0,8},{4,12},{8,0},{12,4},{16,24},{20,28},{24,16},{28,20},{1,9},{5... | collective-permute-start | bytes 393224 | tf_op jit(solution)/shard_map/ppermute | solution.py:608
  32.5 6.7 %collective-permute-start.25 = (f32[2,8,16,128]{3,2,1,0:T(8,128)S(1)}, f32[2,8,16,128]{3,2,1,0:T(8,128)S(1)}, u32[]{:S(2)}, u32[]{:S(2)}) collective-permute-start(f32[2,8,16,128]{3,2,1,0:T(8,128)S(1)} %get-tuple-element.83), channel_id=1, source_target_pairs={{0,12},{4,8},{8,4},{12,0},{16,28},{20,24},{24,20},{28,16},{1,13},{... | collective-permute-start | bytes 393224 | tf_op jit(solution)/shard_map/ppermute | solution.py:608
  32.7 10.2 %collective-permute-start.18 = (f32[2,8,16,128]{3,2,1,0:T(8,128)S(1)}, f32[2,8,16,128]{3,2,1,0:T(8,128)S(1)}, u32[]{:S(2)}, u32[]{:S(2)}) collective-permute-start(f32[2,8,16,128]{3,2,1,0:T(8,128)S(1)} %get-tuple-element.76), channel_id=1, source_target_pairs={{0,8},{4,12},{8,0},{12,4},{16,24},{20,28},{24,16},{28,20},{1,9},{5... | collective-permute-start | bytes 393224 | tf_op jit(solution)/shard_map/ppermute | solution.py:608
  34.3 14.8 %collective-permute-start.19 = (f32[2,8,16,128]{3,2,1,0:T(8,128)S(1)}, f32[2,8,16,128]{3,2,1,0:T(8,128)S(1)}, u32[]{:S(2)}, u32[]{:S(2)}) collective-permute-start(f32[2,8,16,128]{3,2,1,0:T(8,128)S(1)} %get-tuple-element.77), channel_id=1, source_target_pairs={{0,12},{4,8},{8,4},{12,0},{16,28},{20,24},{24,20},{28,16},{1,13},{... | collective-permute-start | bytes 393224 | tf_op jit(solution)/shard_map/ppermute | solution.py:608
  37.3 16.1 %collective-permute-start.12 = (f32[2,8,16,128]{3,2,1,0:T(8,128)S(1)}, f32[2,8,16,128]{3,2,1,0:T(8,128)S(1)}, u32[]{:S(2)}, u32[]{:S(2)}) collective-permute-start(f32[2,8,16,128]{3,2,1,0:T(8,128)S(1)} %get-tuple-element.70), channel_id=1, source_target_pairs={{0,8},{4,12},{8,0},{12,4},{16,24},{20,28},{24,16},{28,20},{1,9},{5... | collective-permute-start | bytes 393224 | tf_op jit(solution)/shard_map/ppermute | solution.py:608
  39.2 14.6 %collective-permute-start.13 = (f32[2,8,16,128]{3,2,1,0:T(8,128)S(1)}, f32[2,8,16,128]{3,2,1,0:T(8,128)S(1)}, u32[]{:S(2)}, u32[]{:S(2)}) collective-permute-start(f32[2,8,16,128]{3,2,1,0:T(8,128)S(1)} %get-tuple-element.71), channel_id=1, source_target_pairs={{0,12},{4,8},{8,4},{12,0},{16,28},{20,24},{24,20},{28,16},{1,13},{... | collective-permute-start | bytes 393224 | tf_op jit(solution)/shard_map/ppermute | solution.py:608
  42.9 12.8 %collective-permute-start.30 = (f32[1,8,16,128]{3,2,1,0:T(8,128)S(1)}, f32[1,8,16,128]{3,2,1,0:T(8,128)S(1)}, u32[]{:S(2)}, u32[]{:S(2)}) collective-permute-start(f32[1,8,16,128]{3,2,1,0:T(8,128)S(1)} %get-tuple-element.88), channel_id=1, source_target_pairs={{0,8},{4,12},{8,0},{12,4},{16,24},{20,28},{24,16},{28,20},{1,9},{5... | collective-permute-start | bytes 196616 | tf_op jit(solution)/shard_map/ppermute | solution.py:608
  44.5 12.3 %collective-permute-start.31 = (f32[1,8,16,128]{3,2,1,0:T(8,128)S(1)}, f32[1,8,16,128]{3,2,1,0:T(8,128)S(1)}, u32[]{:S(2)}, u32[]{:S(2)}) collective-permute-start(f32[1,8,16,128]{3,2,1,0:T(8,128)S(1)} %get-tuple-element.89), channel_id=1, source_target_pairs={{0,12},{4,8},{8,4},{12,0},{16,28},{20,24},{24,20},{28,16},{1,13},{... | collective-permute-start | bytes 196616 | tf_op jit(solution)/shard_map/ppermute | solution.py:608
  49.1 51.4 %collective-permute-start.26 = (f32[2,16,16,128]{3,2,1,0:T(8,128)S(1)}, f32[2,16,16,128]{3,2,1,0:T(8,128)S(1)}, u32[]{:S(2)}, u32[]{:S(2)}) collective-permute-start(f32[2,16,16,128]{3,2,1,0:T(8,128)S(1)} %cross_sums.8), channel_id=1, source_target_pairs={{0,16},{4,20},{8,24},{12,28},{16,0},{20,4},{24,8},{28,12},{1,17},{... | collective-permute-start | bytes 786440 | tf_op jit(solution)/shard_map/ppermute | solution.py:608
  53.3 48.3 %collective-permute-start.20 = (f32[2,16,16,128]{3,2,1,0:T(8,128)S(1)}, f32[2,16,16,128]{3,2,1,0:T(8,128)S(1)}, u32[]{:S(2)}, u32[]{:S(2)}) collective-permute-start(f32[2,16,16,128]{3,2,1,0:T(8,128)S(1)} %cross_sums.7), channel_id=1, source_target_pairs={{0,16},{4,20},{8,24},{12,28},{16,0},{20,4},{24,8},{28,12},{1,17},{... | collective-permute-start | bytes 786440 | tf_op jit(solution)/shard_map/ppermute | solution.py:608
  53.8 11.9 %collective-permute-start.6 = (f32[1,8,16,128]{3,2,1,0:T(8,128)S(1)}, f32[1,8,16,128]{3,2,1,0:T(8,128)S(1)}, u32[]{:S(2)}, u32[]{:S(2)}) collective-permute-start(f32[1,8,16,128]{3,2,1,0:T(8,128)S(1)} %get-tuple-element.64), channel_id=1, source_target_pairs={{0,8},{4,12},{8,0},{12,4},{16,24},{20,28},{24,16},{28,20},{1,9},{5... | collective-permute-start | bytes 196616 | tf_op jit(solution)/shard_map/ppermute | solution.py:608
  55.7 13.7 %collective-permute-start.7 = (f32[1,8,16,128]{3,2,1,0:T(8,128)S(1)}, f32[1,8,16,128]{3,2,1,0:T(8,128)S(1)}, u32[]{:S(2)}, u32[]{:S(2)}) collective-permute-start(f32[1,8,16,128]{3,2,1,0:T(8,128)S(1)} %get-tuple-element.65), channel_id=1, source_target_pairs={{0,12},{4,8},{8,4},{12,0},{16,28},{20,24},{24,20},{28,16},{1,13},{... | collective-permute-start | bytes 196616 | tf_op jit(solution)/shard_map/ppermute | solution.py:608
  56.7 51.7 %collective-permute-start.14 = (f32[2,16,16,128]{3,2,1,0:T(8,128)S(1)}, f32[2,16,16,128]{3,2,1,0:T(8,128)S(1)}, u32[]{:S(2)}, u32[]{:S(2)}) collective-permute-start(f32[2,16,16,128]{3,2,1,0:T(8,128)S(1)} %cross_sums.6), channel_id=1, source_target_pairs={{0,16},{4,20},{8,24},{12,28},{16,0},{20,4},{24,8},{28,12},{1,17},{... | collective-permute-start | bytes 786440 | tf_op jit(solution)/shard_map/ppermute | solution.py:608
  65.6 30.2 %collective-permute-start.32 = (f32[1,16,16,128]{3,2,1,0:T(8,128)S(1)}, f32[1,16,16,128]{3,2,1,0:T(8,128)S(1)}, u32[]{:S(2)}, u32[]{:S(2)}) collective-permute-start(f32[1,16,16,128]{3,2,1,0:T(8,128)S(1)} %cross_sums.9), channel_id=1, source_target_pairs={{0,16},{4,20},{8,24},{12,28},{16,0},{20,4},{24,8},{28,12},{1,17},{... | collective-permute-start | bytes 393224 | tf_op jit(solution)/shard_map/ppermute | solution.py:608
  70.6 27.6 %collective-permute-start.8 = (f32[1,16,16,128]{3,2,1,0:T(8,128)S(1)}, f32[1,16,16,128]{3,2,1,0:T(8,128)S(1)}, u32[]{:S(2)}, u32[]{:S(2)}) collective-permute-start(f32[1,16,16,128]{3,2,1,0:T(8,128)S(1)} %cross_sums.5), channel_id=1, source_target_pairs={{0,16},{4,20},{8,24},{12,28},{16,0},{20,4},{24,8},{28,12},{1,17},{... | collective-permute-start | bytes 393224 | tf_op jit(solution)/shard_map/ppermute | solution.py:608
  97.0 2.4 %collective-permute-start.33 = (f32[1,4,16,128]{3,2,1,0:T(8,128)S(1)}, f32[1,4,16,128]{3,2,1,0:T(8,128)S(1)}, u32[]{:S(2)}, u32[]{:S(2)}) collective-permute-start(f32[1,4,16,128]{3,2,1,0:T(8,128)S(1)} %get-tuple-element.91), channel_id=1, source_target_pairs={{0,4},{4,0},{8,12},{12,8},{16,20},{20,16},{24,28},{28,24},{1,5},{5... | collective-permute-start | bytes 98312 | tf_op jit(solution)/shard_map/ppermute | solution.py:608
  98.2 7.9 %collective-permute-start.34 = (f32[1,4,16,128]{3,2,1,0:T(8,128)S(1)}, f32[1,4,16,128]{3,2,1,0:T(8,128)S(1)}, u32[]{:S(2)}, u32[]{:S(2)}) collective-permute-start(f32[1,4,16,128]{3,2,1,0:T(8,128)S(1)} %get-tuple-element.92), channel_id=1, source_target_pairs={{0,8},{4,12},{8,0},{12,4},{16,24},{20,28},{24,16},{28,20},{1,9},{5... | collective-permute-start | bytes 98312 | tf_op jit(solution)/shard_map/ppermute | solution.py:608
  99.4 6.7 %collective-permute-start.35 = (f32[1,4,16,128]{3,2,1,0:T(8,128)S(1)}, f32[1,4,16,128]{3,2,1,0:T(8,128)S(1)}, u32[]{:S(2)}, u32[]{:S(2)}) collective-permute-start(f32[1,4,16,128]{3,2,1,0:T(8,128)S(1)} %get-tuple-element.93), channel_id=1, source_target_pairs={{0,12},{4,8},{8,4},{12,0},{16,28},{20,24},{24,20},{28,16},{1,13},{... | collective-permute-start | bytes 98312 | tf_op jit(solution)/shard_map/ppermute | solution.py:608
  100.6 6.4 %collective-permute-start.10 = (f32[1,4,16,128]{3,2,1,0:T(8,128)S(1)}, f32[1,4,16,128]{3,2,1,0:T(8,128)S(1)}, u32[]{:S(2)}, u32[]{:S(2)}) collective-permute-start(f32[1,4,16,128]{3,2,1,0:T(8,128)S(1)} %get-tuple-element.68), channel_id=1, source_target_pairs={{0,8},{4,12},{8,0},{12,4},{16,24},{20,28},{24,16},{28,20},{1,9},{5... | collective-permute-start | bytes 98312 | tf_op jit(solution)/shard_map/ppermute | solution.py:608
  101.6 6.4 %collective-permute-start.11 = (f32[1,4,16,128]{3,2,1,0:T(8,128)S(1)}, f32[1,4,16,128]{3,2,1,0:T(8,128)S(1)}, u32[]{:S(2)}, u32[]{:S(2)}) collective-permute-start(f32[1,4,16,128]{3,2,1,0:T(8,128)S(1)} %get-tuple-element.69), channel_id=1, source_target_pairs={{0,12},{4,8},{8,4},{12,0},{16,28},{20,24},{24,20},{28,16},{1,13},{... | collective-permute-start | bytes 98312 | tf_op jit(solution)/shard_map/ppermute | solution.py:608
  106.1 4.6 %collective-permute-start.27 = (f32[2,4,16,128]{3,2,1,0:T(8,128)S(1)}, f32[2,4,16,128]{3,2,1,0:T(8,128)S(1)}, u32[]{:S(2)}, u32[]{:S(2)}) collective-permute-start(f32[2,4,16,128]{3,2,1,0:T(8,128)S(1)} %get-tuple-element.85), channel_id=1, source_target_pairs={{0,4},{4,0},{8,12},{12,8},{16,20},{20,16},{24,28},{28,24},{1,5},{5... | collective-permute-start | bytes 196616 | tf_op jit(solution)/shard_map/ppermute | solution.py:608
  106.2 5.7 %collective-permute-start.28 = (f32[2,4,16,128]{3,2,1,0:T(8,128)S(1)}, f32[2,4,16,128]{3,2,1,0:T(8,128)S(1)}, u32[]{:S(2)}, u32[]{:S(2)}) collective-permute-start(f32[2,4,16,128]{3,2,1,0:T(8,128)S(1)} %get-tuple-element.86), channel_id=1, source_target_pairs={{0,8},{4,12},{8,0},{12,4},{16,24},{20,28},{24,16},{28,20},{1,9},{5... | collective-permute-start | bytes 196616 | tf_op jit(solution)/shard_map/ppermute | solution.py:608
  106.9 5.3 %collective-permute-start.29 = (f32[2,4,16,128]{3,2,1,0:T(8,128)S(1)}, f32[2,4,16,128]{3,2,1,0:T(8,128)S(1)}, u32[]{:S(2)}, u32[]{:S(2)}) collective-permute-start(f32[2,4,16,128]{3,2,1,0:T(8,128)S(1)} %get-tuple-element.87), channel_id=1, source_target_pairs={{0,12},{4,8},{8,4},{12,0},{16,28},{20,24},{24,20},{28,16},{1,13},{... | collective-permute-start | bytes 196616 | tf_op jit(solution)/shard_map/ppermute | solution.py:608
  108.0 4.8 %collective-permute-start.21 = (f32[2,4,16,128]{3,2,1,0:T(8,128)S(1)}, f32[2,4,16,128]{3,2,1,0:T(8,128)S(1)}, u32[]{:S(2)}, u32[]{:S(2)}) collective-permute-start(f32[2,4,16,128]{3,2,1,0:T(8,128)S(1)} %get-tuple-element.79), channel_id=1, source_target_pairs={{0,4},{4,0},{8,12},{12,8},{16,20},{20,16},{24,28},{28,24},{1,5},{5... | collective-permute-start | bytes 196616 | tf_op jit(solution)/shard_map/ppermute | solution.py:608
  108.4 1.6 %collective-permute-start.9 = (f32[1,4,16,128]{3,2,1,0:T(8,128)S(1)}, f32[1,4,16,128]{3,2,1,0:T(8,128)S(1)}, u32[]{:S(2)}, u32[]{:S(2)}) collective-permute-start(f32[1,4,16,128]{3,2,1,0:T(8,128)S(1)} %get-tuple-element.67), channel_id=1, source_target_pairs={{0,4},{4,0},{8,12},{12,8},{16,20},{20,16},{24,28},{28,24},{1,5},{5... | collective-permute-start | bytes 98312 | tf_op jit(solution)/shard_map/ppermute | solution.py:608
  110.1 5.8 %collective-permute-start.22 = (f32[2,4,16,128]{3,2,1,0:T(8,128)S(1)}, f32[2,4,16,128]{3,2,1,0:T(8,128)S(1)}, u32[]{:S(2)}, u32[]{:S(2)}) collective-permute-start(f32[2,4,16,128]{3,2,1,0:T(8,128)S(1)} %get-tuple-element.80), channel_id=1, source_target_pairs={{0,8},{4,12},{8,0},{12,4},{16,24},{20,28},{24,16},{28,20},{1,9},{5... | collective-permute-start | bytes 196616 | tf_op jit(solution)/shard_map/ppermute | solution.py:608
  110.7 5.1 %collective-permute-start.23 = (f32[2,4,16,128]{3,2,1,0:T(8,128)S(1)}, f32[2,4,16,128]{3,2,1,0:T(8,128)S(1)}, u32[]{:S(2)}, u32[]{:S(2)}) collective-permute-start(f32[2,4,16,128]{3,2,1,0:T(8,128)S(1)} %get-tuple-element.81), channel_id=1, source_target_pairs={{0,12},{4,8},{8,4},{12,0},{16,28},{20,24},{24,20},{28,16},{1,13},{... | collective-permute-start | bytes 196616 | tf_op jit(solution)/shard_map/ppermute | solution.py:608
  111.8 4.0 %collective-permute-start.15 = (f32[2,4,16,128]{3,2,1,0:T(8,128)S(1)}, f32[2,4,16,128]{3,2,1,0:T(8,128)S(1)}, u32[]{:S(2)}, u32[]{:S(2)}) collective-permute-start(f32[2,4,16,128]{3,2,1,0:T(8,128)S(1)} %get-tuple-element.73), channel_id=1, source_target_pairs={{0,4},{4,0},{8,12},{12,8},{16,20},{20,16},{24,28},{28,24},{1,5},{5... | collective-permute-start | bytes 196616 | tf_op jit(solution)/shard_map/ppermute | solution.py:608
  112.3 5.6 %collective-permute-start.16 = (f32[2,4,16,128]{3,2,1,0:T(8,128)S(1)}, f32[2,4,16,128]{3,2,1,0:T(8,128)S(1)}, u32[]{:S(2)}, u32[]{:S(2)}) collective-permute-start(f32[2,4,16,128]{3,2,1,0:T(8,128)S(1)} %get-tuple-element.74), channel_id=1, source_target_pairs={{0,8},{4,12},{8,0},{12,4},{16,24},{20,28},{24,16},{28,20},{1,9},{5... | collective-permute-start | bytes 196616 | tf_op jit(solution)/shard_map/ppermute | solution.py:608
  112.9 5.2 %collective-permute-start.17 = (f32[2,4,16,128]{3,2,1,0:T(8,128)S(1)}, f32[2,4,16,128]{3,2,1,0:T(8,128)S(1)}, u32[]{:S(2)}, u32[]{:S(2)}) collective-permute-start(f32[2,4,16,128]{3,2,1,0:T(8,128)S(1)} %get-tuple-element.75), channel_id=1, source_target_pairs={{0,12},{4,8},{8,4},{12,0},{16,28},{20,24},{24,20},{28,16},{1,13},{... | collective-permute-start | bytes 196616 | tf_op jit(solution)/shard_map/ppermute | solution.py:608
